TPU v7x, 32 devices: a whole 2x2x4 slice. The times are simulated.
32 devices in a mesh: dp: 16 (over z, y, x), tensor: 2 (over core).
Axes of the slice: x: 2, y: 2, z: 4, core: 2. Of those that a mesh axis runs over, the one named last changes fastest.
Arguments:
- tokens: bfloat16 [16384, 768], P(('dp', 'tensor')), may hold values from -6 to 6
- cotangent: bfloat16 [16384, 768], P(('dp', 'tensor')), may hold values from -6 to 6
- prefix: int32 [16], P('dp'), may hold values from 0 to 1024
- query_weight: bfloat16 [768, 768], P('dp', 'tensor'), may hold values from -0.21875 to 0.21875
- key_weight: bfloat16 [768, 768], P('dp', 'tensor'), may hold values from -0.21875 to 0.21875
- value_weight: bfloat16 [768, 768], P('dp', 'tensor'), may hold values from -0.375 to 0.375
- out_weight: bfloat16 [768, 768], P('dp', 'tensor'), may hold values from -0.375 to 0.375
- up_weight: bfloat16 [768, 3072], P('dp', 'tensor'), may hold values from -0.375 to 0.375
- down_weight: bfloat16 [768, 3072], P('dp', 'tensor'), may hold values from -0.1875 to 0.1875
- model_vectors: float32 [6, 768], replicated, may hold values from -1.2 to 2, as said below
- head_vectors: float32 [4, 768], P(None, 'tensor'), may hold values from -1.2 to 2, as said below
- hidden_vectors: float32 [3, 3072], P(None, 'tensor'), may hold values from -1.2 to 2, as said below
Outputs:
- output: bfloat16 [16384, 768], P(('dp', 'tensor'))
- input_grad: float32 [16384, 768], P(('dp', 'tensor'))
- query_weight_grad: float32 [768, 768], P('dp', 'tensor')
- key_weight_grad: float32 [768, 768], P('dp', 'tensor')
- value_weight_grad: float32 [768, 768], P('dp', 'tensor')
- out_weight_grad: float32 [768, 768], P('dp', 'tensor')
- up_weight_grad: float32 [768, 3072], P('dp', 'tensor')
- down_weight_grad: float32 [768, 3072], P('dp', 'tensor')
- model_vectors_grad: float32 [6, 768], replicated
- head_vectors_grad: float32 [4, 768], P(None, 'tensor')
- hidden_vectors_grad: float32 [3, 3072], P(None, 'tensor')
Inputs may be any that keep to these rules, and one draw needn't show every extreme that they name: `model_vectors`: gains and biases as in the rows named by the meaning. `head_vectors`: gains and biases as in the rows named by the meaning. `hidden_vectors`: gains and biases as in the rows named by the meaning.
All inputs are finite; a program needn't handle non-finite values.
Results may differ from a plain program's by a relative error of at most 0.014.
Values may be sent and summed in bfloat16 or wider, within the bound.
No kernel may reach another device: no remote copies, remote signals or barrier semaphores. Data moves between devices by JAX's collectives and lax.ppermute only.
A program may use at most 128 MiB of HBM per device.

v0:
```python
from functools import partial

import jax
import jax.numpy as jnp
from jax import lax
from jax.sharding import PartitionSpec as P

HEAD_DIM = 64


epsilon = 1e-05
masked = -1e30


def whole_sequence(values):
    return lax.all_gather(values, "tensor", axis=0, tiled=True)


def share_of_sum(values):
    return lax.psum_scatter(values, "tensor", scatter_dimension=0, tiled=True)


def feature_totals(left_terms, right_terms):
    return lax.psum((jnp.sum(left_terms, axis=-1), jnp.sum(right_terms, axis=-1)), "tensor")


def matmul(left_side, right_side):
    return jnp.dot(left_side, right_side, preferred_element_type=jnp.float32)


def matmul_transposed(left_side, right_side):
    return lax.dot_general(
        left_side, right_side, (((1,), (1,)), ((), ())), preferred_element_type=jnp.float32
    )


def row_contract(left_side, right_side):
    return lax.dot_general(
        left_side, right_side, (((0,), (0,)), ((), ())), preferred_element_type=jnp.float32
    )


def local_stats(values):
    center = jnp.mean(values, axis=-1, keepdims=True)
    spread = jnp.mean(values * values, axis=-1, keepdims=True) - center * center
    inverse = lax.rsqrt(spread + epsilon)
    return ((values - center) * inverse, inverse)


def split_stats(values):
    full_width = values.shape[-1] * lax.axis_size("tensor")
    row_total, squares = feature_totals(values, values * values)
    center = (row_total / full_width)[:, None]
    inverse = lax.rsqrt((squares / full_width)[:, None] - center * center + epsilon)
    return ((values - center) * inverse, inverse)


def local_back(grad_out, normal, inverse, gain_row):
    scaled = grad_out * gain_row
    return inverse * (
        scaled
        - jnp.mean(scaled, axis=-1, keepdims=True)
        - normal * jnp.mean(scaled * normal, axis=-1, keepdims=True)
    )


def split_back(grad_out, normal, inverse, gain_row):
    full_width = grad_out.shape[-1] * lax.axis_size("tensor")
    scaled = grad_out * gain_row
    row_total, crossed = feature_totals(scaled, scaled * normal)
    return inverse * (
        scaled - (row_total / full_width)[:, None] - normal * (crossed / full_width)[:, None]
    )


def on_device(
    tokens,
    cotangent,
    prefix,
    query_weight,
    key_weight,
    value_weight,
    out_weight,
    up_weight,
    down_weight,
    model_vectors,
    head_vectors,
    hidden_vectors,
):
    query_full, key_full, value_full, out_full, up_full, down_full = (
        lax.all_gather(query_weight, "dp", axis=0, tiled=True),
        lax.all_gather(key_weight, "dp", axis=0, tiled=True),
        lax.all_gather(value_weight, "dp", axis=0, tiled=True),
        lax.all_gather(out_weight, "dp", axis=0, tiled=True),
        lax.all_gather(up_weight, "dp", axis=0, tiled=True),
        lax.all_gather(down_weight, "dp", axis=0, tiled=True),
    )
    inputs = tokens.astype(jnp.float32)
    prefix_len = prefix[0]
    normal_one, inverse_one = local_stats(inputs)
    attend_in = whole_sequence(
        (normal_one * model_vectors[0] + model_vectors[1]).astype(jnp.bfloat16)
    )
    query_states = (matmul(attend_in, query_full) + head_vectors[0]).astype(jnp.bfloat16)
    key_states = matmul(attend_in, key_full).astype(jnp.bfloat16)
    value_states = (matmul(attend_in, value_full) + head_vectors[1]).astype(jnp.bfloat16)
    length = attend_in.shape[0]
    head_count = query_states.shape[1] // HEAD_DIM
    block_rows = min(512, length)
    block_count = length // block_rows
    key_split = key_states.reshape(length, head_count, HEAD_DIM)
    value_split = value_states.reshape(length, head_count, HEAD_DIM)
    columns = jnp.arange(length, dtype=jnp.int32)

    def allowed(first_row):
        places = first_row + jnp.arange(block_rows, dtype=jnp.int32)
        return (columns[None, :] <= places[:, None]) | (columns[None, :] < prefix_len)

    def block_scores(first_row):
        query_rows = lax.dynamic_slice_in_dim(query_states, first_row, block_rows, 0).reshape(
            block_rows, head_count, HEAD_DIM
        )
        scores = (
            jnp.einsum("qhd,khd->hqk", query_rows, key_split, preferred_element_type=jnp.float32)
            * 0.125
        )
        return (query_rows, jnp.where(allowed(first_row)[None], scores, masked))

    def forward_block(block_index):
        query_rows, scores = block_scores(block_index * block_rows)
        row_max = jnp.max(scores, axis=-1, keepdims=True)
        raised = jnp.exp(scores - row_max)
        totals = jnp.sum(raised, axis=-1, keepdims=True)
        softmax_out = (raised / totals).astype(jnp.bfloat16)
        attended_rows = jnp.einsum(
            "hqk,khd->qhd", softmax_out, value_split, preferred_element_type=jnp.float32
        )
        return (
            attended_rows.reshape(block_rows, head_count * HEAD_DIM),
            (row_max + jnp.log(totals))[..., 0],
        )

    attended_blocks, log_totals = lax.map(forward_block, jnp.arange(block_count, dtype=jnp.int32))
    attended = attended_blocks.reshape(length, head_count * HEAD_DIM)
    normal_two, inverse_two = split_stats(attended)
    mixed_in = (normal_two * head_vectors[2] + head_vectors[3]).astype(jnp.bfloat16)
    middle = inputs + share_of_sum(matmul_transposed(mixed_in, out_full)) + model_vectors[2]
    normal_three, inverse_three = local_stats(middle)
    feed_in = whole_sequence(
        (normal_three * model_vectors[3] + model_vectors[4]).astype(jnp.bfloat16)
    )
    before = matmul(feed_in, up_full) + hidden_vectors[0]
    hidden, gelu_pull = jax.vjp(partial(jax.nn.gelu, approximate=False), before)
    normal_four, inverse_four = split_stats(hidden)
    feed_mid = (normal_four * hidden_vectors[1] + hidden_vectors[2]).astype(jnp.bfloat16)
    result = middle + share_of_sum(matmul_transposed(feed_mid, down_full)) + model_vectors[5]
    output = result.astype(jnp.bfloat16)
    grad_out = cotangent.astype(jnp.float32)
    grad_full = whole_sequence(cotangent)
    down_grad = row_contract(grad_full, feed_mid)
    mid_grad = matmul(grad_full, down_full)
    feed_gain_grad = jnp.sum(mid_grad * normal_four, axis=0)
    feed_offset_grad = jnp.sum(mid_grad, axis=0)
    hidden_grad = split_back(mid_grad, normal_four, inverse_four, hidden_vectors[1])
    before_grad = gelu_pull(hidden_grad)[0].astype(jnp.bfloat16)
    up_bias_grad = jnp.sum(before_grad, axis=0, dtype=jnp.float32)
    up_grad = row_contract(feed_in, before_grad)
    feed_in_grad = share_of_sum(matmul_transposed(before_grad, up_full))
    second_gain_grad = jnp.sum(feed_in_grad * normal_three, axis=0)
    second_offset_grad = jnp.sum(feed_in_grad, axis=0)
    middle_grad = grad_out + local_back(feed_in_grad, normal_three, inverse_three, model_vectors[3])
    down_bias_grad = jnp.sum(grad_out, axis=0)
    branch_grad = middle_grad.astype(jnp.bfloat16)
    out_bias_grad = jnp.sum(branch_grad, axis=0, dtype=jnp.float32)
    branch_full = whole_sequence(branch_grad)
    out_grad = row_contract(branch_full, mixed_in)
    mixed_grad = matmul(branch_full, out_full)
    attend_gain_grad = jnp.sum(mixed_grad * normal_two, axis=0)
    attend_offset_grad = jnp.sum(mixed_grad, axis=0)
    attended_grad = split_back(mixed_grad, normal_two, inverse_two, head_vectors[2]).astype(
        jnp.bfloat16
    )

    def backward_block(running, block_item):
        key_total, value_total = running
        block_index, log_rows = block_item
        first_row = block_index * block_rows
        query_rows, scores = block_scores(first_row)
        grad_rows = lax.dynamic_slice_in_dim(attended_grad, first_row, block_rows, 0).reshape(
            block_rows, head_count, HEAD_DIM
        )
        softmax_out = jnp.exp(scores - log_rows[..., None])
        prob_grad = jnp.einsum(
            "qhd,khd->hqk", grad_rows, value_split, preferred_element_type=jnp.float32
        )
        score_grad = (
            softmax_out * (prob_grad - jnp.sum(softmax_out * prob_grad, axis=-1, keepdims=True))
        ).astype(jnp.bfloat16)
        query_block = (
            jnp.einsum("hqk,khd->qhd", score_grad, key_split, preferred_element_type=jnp.float32)
            * 0.125
        ).astype(jnp.bfloat16)
        key_total = (
            key_total
            + jnp.einsum("hqk,qhd->khd", score_grad, query_rows, preferred_element_type=jnp.float32)
            * 0.125
        )
        value_total = value_total + jnp.einsum(
            "hqk,qhd->khd",
            softmax_out.astype(jnp.bfloat16),
            grad_rows,
            preferred_element_type=jnp.float32,
        )
        return ((key_total, value_total), query_block.reshape(block_rows, head_count * HEAD_DIM))

    empty_grad = jnp.zeros((length, head_count, HEAD_DIM), jnp.float32)
    (key_total, value_total), query_blocks = lax.scan(
        backward_block,
        (empty_grad, empty_grad),
        (jnp.arange(block_count, dtype=jnp.int32), log_totals),
    )
    query_grad = query_blocks.reshape(length, head_count * HEAD_DIM)
    key_grad = key_total.reshape(length, head_count * HEAD_DIM).astype(jnp.bfloat16)
    value_grad = value_total.reshape(length, head_count * HEAD_DIM).astype(jnp.bfloat16)
    query_bias_grad = jnp.sum(query_grad, axis=0, dtype=jnp.float32)
    value_bias_grad = jnp.sum(value_grad, axis=0, dtype=jnp.float32)
    query_weight_grad = row_contract(attend_in, query_grad)
    key_weight_grad = row_contract(attend_in, key_grad)
    value_weight_grad = row_contract(attend_in, value_grad)
    attend_in_grad = share_of_sum(
        matmul_transposed(query_grad, query_full)
        + matmul_transposed(key_grad, key_full)
        + matmul_transposed(value_grad, value_full)
    )
    first_gain_grad = jnp.sum(attend_in_grad * normal_one, axis=0)
    first_offset_grad = jnp.sum(attend_in_grad, axis=0)
    input_grad = middle_grad + local_back(attend_in_grad, normal_one, inverse_one, model_vectors[0])
    query_weight_grad, key_weight_grad, value_weight_grad, out_grad, up_grad, down_grad = (
        lax.psum_scatter(query_weight_grad, "dp", scatter_dimension=0, tiled=True),
        lax.psum_scatter(key_weight_grad, "dp", scatter_dimension=0, tiled=True),
        lax.psum_scatter(value_weight_grad, "dp", scatter_dimension=0, tiled=True),
        lax.psum_scatter(out_grad, "dp", scatter_dimension=0, tiled=True),
        lax.psum_scatter(up_grad, "dp", scatter_dimension=0, tiled=True),
        lax.psum_scatter(down_grad, "dp", scatter_dimension=0, tiled=True),
    )
    model_grads = jnp.stack(
        [
            first_gain_grad,
            first_offset_grad,
            out_bias_grad,
            second_gain_grad,
            second_offset_grad,
            down_bias_grad,
        ]
    )
    head_grads = jnp.stack([query_bias_grad, value_bias_grad, attend_gain_grad, attend_offset_grad])
    hidden_grads = jnp.stack([up_bias_grad, feed_gain_grad, feed_offset_grad])
    model_sum = lax.psum(model_grads, ("dp", "tensor"))
    head_sum, hidden_sum = lax.psum((head_grads, hidden_grads), "dp")
    return (
        output,
        input_grad,
        query_weight_grad,
        key_weight_grad,
        value_weight_grad,
        out_grad,
        up_grad,
        down_grad,
        model_sum,
        head_sum,
        hidden_sum,
    )


def solution(mesh):
    return jax.shard_map(
        on_device,
        mesh=mesh,
        in_specs=(
            P(("dp", "tensor"), None),
            P(("dp", "tensor"), None),
            P("dp"),
            P("dp", "tensor"),
            P("dp", "tensor"),
            P("dp", "tensor"),
            P("dp", "tensor"),
            P("dp", "tensor"),
            P("dp", "tensor"),
            P(),
            P(None, "tensor"),
            P(None, "tensor"),
        ),
        out_specs=(
            P(("dp", "tensor"), None),
            P(("dp", "tensor"), None),
            P("dp", "tensor"),
            P("dp", "tensor"),
            P("dp", "tensor"),
            P("dp", "tensor"),
            P("dp", "tensor"),
            P("dp", "tensor"),
            P(),
            P(None, "tensor"),
            P(None, "tensor"),
        ),
        check_vma=False,
    )
```

profile of v0, /device:TPU:0, one launch (start us, length us, event | category | flops | bytes accessed | tf_op | source)
XLA Modules:
  0.0 1363.6 jit_solution(14468043002619853265)
XLA Ops:
  14.3 45.8 %all_gather.31 = bf16[768,384]{1,0:T(8,128)(2,1)S(1)} all-gather(bf16[48,384]{1,0:T(8,128)(2,1)S(1)} %copy-done.31), channel_id=1, replica_groups=mesh['dp'=16,'tensor'=2] {'dp'}, dimensions={0}, use_global_device_ids=true | all-gather | bytes 626688 | tf_op jit(solution)/shard_map/all_gather | solution.py:91
  60.1 38.9 %all_gather.32 = bf16[768,384]{1,0:T(8,128)(2,1)S(1)} all-gather(bf16[48,384]{1,0:T(8,128)(2,1)S(1)} %copy-done.32), channel_id=1, replica_groups=mesh['dp'=16,'tensor'=2] {'dp'}, dimensions={0}, use_global_device_ids=true | all-gather | bytes 626688 | tf_op jit(solution)/shard_map/all_gather | solution.py:92
  99.1 43.4 %all_gather.33 = bf16[768,384]{1,0:T(8,128)(2,1)} all-gather(bf16[48,384]{1,0:T(8,128)(2,1)S(1)} %copy-done.33), channel_id=1, replica_groups=mesh['dp'=16,'tensor'=2] {'dp'}, dimensions={0}, use_global_device_ids=true | all-gather | bytes 626688 | tf_op jit(solution)/shard_map/all_gather | solution.py:93
  142.4 41.9 %all_gather.34 = bf16[768,384]{1,0:T(8,128)(2,1)} all-gather(bf16[48,384]{1,0:T(8,128)(2,1)S(1)} %copy-done.34), channel_id=1, replica_groups=mesh['dp'=16,'tensor'=2] {'dp'}, dimensions={0}, use_global_device_ids=true | all-gather | bytes 626688 | tf_op jit(solution)/shard_map/all_gather | solution.py:94
  190.3 27.0 %while.30 = (s32[]{:T(128)}, f32[2,512,384]{1,2,0:T(8,128)}, f32[2,6,512]{2,1,0:T(8,128)S(1)}, s32[2]{0:T(128)S(1)}, s32[]{:T(128)}, /*index=5*/bf16[1024,384]{0...) while((s32[]{:T(128)}, f32[2,512,384]{1,2,0:T(8,128)}, ...), condition=%wide.region_5.6_spmd.clone.clone, body=%wide.region_2.5_spmd.clone.clone.sunk | while | flops 844102144 | bytes 57657604 | solution.py:143
  231.8 7.2 reduce-scatter.13.cloned.1.call-done
  246.1 46.9 %all-gather.11.cloned.1.call-done = bf16[768,1536]{1,0:T(8,128)(2,1)} async-done(((bf16[48,1536]{1,0:T(8,128)(2,1)}), bf16[768,1536]{1,0:T(8,128)(2,1)}) %all-gather.11.cloned.1.call-update) | async-done | bytes 2359312 | tf_op jit(solution)/shard_map/all_gather | solution.py:95
  293.0 10.1 all-gather.9.cloned.1.call-done
  303.1 20.9 %fusion.41 = (f32[1024]{0:T(1024)S(1)}, f32[1024]{0:T(1024)S(1)}, f32[1024,1536]{1,0:T(8,128)}, f32[1024,1536]{1,0:T(8,128)}, f32[1024,1536]{1,0:T(8,128)}) fusion(f32[1536]{0:T(1024)S(1)} %get-tuple-element.361, bf16[1024,768]{1,0:T(8,128)(2,1)} %all-gather.9.cloned.1.call-done, bf16[768,1536]{1,0:T(8,128)(2,1)} %all-gather.11.cloned.1.call-done), kind=kOutput, calls=%fused_computation.136 | convolution fusion | flops 2522871808 | bytes 22820864 | tf_op jit(solution)/shard_map/dot_general | solution.py:28
  326.5 55.1 %all-gather.13.cloned.1.call-done = bf16[768,1536]{1,0:T(8,128)(2,1)} async-done(((bf16[48,1536]{1,0:T(8,128)(2,1)}), bf16[768,1536]{1,0:T(8,128)(2,1)}) %all-gather.13.cloned.1.call-update) | async-done | bytes 2359312 | tf_op jit(solution)/shard_map/all_gather | solution.py:96
  381.6 10.3 multiply_reduce_fusion.1
  394.3 13.5 convert_reduce_fusion
  413.9 6.9 fusion.48
  426.8 11.4 reduce-scatter.15.cloned.1.call-done
  444.0 11.0 all-gather.17.cloned.1.call-done
  465.4 60.8 %while.31 = (s32[]{:T(128)}, f32[1024,6,64]{0,2,1:T(8,128)}, f32[1024,6,64]{0,2,1:T(8,128)}, bf16[2,512,384]{1,2,0:T(8,128)(2,1)}, s32[2]{0:T(128)S(1)}, /*index...) while((s32[]{:T(128)}, f32[1024,6,64]{0,2,1:T(8,128)}, ...), condition=%wide.region_31.32_spmd.clone.clone, body=%wide.region_29.31_spmd.clone.clone.sunk | while | flops 2063858176 | bytes 154364368 | solution.py:217
  552.1 6.1 copy.40
  571.5 78.3 %all-reduce = (f32[4,384]{1,0:T(4,128)}, f32[3,1536]{1,0:T(4,128)}) all-reduce(f32[4,384]{1,0:T(4,128)S(1)} %pad_maximum_fusion.1, f32[3,1536]{1,0:T(4,128)S(1)} %pad_maximum_fusion), channel_id=1, replica_groups=mesh['dp'=16,'tensor'=2] {'dp'}, use_global_device_ids=true, to_apply=%region_52.53 | all-reduce | flops 6144 | bytes 49152 | tf_op jit(solution)/shard_map/psum | solution.py:259
  652.1 38.5 %psum.85 = f32[6,768]{1,0:T(8,128)} all-reduce(f32[6,768]{1,0:T(8,128)S(1)} %stack.54), channel_id=1, replica_groups=mesh['dp'=16,'tensor'=2] {'dp','tensor'}, use_global_device_ids=true, to_apply=%region_47.48 | all-reduce | flops 4608 | bytes 36864 | tf_op jit(solution)/shard_map/psum | solution.py:258
  695.8 143.2 %reduce-scatter.31.cloned.1.call-done = f32[48,1536]{1,0:T(8,128)} async-done(((f32[768,1536]{1,0:T(8,128)}), f32[48,1536]{1,0:T(8,128)}) %reduce-scatter.31.cloned.1.call-update) | async-done | bytes 294928
  839.0 129.2 %reduce-scatter.27.cloned.1.call-done = f32[48,384]{1,0:T(8,128)} async-done(((f32[768,384]{1,0:T(8,128)}), f32[48,384]{1,0:T(8,128)}) %reduce-scatter.27.cloned.1.call-update) | async-done | bytes 73744 | tf_op jit(solution)/shard_map/reduce_scatter | solution.py:242
  968.2 129.4 %reduce-scatter.25.cloned.1.call-done = f32[48,384]{1,0:T(8,128)} async-done(((f32[768,384]{1,0:T(8,128)}), f32[48,384]{1,0:T(8,128)}) %reduce-scatter.25.cloned.1.call-update) | async-done | bytes 73744 | tf_op jit(solution)/shard_map/reduce_scatter | solution.py:241
  1097.6 129.2 %reduce-scatter.23.cloned.1.call-done = f32[48,384]{1,0:T(8,128)} async-done(((f32[768,384]{1,0:T(8,128)}), f32[48,384]{1,0:T(8,128)}) %reduce-scatter.23.cloned.1.call-update) | async-done | bytes 73744 | tf_op jit(solution)/shard_map/reduce_scatter | solution.py:240
  1226.8 129.4 %reduce-scatter.21.cloned.1.call-done = f32[48,384]{1,0:T(8,128)} async-done(((f32[768,384]{1,0:T(8,128)}), f32[48,384]{1,0:T(8,128)}) %reduce-scatter.21.cloned.1.call-update) | async-done | bytes 73744 | tf_op jit(solution)/shard_map/reduce_scatter | solution.py:239
  (288 shorter events, 197.2 us)
Async XLA Ops:
  8.0 91.0 %copy-start.33 = (bf16[48,384]{1,0:T(8,128)(2,1)S(1)}, bf16[48,384]{1,0:T(8,128)(2,1)}, u32[]{:S(2)}) copy-start(bf16[48,384]{1,0:T(8,128)(2,1)} %param.21) | copy-start | bytes 110596
  8.0 134.4 %copy-start.34 = (bf16[48,384]{1,0:T(8,128)(2,1)S(1)}, bf16[48,384]{1,0:T(8,128)(2,1)}, u32[]{:S(2)}) copy-start(bf16[48,384]{1,0:T(8,128)(2,1)} %param.22) | copy-start | bytes 110596
  8.1 176.2 %all-gather.7.cloned.1.call-start = ((), (), s32[]{:S(2)}) async-start(), calls=%async_computation.10 | async-start | bytes 2359296 | tf_op jit(solution)/shard_map/all_gather | solution.py:16
  14.2 224.8 %reduce-scatter.13.cloned.1.call-start = ((), (), s32[]{:S(2)}) async-start(), calls=%async_computation.11 | async-start | bytes 4718592 | tf_op jit(solution)/shard_map/reduce_scatter | solution.py:20
  60.1 124.2 %copy-start.23 = (bf16[768,384]{1,0:T(8,128)(2,1)}, bf16[768,384]{1,0:T(8,128)(2,1)S(1)}, u32[]{:S(2)}) copy-start(bf16[768,384]{1,0:T(8,128)(2,1)S(1)} %all_gather.31) | copy-start | bytes 1769476
  99.1 87.9 %copy-start.25 = (bf16[768,384]{1,0:T(8,128)(2,1)}, bf16[768,384]{1,0:T(8,128)(2,1)S(1)}, u32[]{:S(2)}) copy-start(bf16[768,384]{1,0:T(8,128)(2,1)S(1)} %all_gather.32) | copy-start | bytes 1769476
  230.8 62.2 %all-gather.11.cloned.1.call-start = ((), (), s32[]{:S(2)}) async-start(), calls=%async_computation.13 | async-start | bytes 2506752 | tf_op jit(solution)/shard_map/all_gather | solution.py:95
  231.4 71.7 %all-gather.9.cloned.1.call-start = ((), (), s32[]{:S(2)}) async-start(), calls=%async_computation.12 | async-start | bytes 2359296 | tf_op jit(solution)/shard_map/all_gather | solution.py:16
  244.7 81.8 %all-gather.15.cloned.1.call-start = ((), (), s32[]{:S(2)}) async-start(), calls=%async_computation.16 | async-start | bytes 2359296 | tf_op jit(solution)/shard_map/all_gather | solution.py:16
  245.2 136.3 %all-gather.13.cloned.1.call-start = ((), (), s32[]{:S(2)}) async-start(), calls=%async_computation.14 | async-start | bytes 2506752 | tf_op jit(solution)/shard_map/all_gather | solution.py:96
  246.0 177.6 %reduce-scatter.17.cloned.1.call-start = ((), (), s32[]{:S(2)}) async-start(), calls=%async_computation.17 | async-start | bytes 4718592 | tf_op jit(solution)/shard_map/reduce_scatter | solution.py:20
  413.9 24.3 %reduce-scatter.15.cloned.1.call-start = ((), (), s32[]{:S(2)}) async-start(), calls=%async_computation.15 | async-start | bytes 4718592 | tf_op jit(solution)/shard_map/reduce_scatter | solution.py:20
  420.9 34.1 %all-gather.17.cloned.1.call-start = ((), (), s32[]{:S(2)}) async-start(), calls=%async_computation.18 | async-start | bytes 2359296 | tf_op jit(solution)/shard_map/all_gather | solution.py:16
  443.9 205.9 %reduce-scatter.19.cloned.1.call-start = ((), (), s32[]{:S(2)}) async-start(), calls=%async_computation.19 | async-start | bytes 4718592 | tf_op jit(solution)/shard_map/reduce_scatter | solution.py:20
  536.3 159.5 %reduce-scatter.29.cloned.1.call-start = ((), (), s32[]{:S(2)}) async-start(), calls=%async_computation.24 | async-start | bytes 5013504 | tf_op jit(solution)/shard_map/reduce_scatter | solution.py:243
  544.0 295.0 %reduce-scatter.31.cloned.1.call-start = ((), (), s32[]{:S(2)}) async-start(), calls=%async_computation.25 | async-start | bytes 5013504
  558.3 409.9 %reduce-scatter.27.cloned.1.call-start = ((), (), s32[]{:S(2)}) async-start(), calls=%async_computation.23 | async-start | bytes 1253376 | tf_op jit(solution)/shard_map/reduce_scatter | solution.py:242
  562.9 534.7 %reduce-scatter.25.cloned.1.call-start = ((), (), s32[]{:S(2)}) async-start(), calls=%async_computation.22 | async-start | bytes 1253376 | tf_op jit(solution)/shard_map/reduce_scatter | solution.py:241
  565.0 661.8 %reduce-scatter.23.cloned.1.call-start = ((), (), s32[]{:S(2)}) async-start(), calls=%async_computation.21 | async-start | bytes 1253376 | tf_op jit(solution)/shard_map/reduce_scatter | solution.py:240
  567.3 82.5 %copy-start.5 = (bf16[512,768]{1,0:T(8,128)(2,1)S(1)}, bf16[512,768]{1,0:T(8,128)(2,1)}, u32[]{:S(2)}) copy-start(bf16[512,768]{1,0:T(8,128)(2,1)} %param.16) | copy-start | bytes 2359300
  567.3 82.5 %copy-start.30 = (f32[768]{0:T(1024)S(1)}, f32[768]{0:T(1024)}, u32[]{:S(2)}) copy-start(f32[768]{0:T(1024)} %copy-done.29) | copy-start | bytes 9220
  567.3 82.5 %copy-start.36 = (f32[512]{0:T(512)S(1)}, f32[512]{0:T(512)}, u32[]{:S(2)}) copy-start(f32[512]{0:T(512)} %copy-done.35) | copy-start | bytes 6148
  567.3 788.8 %reduce-scatter.21.cloned.1.call-start = ((), (), s32[]{:S(2)}) async-start(), calls=%async_computation.20 | async-start | bytes 1253376 | tf_op jit(solution)/shard_map/reduce_scatter | solution.py:239
  570.9 119.6 %copy-start.8 = (f32[512,768]{1,0:T(8,128)S(1)}, f32[512,768]{1,0:T(8,128)}, u32[]{:S(2)}) copy-start(f32[512,768]{1,0:T(8,128)} %get-tuple-element.421) | copy-start | bytes 4718596
  (55 other events, 340.0 us)
Sparse Core Ops, SparseCore 0:
  14.3 12.5 all-gather.6
  230.9 8.0 reduce-scatter.12
  414.0 9.5 reduce-scatter.16
  425.7 12.4 reduce-scatter.14
Sparse Core Ops, SparseCore 1:
  234.1 58.9 all-gather.10
  295.0 8.1 all-gather.8
  304.5 10.9 all-gather.14
  318.3 63.2 all-gather.12
  444.0 10.9 all-gather.16
  536.4 12.2 reduce-scatter.18
  554.3 141.5 reduce-scatter.28
  701.4 137.6 reduce-scatter.30
  844.2 124.0 reduce-scatter.26
  973.6 123.9 reduce-scatter.24
  1102.8 123.9 reduce-scatter.22
  1232.1 123.9 reduce-scatter.20
where the time goes:
time: 1370 us; the launch traced here: 1360 us
  waiting for transfers between devices  809 us (59%)
  blocking collectives  297 us (22%)
  matrix products  137 us (10%)
  other arithmetic  69 us (5%)
  local copies, waits for them, and re-layouts  30.9 us (2%)
  between operations  16.5 us (1%)
    unnamed x17, waiting for transfers between devices  145 us
    reduce_scatter x1, waiting for transfers between devices, on_device(): lax.psum_scatter(value_weight_grad, 'dp', scatter_dimension=0, tiled=True)  129 us
    reduce_scatter x1, waiting for transfers between devices, on_device(): lax.psum_scatter(query_weight_grad, 'dp', scatter_dimension=0, tiled=True)  129 us
    reduce_scatter x1, waiting for transfers between devices, on_device(): lax.psum_scatter(out_grad, 'dp', scatter_dimension=0, tiled=True)  129 us
    reduce_scatter x1, waiting for transfers between devices, on_device(): lax.psum_scatter(key_weight_grad, 'dp', scatter_dimension=0, tiled=True)  129 us
    psum x1, blocking collectives, on_device(): head_sum, hidden_sum = lax.psum((head_grads, hidden_grads), 'dp')  78.3 us
    all_gather x1, waiting for transfers between devices, on_device(): lax.all_gather(down_weight, 'dp', axis=0, tiled=True)  55.1 us
    all_gather x1, waiting for transfers between devices, on_device(): lax.all_gather(up_weight, 'dp', axis=0, tiled=True)  46.9 us
  transfers between devices with their start and end apart: 16, of which 13 were waited for; matrix products, arithmetic and copies ran while one was open for 5% of the time, Pallas kernels for 0%

commit v1 on v0

--- a/solution.py
+++ b/solution.py
@@ -3,6 +3,8 @@
 import jax
 import jax.numpy as jnp
 from jax import lax
+from jax.experimental import pallas as pl
+from jax.experimental.pallas import tpu as pltpu
 from jax.sharding import PartitionSpec as P
 
 HEAD_DIM = 64
@@ -12,16 +14,207 @@
 masked = -1e30
 
 
+def flip_partner(values):
+    return lax.ppermute(values, "tensor", [(0, 1), (1, 0)])
+
+
 def whole_sequence(values):
-    return lax.all_gather(values, "tensor", axis=0, tiled=True)
+    other = flip_partner(values)
+    first = lax.axis_index("tensor") == 0
+    return jnp.where(
+        first, jnp.concatenate([values, other], 0), jnp.concatenate([other, values], 0)
+    )
 
 
 def share_of_sum(values):
-    return lax.psum_scatter(values, "tensor", scatter_dimension=0, tiled=True)
+    halves = values.reshape(2, values.shape[0] // 2, values.shape[1])
+    core = lax.axis_index("tensor")
+    mine = lax.dynamic_index_in_dim(halves, core, 0, keepdims=False)
+    theirs = lax.dynamic_index_in_dim(halves, 1 - core, 0, keepdims=False)
+    return mine + flip_partner(theirs.astype(jnp.bfloat16)).astype(jnp.float32)
 
 
 def feature_totals(left_terms, right_terms):
-    return lax.psum((jnp.sum(left_terms, axis=-1), jnp.sum(right_terms, axis=-1)), "tensor")
+    totals = jnp.stack([jnp.sum(left_terms, axis=-1), jnp.sum(right_terms, axis=-1)])
+    totals = totals + flip_partner(totals)
+    return totals[0], totals[1]
+
+
+class Ring:
+    def __init__(self, size):
+        self.size = size
+        rest, stride = size // 4, 4
+        self.lines = []
+        while rest > 1:
+            factor = 4 if rest % 4 == 0 else 2 if rest % 2 == 0 else rest
+            self.lines.append((factor, stride))
+            rest, stride = rest // factor, stride * factor
+        self.line_count = size // 4
+
+    def shift(self, values, factor, stride, step):
+        pairs = []
+        for place in range(self.size):
+            digit = place // stride % factor
+            pairs.append((place, place + ((digit + step) % factor - digit) * stride))
+        return lax.ppermute(values, "dp", pairs)
+
+    def flip(self, values, stride):
+        return self.shift(values, 2, stride, 1)
+
+    def line_places(self, sign):
+        own = lax.axis_index("dp")
+        places = [jnp.int32(0)]
+        for factor, stride in self.lines:
+            digit = own // stride % factor
+            places = [
+                base + (digit + sign * step) % factor * stride
+                for base in places
+                for step in range(factor)
+            ]
+        return places
+
+    def gather_order(self):
+        own = lax.axis_index("dp")
+        places = self.line_places_gather()
+        return jnp.stack([base + (own % 4 ^ bits) for bits in (0, 1, 2, 3) for base in places])
+
+    def line_places_gather(self):
+        own = lax.axis_index("dp")
+        places = [jnp.int32(0)]
+        for factor, stride in self.lines:
+            digit = own // stride % factor
+            places = [
+                base + (digit + factor - step) % factor * stride
+                for step in range(factor)
+                for base in places
+            ]
+        return places
+
+    def gather(self, values):
+        block = values
+        for factor, stride in self.lines:
+            block = jnp.concatenate(
+                [block] + [self.shift(block, factor, stride, step) for step in range(1, factor)], 0
+            )
+        from_x, from_y = self.flip(block, 1), self.flip(block, 2)
+        half = block.shape[0] // 2
+        corner = (self.flip(from_x[:half], 2), self.flip(from_y[half:], 1))
+        return (block, from_x, from_y) + corner
+
+    def scatter_order(self, first_bit):
+        own = lax.axis_index("dp")
+        other_bit = 3 - first_bit
+        places = self.line_places(1)
+        return jnp.stack(
+            [
+                base + (own % 4 ^ (cross + side))
+                for cross in (0, first_bit)
+                for side in (0, other_bit)
+                for base in places
+            ]
+        )
+
+    def square_sum(self, keep, send, first_bit):
+        f32 = jnp.float32
+        half = keep.shape[0] // 2
+        got = self.flip(send, first_bit)
+        away = (keep[half:].astype(f32) + got[half:].astype(f32)).astype(jnp.bfloat16)
+        second = self.flip(away, 3 - first_bit)
+        return keep[:half].astype(f32) + got[:half].astype(f32) + second.astype(f32)
+
+    def scatter(self, pair_one, pair_two):
+        total = jnp.concatenate(
+            [self.square_sum(*pair_one, 1), self.square_sum(*pair_two, 2)], axis=1
+        )
+        for factor, stride in self.lines:
+            rows = total.shape[0] // factor
+            rounded = total.astype(jnp.bfloat16)
+            running = total[:rows]
+            for step in range(1, factor):
+                got = self.shift(rounded[step * rows : (step + 1) * rows], factor, stride, step)
+                running = running + got.astype(jnp.float32)
+            total = running
+        return total
+
+    def all_sum(self, values):
+        stride = 1
+        while stride < self.size:
+            values = values + self.flip(values, stride)
+            stride *= 2
+        return values
+
+
+def assemble(order, pieces, widths):
+    rows = pieces[0].shape[0]
+    count = order.shape[0]
+    shard = rows // (count // 4)
+
+    def body(order_ref, own, from_x, from_y, corner_a, corner_b, *outs):
+        blocks = [(own, 0), (from_x, 0), (from_y, 0)]
+        for block in range(count):
+            kind, inner = divmod(block, count // 4)
+            start = inner * shard
+            if kind < 3:
+                ref = blocks[kind][0]
+            elif start < rows // 2:
+                ref = corner_a
+            else:
+                ref, start = corner_b, start - rows // 2
+            place = pl.multiple_of(order_ref[block] * shard, 16)
+            left = 0
+            for out, width in zip(outs, widths):
+                out[pl.ds(place, shard), :] = ref[start : start + shard, left : left + width]
+                left += width
+
+    return pl.pallas_call(
+        body,
+        out_shape=[jax.ShapeDtypeStruct((count * shard, width), jnp.bfloat16) for width in widths],
+        in_specs=[pl.BlockSpec(memory_space=pltpu.SMEM)]
+        + [pl.BlockSpec(memory_space=pltpu.VMEM)] * 5,
+        out_specs=[pl.BlockSpec(memory_space=pltpu.VMEM)] * len(widths),
+    )(order, *pieces)
+
+
+def weight_grad(order, left_side, right_side):
+    tokens, features = left_side.shape
+    width = right_side.shape[1]
+    count = order.shape[0]
+    shard = features // count
+    tile = 384
+
+    def body(order_ref, left, right, keep, send, turned, total):
+        @pl.when(pl.program_id(0) == 0)
+        def _():
+            turned[...] = left[...].T
+
+        total[...] = jnp.dot(turned[...], right[...], preferred_element_type=jnp.float32)
+        for block in range(count):
+            place = pl.multiple_of(order_ref[block] * shard, 16)
+            out, at = (keep, block) if block < count // 2 else (send, block - count // 2)
+            out[at * shard : (at + 1) * shard, :] = total[pl.ds(place, shard), :].astype(
+                jnp.bfloat16
+            )
+
+    return pl.pallas_call(
+        body,
+        grid=(width // tile,),
+        out_shape=[jax.ShapeDtypeStruct((features // 2, width), jnp.bfloat16)] * 2,
+        in_specs=[
+            pl.BlockSpec(memory_space=pltpu.SMEM),
+            pl.BlockSpec((tokens, features), lambda i: (0, 0)),
+            pl.BlockSpec((tokens, tile), lambda i: (0, i)),
+        ],
+        out_specs=[pl.BlockSpec((features // 2, tile), lambda i: (0, i))] * 2,
+        scratch_shapes=[
+            pltpu.VMEM((features, tokens), jnp.bfloat16),
+            pltpu.VMEM((features, tile), jnp.float32),
+        ],
+        cost_estimate=pl.CostEstimate(
+            flops=2 * tokens * features * width,
+            bytes_accessed=2 * (tokens * features + tokens * width + features * width),
+            transcendentals=0,
+        ),
+    )(order, left_side, right_side)
 
 
 def matmul(left_side, right_side):
@@ -31,12 +224,6 @@
 def matmul_transposed(left_side, right_side):
     return lax.dot_general(
         left_side, right_side, (((1,), (1,)), ((), ())), preferred_element_type=jnp.float32
-    )
-
-
-def row_contract(left_side, right_side):
-    return lax.dot_general(
-        left_side, right_side, (((0,), (0,)), ((), ())), preferred_element_type=jnp.float32
     )
 
 
@@ -87,14 +274,19 @@
     head_vectors,
     hidden_vectors,
 ):
-    query_full, key_full, value_full, out_full, up_full, down_full = (
-        lax.all_gather(query_weight, "dp", axis=0, tiled=True),
-        lax.all_gather(key_weight, "dp", axis=0, tiled=True),
-        lax.all_gather(value_weight, "dp", axis=0, tiled=True),
-        lax.all_gather(out_weight, "dp", axis=0, tiled=True),
-        lax.all_gather(up_weight, "dp", axis=0, tiled=True),
-        lax.all_gather(down_weight, "dp", axis=0, tiled=True),
-    )
+    ring = Ring(lax.axis_size("dp"))
+    order = ring.gather_order()
+    near, far = ring.scatter_order(1), ring.scatter_order(2)
+    half, full = query_weight.shape[1], up_weight.shape[1]
+    query_full, key_full, value_full = assemble(
+        order,
+        ring.gather(jnp.concatenate([query_weight, key_weight, value_weight], 1)),
+        (half, half, half),
+    )
+    out_full, up_full = assemble(
+        order, ring.gather(jnp.concatenate([out_weight, up_weight], 1)), (half, full)
+    )
+    (down_full,) = assemble(order, ring.gather(down_weight), (full,))
     inputs = tokens.astype(jnp.float32)
     prefix_len = prefix[0]
     normal_one, inverse_one = local_stats(inputs)
@@ -157,14 +349,16 @@
     output = result.astype(jnp.bfloat16)
     grad_out = cotangent.astype(jnp.float32)
     grad_full = whole_sequence(cotangent)
-    down_grad = row_contract(grad_full, feed_mid)
+    down_pair = weight_grad(far, grad_full, feed_mid)
     mid_grad = matmul(grad_full, down_full)
     feed_gain_grad = jnp.sum(mid_grad * normal_four, axis=0)
     feed_offset_grad = jnp.sum(mid_grad, axis=0)
     hidden_grad = split_back(mid_grad, normal_four, inverse_four, hidden_vectors[1])
     before_grad = gelu_pull(hidden_grad)[0].astype(jnp.bfloat16)
     up_bias_grad = jnp.sum(before_grad, axis=0, dtype=jnp.float32)
-    up_grad = row_contract(feed_in, before_grad)
+    up_pair = weight_grad(near, feed_in, before_grad)
+    wide_grads = ring.scatter(up_pair, down_pair)
+    up_grad, down_grad = wide_grads[:, :full], wide_grads[:, full:]
     feed_in_grad = share_of_sum(matmul_transposed(before_grad, up_full))
     second_gain_grad = jnp.sum(feed_in_grad * normal_three, axis=0)
     second_offset_grad = jnp.sum(feed_in_grad, axis=0)
@@ -173,7 +367,7 @@
     branch_grad = middle_grad.astype(jnp.bfloat16)
     out_bias_grad = jnp.sum(branch_grad, axis=0, dtype=jnp.float32)
     branch_full = whole_sequence(branch_grad)
-    out_grad = row_contract(branch_full, mixed_in)
+    out_pair = weight_grad(far, branch_full, mixed_in)
     mixed_grad = matmul(branch_full, out_full)
     attend_gain_grad = jnp.sum(mixed_grad * normal_two, axis=0)
     attend_offset_grad = jnp.sum(mixed_grad, axis=0)
@@ -224,9 +418,13 @@
     value_grad = value_total.reshape(length, head_count * HEAD_DIM).astype(jnp.bfloat16)
     query_bias_grad = jnp.sum(query_grad, axis=0, dtype=jnp.float32)
     value_bias_grad = jnp.sum(value_grad, axis=0, dtype=jnp.float32)
-    query_weight_grad = row_contract(attend_in, query_grad)
-    key_weight_grad = row_contract(attend_in, key_grad)
-    value_weight_grad = row_contract(attend_in, value_grad)
+    query_pair = weight_grad(near, attend_in, jnp.concatenate([query_grad, value_grad], 1))
+    key_pair = weight_grad(far, attend_in, key_grad)
+    second_pair = [jnp.concatenate(both, 1) for both in zip(key_pair, out_pair)]
+    narrow = ring.scatter(query_pair, second_pair)
+    query_weight_grad, value_weight_grad, key_weight_grad, out_grad = (
+        narrow[:, i * half : (i + 1) * half] for i in range(4)
+    )
     attend_in_grad = share_of_sum(
         matmul_transposed(query_grad, query_full)
         + matmul_transposed(key_grad, key_full)
@@ -235,14 +433,6 @@
     first_gain_grad = jnp.sum(attend_in_grad * normal_one, axis=0)
     first_offset_grad = jnp.sum(attend_in_grad, axis=0)
     input_grad = middle_grad + local_back(attend_in_grad, normal_one, inverse_one, model_vectors[0])
-    query_weight_grad, key_weight_grad, value_weight_grad, out_grad, up_grad, down_grad = (
-        lax.psum_scatter(query_weight_grad, "dp", scatter_dimension=0, tiled=True),
-        lax.psum_scatter(key_weight_grad, "dp", scatter_dimension=0, tiled=True),
-        lax.psum_scatter(value_weight_grad, "dp", scatter_dimension=0, tiled=True),
-        lax.psum_scatter(out_grad, "dp", scatter_dimension=0, tiled=True),
-        lax.psum_scatter(up_grad, "dp", scatter_dimension=0, tiled=True),
-        lax.psum_scatter(down_grad, "dp", scatter_dimension=0, tiled=True),
-    )
     model_grads = jnp.stack(
         [
             first_gain_grad,
@@ -255,8 +445,14 @@
     )
     head_grads = jnp.stack([query_bias_grad, value_bias_grad, attend_gain_grad, attend_offset_grad])
     hidden_grads = jnp.stack([up_bias_grad, feed_gain_grad, feed_offset_grad])
-    model_sum = lax.psum(model_grads, ("dp", "tensor"))
-    head_sum, hidden_sum = lax.psum((head_grads, hidden_grads), "dp")
+    model_grads = model_grads + flip_partner(model_grads)
+    sums = ring.all_sum(
+        jnp.concatenate([g.reshape(-1, 128) for g in (model_grads, head_grads, hidden_grads)], 0)
+    )
+    rows_one, rows_two = model_grads.size // 128, head_grads.size // 128
+    model_sum = sums[:rows_one].reshape(model_grads.shape)
+    head_sum = sums[rows_one : rows_one + rows_two].reshape(head_grads.shape)
+    hidden_sum = sums[rows_one + rows_two :].reshape(hidden_grads.shape)
     return (
         output,
         input_grad,

time: 1370 us -> 455 us (0.33)
  waiting for transfers between devices: 809 us -> 102 us
  blocking collectives: 297 us -> 0 us
  starting transfers between devices: 1.03 us -> 52.6 us
  Pallas kernels: 0 us -> 37 us
  matrix products: 137 us -> 108 us
  local copies, waits for them, and re-layouts: 30.9 us -> 57.6 us
  other arithmetic: 69 us -> 85.4 us
  between operations: 16.5 us -> 1.95 us
    reduce_scatter x9 -> x0, waiting for transfers between devices: 541 us -> none  [the longest x1 129 us: on_device(): lax.psum_scatter(value_weight_grad, 'dp', scatter_dimension=0, tiled=True)]
    all_gather x4 -> x0, blocking collectives: 170 us -> none  [the longest x1 45.8 us: on_device(): lax.all_gather(query_weight, 'dp', axis=0, tiled=True)]
    unnamed x17 -> x0, waiting for transfers between devices: 145 us -> none
    psum x6 -> x0, blocking collectives: 127 us -> none  [the longest x1 78.3 us: on_device(): head_sum, hidden_sum = lax.psum((head_grads, hidden_grads), 'dp')]
    all_gather x6 -> x0, waiting for transfers between devices: 123 us -> none  [the longest x1 55.1 us: on_device(): lax.all_gather(down_weight, 'dp', axis=0, tiled=True)]
    ppermute x0 -> x52, waiting for transfers between devices: none -> 102 us  [the longest x39 99.5 us: shift(): return lax.ppermute(values, 'dp', pairs)]
    ppermute x0 -> x52, starting transfers between devices: none -> 52.6 us  [the longest x39 50.7 us: shift(): return lax.ppermute(values, 'dp', pairs)]
    pallas_call x0 -> x8, Pallas kernels: none -> 37 us  [the longest x5 27.4 us: weight_grad(): pl.pallas_call(body, grid=(width // tile,), out_shape=[jax.ShapeDtypeStru...]
  transfers between devices with their start and end apart: 16 -> 52, of which waited for: 13 -> 23; matrix products, arithmetic and copies ran while one was open for 5% -> 46% of each run, Pallas kernels for 0% -> 7%
where the time goes in v1:
time: 455 us; the launch traced here: 448 us
  matrix products  108 us (24%)
  waiting for transfers between devices  102 us (22%)
  other arithmetic  85.4 us (19%)
  local copies, waits for them, and re-layouts  57.6 us (13%)
  starting transfers between devices  52.6 us (12%)
  Pallas kernels  37 us (8%)
    ppermute x39, waiting for transfers between devices, shift(): return lax.ppermute(values, 'dp', pairs)  99.5 us
    ppermute x39, starting transfers between devices, shift(): return lax.ppermute(values, 'dp', pairs)  50.7 us
    dot_general x6, matrix products, matmul(): return jnp.dot(left_side, right_side, preferred_element_type=jnp.float32)  34.6 us
    pallas_call x5, Pallas kernels, weight_grad(): pl.pallas_call(body, grid=(width // tile,), out_shape=[jax.ShapeDtypeStru...  27.4 us
    dot_general x6, matrix products, matmul_transposed(): lax.dot_general(left_side, right_side, (((1,), (1,)), ((), ())), preferre...  20.6 us
    unnamed x142, local copies, waits for them, and re-layouts  13.1 us
    dot_general x2, matrix products, backward_block(): jnp.einsum('qhd,khd->hqk', grad_rows, value_split, preferred_element_type...  10.5 us
    dot_general x2, matrix products, backward_block(): jnp.einsum('hqk,qhd->khd', softmax_out.astype(jnp.bfloat16), grad_rows, p...  10.3 us
  transfers between devices with their start and end apart: 52, of which 23 were waited for; matrix products, arithmetic and copies ran while one was open for 46% of the time, Pallas kernels for 7%

profile of v1, /device:TPU:0, one launch (start us, length us, event | category | flops | bytes accessed | tf_op | source)
XLA Modules:
  0.0 448.0 jit_solution(11688964930806015010)
XLA Ops:
  12.3 5.6 %collective-permute-done.2 = bf16[48,1152]{1,0:T(8,128)(2,1)S(1)} collective-permute-done((bf16[48,1152]{1,0:T(8,128)(2,1)S(1)}, bf16[48,1152]{1,0:T(8,128)(2,1)S(1)}, u32[]{:S(2)}, u32[]{:S(2)}) %collective-permute-start.2) | collective-permute-done | bytes 110624 | tf_op jit(solution)/shard_map/ppermute | solution.py:59
  24.1 5.3 %collective-permute-done.5.from_y = bf16[192,1152]{1,0:T(8,128)(2,1)S(1)} collective-permute-done((bf16[192,1152]{1,0:T(8,128)(2,1)S(1)}, bf16[192,1152]{1,0:T(8,128)(2,1)S(1)}, u32[]{:S(2)}, u32[]{:S(2)}) %collective-permute-start.5) | collective-permute-done | bytes 442400 | tf_op jit(solution)/shard_map/ppermute | solution.py:59
  34.6 6.3 %collective-permute-done.10 = bf16[48,1920]{1,0:T(8,128)(2,1)} collective-permute-done((bf16[48,1920]{1,0:T(8,128)(2,1)S(1)}, bf16[48,1920]{1,0:T(8,128)(2,1)}, u32[]{:S(2)}, u32[]{:S(2)}) %collective-permute-start.10) | collective-permute-done | bytes 184352 | tf_op jit(solution)/shard_map/ppermute | solution.py:59
  54.8 27.2 %while.30 = (s32[]{:T(128)}, f32[2,512,384]{1,2,0:T(8,128)}, f32[2,6,512]{2,1,0:T(8,128)S(1)}, s32[2]{0:T(128)S(1)}, s32[]{:T(128)}, /*index=5*/bf16[1024,384]{0...) while((s32[]{:T(128)}, f32[2,512,384]{1,2,0:T(8,128)}, ...), condition=%wide.region_5.6_spmd.clone.clone, body=%wide.region_2.5_spmd.clone.clone.sunk | while | flops 844102144 | bytes 57657604 | solution.py:335
  91.5 6.0 %collective-permute-done.15.corner_b = bf16[96,1920]{1,0:T(8,128)(2,1)S(1)} collective-permute-done((bf16[96,1920]{1,0:T(8,128)(2,1)}, bf16[96,1920]{1,0:T(8,128)(2,1)S(1)}, u32[]{:S(2)}, u32[]{:S(2)}) %collective-permute-start.15) | collective-permute-done | bytes 368672 | tf_op jit(solution)/shard_map/ppermute | solution.py:59
  133.9 12.7 %collective-permute-done.23.from_y = bf16[192,1536]{1,0:T(8,128)(2,1)} collective-permute-done((bf16[192,1536]{1,0:T(8,128)(2,1)}, bf16[192,1536]{1,0:T(8,128)(2,1)}, u32[]{:S(2)}, u32[]{:S(2)}) %collective-permute-start.23) | collective-permute-done | bytes 589856 | tf_op jit(solution)/shard_map/ppermute | solution.py:59
  153.7 20.2 %fusion.70 = (f32[1024]{0:T(1024)S(1)}, f32[1024]{0:T(1024)S(1)}, f32[1024,1536]{1,0:T(8,128)}, f32[1024,1536]{1,0:T(8,128)}, f32[1024,1536]{1,0:T(8,128)}) fusion(f32[1536]{0:T(1024)S(1)} %get-tuple-element.339, bf16[1024,768]{1,0:T(8,128)(2,1)S(1)} %maximum_select_fusion.1.left, bf16[768,1536]{1,0:T(8,128)(2,1)S(1)} %copy-done.68), kind=kOutput, calls=%fused_computation.213 | convolution fusion | flops 2522871808 | bytes 22820864 | tf_op jit(solution)/shard_map/dot_general | solution.py:221
  185.0 7.7 %multiply_reduce_fusion.1 = (f32[1536]{0:T(1024)S(1)}, f32[1024]{0:T(1024)S(1)}, f32[1024]{0:T(1024)S(1)}, f32[1536]{0:T(1024)S(1)}, f32[1024,1536]{1,0:T(8,128)S(1)}) fusion(f32[1024,1536]{1,0:T(8,128)} %get-tuple-element.394, f32[1024]{0:T(1024)S(1)} %add_rsqrt_fusion.1, f32[1024]{0:T(1024)S(1)} %bitcast.225, f32[1536]{0:T(1024)S(1)} %get-tuple-element.338, ...), kind=kOutput, calls=%fused_computation.39 | convolution fusion | flops 2430069760 | bytes 16549888 | tf_op jit(solution)/shard_map/dot_general | solution.py:221
  194.4 7.7 %convert_reduce_fusion = (f32[1536]{0:T(1024)S(1)}, bf16[1024,1536]{1,0:T(8,128)(2,1)S(1)}, bf16[1024,1536]{1,0:T(8,128)(2,1)}) fusion(f32[1024,1536]{1,0:T(8,128)S(1)} %bitcast.214, f32[1024]{0:T(1024)S(1)} %bitcast.234, f32[1024,1536]{1,0:T(8,128)S(1)} %bitcast.212, f32[1024]{0:T(1024)S(1)} %bitcast.226, f32[1024]{0:T(1024)S(1)} %bitcast.233, ...), kind=kLoop, calls=%fused_computation.40 | loop fusion | flops 42465792 | bytes 31498240 | tf_op jit(solution)/shard_map/reduce_sum | solution.py:358
  202.1 5.5 %fusion.82 = f32[1024,768]{1,0:T(8,128)S(1)} fusion(bf16[1024,1536]{1,0:T(8,128)(2,1)S(1)} %get-tuple-element.391.right, bf16[768,1536]{1,0:T(8,128)(2,1)} %get-tuple-element.149), kind=kOutput, calls=%fused_computation.223 | convolution fusion | flops 2415919104 | bytes 8650752 | tf_op jit(solution)/shard_map/dot_general | solution.py:225
  214.5 7.6 %shard_map.210 = (bf16[384,1536]{1,0:T(8,128)(2,1)}, bf16[384,1536]{1,0:T(8,128)(2,1)}) custom-call(s32[16]{0:T(128)} %stack.215.order_ref, bf16[1024,768]{1,0:T(8,128)(2,1)} %maximum_select_fusion.2.left, bf16[1024,1536]{1,0:T(8,128)(2,1)} %get-tuple-element.401.right), custom_call_target="tpu_custom_call" | custom-call | flops 2415919104 | bytes 7077888 | tf_op jit(solution)/shard_map/pallas_call | solution.py:198
  223.3 7.7 %shard_map.209 = (bf16[384,1536]{1,0:T(8,128)(2,1)}, bf16[384,1536]{1,0:T(8,128)(2,1)}) custom-call(s32[16]{0:T(128)} %stack.214.order_ref, bf16[1024,768]{1,0:T(8,128)(2,1)} %copy-done.27, bf16[1024,1536]{1,0:T(8,128)(2,1)} %copy-done.17), custom_call_target="tpu_custom_call" | custom-call | flops 2415919104 | bytes 7077888 | tf_op jit(solution)/shard_map/pallas_call | solution.py:198
  242.3 8.6 %collective-permute-done.42 = bf16[384,1536]{1,0:T(8,128)(2,1)} collective-permute-done((bf16[384,1536]{1,0:T(8,128)(2,1)}, bf16[384,1536]{1,0:T(8,128)(2,1)}, u32[]{:S(2)}, u32[]{:S(2)}) %collective-permute-start.42) | collective-permute-done | bytes 1179680 | tf_op jit(solution)/shard_map/ppermute | solution.py:59
  254.5 5.7 %collective-permute-done.40 = bf16[384,1536]{1,0:T(8,128)(2,1)S(1)} collective-permute-done((bf16[384,1536]{1,0:T(8,128)(2,1)}, bf16[384,1536]{1,0:T(8,128)(2,1)S(1)}, u32[]{:S(2)}, u32[]{:S(2)}) %collective-permute-start.40) | collective-permute-done | bytes 1179680 | tf_op jit(solution)/shard_map/ppermute | solution.py:59
  273.5 61.1 %while.31 = (s32[]{:T(128)}, f32[1024,6,64]{0,2,1:T(8,128)}, f32[1024,6,64]{0,2,1:T(8,128)}, bf16[2,512,384]{1,2,0:T(8,128)(2,1)}, s32[2]{0:T(128)S(1)}, /*index...) while((s32[]{:T(128)}, f32[1024,6,64]{0,2,1:T(8,128)}, ...), condition=%wide.region_20.21_spmd.clone.clone, body=%wide.region_18.20_spmd.clone.clone.sunk | while | flops 2063858176 | bytes 154364368 | solution.py:411
  283.9 5.3 %multiply_reduce_fusion.15 = (f32[6,512]{1,0:T(8,128)S(1)}, f32[6,512,1024]{2,1,0:T(8,128)S(1)}) fusion(f32[6,512,1024]{2,1,0:T(8,128)S(1)} %fusion.157, f32[6,512]{1,0:T(8,128)S(1)} %dynamic-slice_bitcast_fusion.2, pred[512,1024]{1,0:T(8,128)(4,1)S(1)} %fusion.158, bf16[512,6,64]{0,2,1:T(8,128)(2,1)S(1)} %bitcast.199, ...), kind=kOutput, calls=%fused_computation.18.clone.1 | convolution fusion | flops 418378752 | bytes 26894336 | tf_op jit(solution)/shard_map/while/body/eval_jaxpr/qhd,khd->hqk/dot_general | solution.py:387
  308.4 5.7 %bitcast_add_fusion.11 = f32[1024,6,64]{0,2,1:T(8,128)} fusion(f32[1024,6,64]{0,2,1:T(8,128)} %get-tuple-element.613, bf16[512,6,64]{0,2,1:T(8,128)(2,1)S(1)} %bitcast.198, f32[6,512,1024]{2,1,0:T(8,128)S(1)} %fusion.157, f32[6,512]{1,0:T(8,128)S(1)} %dynamic-slice_bitcast_fusion.2, pred[512,1024]{1,0:T(8,128)(4,1)S(1)} %fusion.158, pred[]{:T(512)S(6)} %compare.15), kind=kOutput, calls=%fused_computation.25.clone.1 | convolution fusion | flops 416022528 | bytes 16658433 | tf_op jit(solution)/shard_map/while/body/eval_jaxpr/hqk,qhd->khd/dot_general | solution.py:402
  314.1 5.2 %multiply_reduce_fusion.15 = (f32[6,512]{1,0:T(8,128)S(1)}, f32[6,512,1024]{2,1,0:T(8,128)S(1)}) fusion(f32[6,512,1024]{2,1,0:T(8,128)S(1)} %fusion.157, f32[6,512]{1,0:T(8,128)S(1)} %dynamic-slice_bitcast_fusion.2, pred[512,1024]{1,0:T(8,128)(4,1)S(1)} %fusion.158, bf16[512,6,64]{0,2,1:T(8,128)(2,1)S(1)} %bitcast.199, ...), kind=kOutput, calls=%fused_computation.18.clone.1 | convolution fusion | flops 418378752 | bytes 26894336 | tf_op jit(solution)/shard_map/while/body/eval_jaxpr/qhd,khd->hqk/dot_general | solution.py:387
  319.4 5.1 %multiply_convert_fusion.3 = bf16[6,512,1024]{2,1,0:T(8,128)(2,1)} fusion(f32[6,512,1024]{2,1,0:T(8,128)S(1)} %get-tuple-element.558, f32[6,512,1024]{2,1,0:T(8,128)S(1)} %fusion.157, f32[6,512]{1,0:T(8,128)S(1)} %get-tuple-element.559, f32[6,512]{1,0:T(8,128)S(1)} %dynamic-slice_bitcast_fusion.2, pred[512,1024]{1,0:T(8,128)(4,1)S(1)} %fusion.158), kind=kLoop, calls=%fused_computation.17.clone.1 | loop fusion | flops 18874368 | bytes 32006144 | tf_op jit(solution)/shard_map/while/body/eval_jaxpr/convert_element_type | solution.py:392
  359.0 5.1 %shard_map.206 = (bf16[384,768]{1,0:T(8,128)(2,1)}, bf16[384,768]{1,0:T(8,128)(2,1)}) custom-call(s32[16]{0:T(128)} %stack.214.order_ref, bf16[1024,768]{1,0:T(8,128)(2,1)} %copy-done.14, bf16[1024,768]{1,0:T(8,128)(2,1)} %pad_maximum_fusion.1.right), custom_call_target="tpu_custom_call" | custom-call | flops 1207959552 | bytes 4325376 | tf_op jit(solution)/shard_map/pallas_call | solution.py:198
  378.7 5.5 %collective-permute-done.44 = bf16[48,3072]{1,0:T(8,128)(2,1)S(1)} collective-permute-done((bf16[48,3072]{1,0:T(8,128)(2,1)S(1)}, bf16[48,3072]{1,0:T(8,128)(2,1)S(1)}, u32[]{:S(2)}, u32[]{:S(2)}) %collective-permute-start.44) | collective-permute-done | bytes 294944 | tf_op jit(solution)/shard_map/ppermute | solution.py:59
  384.2 5.2 %collective-permute-done.46 = bf16[48,3072]{1,0:T(8,128)(2,1)S(1)} collective-permute-done((bf16[48,3072]{1,0:T(8,128)(2,1)S(1)}, bf16[48,3072]{1,0:T(8,128)(2,1)S(1)}, u32[]{:S(2)}, u32[]{:S(2)}) %collective-permute-start.46) | collective-permute-done | bytes 294944 | tf_op jit(solution)/shard_map/ppermute | solution.py:59
  389.5 12.6 %collective-permute-done.45 = bf16[48,3072]{1,0:T(8,128)(2,1)S(1)} collective-permute-done((bf16[48,3072]{1,0:T(8,128)(2,1)S(1)}, bf16[48,3072]{1,0:T(8,128)(2,1)S(1)}, u32[]{:S(2)}, u32[]{:S(2)}) %collective-permute-start.45) | collective-permute-done | bytes 294944 | tf_op jit(solution)/shard_map/ppermute | solution.py:59
  440.4 6.6 %collective-permute-done.38 = bf16[48,1536]{1,0:T(8,128)(2,1)S(1)} collective-permute-done((bf16[48,1536]{1,0:T(8,128)(2,1)S(1)}, bf16[48,1536]{1,0:T(8,128)(2,1)S(1)}, u32[]{:S(2)}, u32[]{:S(2)}) %collective-permute-start.38) | collective-permute-done | bytes 147488 | tf_op jit(solution)/shard_map/ppermute | solution.py:59
  (454 shorter events, 279.6 us)
Async XLA Ops:
  19.9 28.3 %collective-permute-start = (bf16[512,768]{1,0:T(8,128)(2,1)S(1)}, bf16[512,768]{1,0:T(8,128)(2,1)S(1)}, u32[]{:S(2)}, u32[]{:S(2)}) collective-permute-start(bf16[512,768]{1,0:T(8,128)(2,1)S(1)} %fusion.33), channel_id=1, source_target_pairs={{0,1},{1,0},{2,3},{3,2},{4,5},{5,4},{6,7},{7,6},{8,9},{9,8},{10,11... | collective-permute-start | bytes 2359304 | tf_op jit(solution)/shard_map/ppermute | solution.py:18
  23.3 17.6 %collective-permute-start.10 = (bf16[48,1920]{1,0:T(8,128)(2,1)S(1)}, bf16[48,1920]{1,0:T(8,128)(2,1)}, u32[]{:S(2)}, u32[]{:S(2)}) collective-permute-start(bf16[48,1920]{1,0:T(8,128)(2,1)S(1)} %constant_dynamic-update-slice_fusion.3), channel_id=1, source_target_pairs={{0,16},{2,18},{4,20},{6,22},{8,24},{10,26},{12,28},{14,30},{16,0},... | collective-permute-start | bytes 552968 | tf_op jit(solution)/shard_map/ppermute | solution.py:59
  42.9 42.0 %collective-permute-start.13 = (bf16[192,1920]{1,0:T(8,128)(2,1)}, bf16[192,1920]{1,0:T(8,128)(2,1)}, u32[]{:S(2)}, u32[]{:S(2)}) collective-permute-start(bf16[192,1920]{1,0:T(8,128)(2,1)} %pad_maximum_fusion.3.own), channel_id=1, source_target_pairs={{0,4},{2,6},{4,0},{6,2},{8,12},{10,14},{12,8},{14,10},{16,20},{18,... | collective-permute-start | bytes 2211848 | tf_op jit(solution)/shard_map/ppermute | solution.py:59
  43.4 44.8 %collective-permute-start.12 = (bf16[192,1920]{1,0:T(8,128)(2,1)}, bf16[192,1920]{1,0:T(8,128)(2,1)}, u32[]{:S(2)}, u32[]{:S(2)}) collective-permute-start(bf16[192,1920]{1,0:T(8,128)(2,1)} %pad_maximum_fusion.3.own), channel_id=1, source_target_pairs={{0,2},{2,0},{4,6},{6,4},{8,10},{10,8},{12,14},{14,12},{16,18},{18,... | collective-permute-start | bytes 2211848 | tf_op jit(solution)/shard_map/ppermute | solution.py:59
  112.2 17.7 %collective-permute-start.21 = (bf16[48,1536]{1,0:T(8,128)(2,1)S(1)}, bf16[48,1536]{1,0:T(8,128)(2,1)S(1)}, u32[]{:S(2)}, u32[]{:S(2)}) collective-permute-start(bf16[48,1536]{1,0:T(8,128)(2,1)S(1)} %copy-done.55), channel_id=1, source_target_pairs={{0,24},{2,26},{4,28},{6,30},{8,0},{10,2},{12,4},{14,6},{16,8},{18,... | collective-permute-start | bytes 442376 | tf_op jit(solution)/shard_map/ppermute | solution.py:59
  129.9 21.5 %collective-permute-start.17 = (bf16[512,768]{1,0:T(8,128)(2,1)}, bf16[512,768]{1,0:T(8,128)(2,1)}, u32[]{:S(2)}, u32[]{:S(2)}) collective-permute-start(bf16[512,768]{1,0:T(8,128)(2,1)} %add_convert_fusion.3), channel_id=1, source_target_pairs={{0,1},{1,0},{2,3},{3,2},{4,5},{5,4},{6,7},{7,6},{8,9},{9,8},{10,11... | collective-permute-start | bytes 2359304 | tf_op jit(solution)/shard_map/ppermute | solution.py:18
  130.5 16.0 %collective-permute-start.23 = (bf16[192,1536]{1,0:T(8,128)(2,1)}, bf16[192,1536]{1,0:T(8,128)(2,1)}, u32[]{:S(2)}, u32[]{:S(2)}) collective-permute-start(bf16[192,1536]{1,0:T(8,128)(2,1)} %constant_dynamic-update-slice_fusion.5.own), channel_id=1, source_target_pairs={{0,4},{2,6},{4,0},{6,2},{8,12},{10,14},{12,8},{14,10},{16,20},{18,... | collective-permute-start | bytes 1769480 | tf_op jit(solution)/shard_map/ppermute | solution.py:59
  132.1 16.1 %collective-permute-start.22 = (bf16[192,1536]{1,0:T(8,128)(2,1)}, bf16[192,1536]{1,0:T(8,128)(2,1)}, u32[]{:S(2)}, u32[]{:S(2)}) collective-permute-start(bf16[192,1536]{1,0:T(8,128)(2,1)} %constant_dynamic-update-slice_fusion.5.own), channel_id=1, source_target_pairs={{0,2},{2,0},{4,6},{6,4},{8,10},{10,8},{12,14},{14,12},{16,18},{18,... | collective-permute-start | bytes 1769480 | tf_op jit(solution)/shard_map/ppermute | solution.py:59
  132.6 41.4 %collective-permute-start.27 = (bf16[512,768]{1,0:T(8,128)(2,1)}, bf16[512,768]{1,0:T(8,128)(2,1)}, u32[]{:S(2)}, u32[]{:S(2)}) collective-permute-start(bf16[512,768]{1,0:T(8,128)(2,1)} %param.17), channel_id=1, source_target_pairs={{0,1},{1,0},{2,3},{3,2},{4,5},{5,4},{6,7},{7,6},{8,9},{9,8},{10,11... | collective-permute-start | bytes 2359304 | tf_op jit(solution)/shard_map/ppermute | solution.py:18
  147.6 32.8 %collective-permute-start.25 = (bf16[96,1536]{1,0:T(8,128)(2,1)S(1)}, bf16[96,1536]{1,0:T(8,128)(2,1)S(1)}, u32[]{:S(2)}, u32[]{:S(2)}) collective-permute-start(bf16[96,1536]{1,0:T(8,128)(2,1)S(1)} %slice.253), channel_id=1, source_target_pairs={{0,2},{2,0},{4,6},{6,4},{8,10},{10,8},{12,14},{14,12},{16,18},{18,... | collective-permute-start | bytes 884744 | tf_op jit(solution)/shard_map/ppermute | solution.py:59
  149.9 30.5 %collective-permute-start.24 = (bf16[96,1536]{1,0:T(8,128)(2,1)}, bf16[96,1536]{1,0:T(8,128)(2,1)S(1)}, u32[]{:S(2)}, u32[]{:S(2)}) collective-permute-start(bf16[96,1536]{1,0:T(8,128)(2,1)} %slice.252), channel_id=1, source_target_pairs={{0,4},{2,6},{4,0},{6,2},{8,12},{10,14},{12,8},{14,10},{16,20},{18,... | collective-permute-start | bytes 884744 | tf_op jit(solution)/shard_map/ppermute | solution.py:59
  211.3 21.2 %collective-permute-start.29 = (bf16[512,768]{1,0:T(8,128)(2,1)}, bf16[512,768]{1,0:T(8,128)(2,1)}, u32[]{:S(2)}, u32[]{:S(2)}) collective-permute-start(bf16[512,768]{1,0:T(8,128)(2,1)} %fusion.49), channel_id=1, source_target_pairs={{0,1},{1,0},{2,3},{3,2},{4,5},{5,4},{6,7},{7,6},{8,9},{9,8},{10,11... | collective-permute-start | bytes 2359304 | tf_op jit(solution)/shard_map/ppermute | solution.py:18
  214.0 22.7 %collective-permute-start.26 = (bf16[512,768]{1,0:T(8,128)(2,1)}, bf16[512,768]{1,0:T(8,128)(2,1)}, u32[]{:S(2)}, u32[]{:S(2)}) collective-permute-start(bf16[512,768]{1,0:T(8,128)(2,1)} %fusion.48), channel_id=1, source_target_pairs={{0,1},{1,0},{2,3},{3,2},{4,5},{5,4},{6,7},{7,6},{8,9},{9,8},{10,11... | collective-permute-start | bytes 2359304 | tf_op jit(solution)/shard_map/ppermute | solution.py:18
  222.7 28.2 %collective-permute-start.42 = (bf16[384,1536]{1,0:T(8,128)(2,1)}, bf16[384,1536]{1,0:T(8,128)(2,1)}, u32[]{:S(2)}, u32[]{:S(2)}) collective-permute-start(bf16[384,1536]{1,0:T(8,128)(2,1)} %get-tuple-element.163), channel_id=1, source_target_pairs={{0,4},{2,6},{4,0},{6,2},{8,12},{10,14},{12,8},{14,10},{16,20},{18,... | collective-permute-start | bytes 3538952 | tf_op jit(solution)/shard_map/ppermute | solution.py:59
  231.0 29.1 %collective-permute-start.40 = (bf16[384,1536]{1,0:T(8,128)(2,1)}, bf16[384,1536]{1,0:T(8,128)(2,1)S(1)}, u32[]{:S(2)}, u32[]{:S(2)}) collective-permute-start(bf16[384,1536]{1,0:T(8,128)(2,1)} %get-tuple-element.161), channel_id=1, source_target_pairs={{0,2},{2,0},{4,6},{6,4},{8,10},{10,8},{12,14},{14,12},{16,18},{18,... | collective-permute-start | bytes 3538952 | tf_op jit(solution)/shard_map/ppermute | solution.py:59
  242.3 20.3 %collective-permute-start.30 = (bf16[512,768]{1,0:T(8,128)(2,1)S(1)}, bf16[512,768]{1,0:T(8,128)(2,1)S(1)}, u32[]{:S(2)}, u32[]{:S(2)}) collective-permute-start(bf16[512,768]{1,0:T(8,128)(2,1)S(1)} %get-tuple-element.386), channel_id=1, source_target_pairs={{0,1},{1,0},{2,3},{3,2},{4,5},{5,4},{6,7},{7,6},{8,9},{9,8},{10,11... | collective-permute-start | bytes 2359304 | tf_op jit(solution)/shard_map/ppermute | solution.py:18
  253.0 116.0 %collective-permute-start.43 = (bf16[192,1536]{1,0:T(8,128)(2,1)}, bf16[192,1536]{1,0:T(8,128)(2,1)}, u32[]{:S(2)}, u32[]{:S(2)}) collective-permute-start(bf16[192,1536]{1,0:T(8,128)(2,1)} %add_convert_fusion.7), channel_id=1, source_target_pairs={{0,2},{2,0},{4,6},{6,4},{8,10},{10,8},{12,14},{14,12},{16,18},{18,... | collective-permute-start | bytes 1769480 | tf_op jit(solution)/shard_map/ppermute | solution.py:59
  261.1 109.6 %collective-permute-start.41 = (bf16[192,1536]{1,0:T(8,128)(2,1)}, bf16[192,1536]{1,0:T(8,128)(2,1)}, u32[]{:S(2)}, u32[]{:S(2)}) collective-permute-start(bf16[192,1536]{1,0:T(8,128)(2,1)} %add_convert_fusion.8), channel_id=1, source_target_pairs={{0,4},{2,6},{4,0},{6,2},{8,12},{10,14},{12,8},{14,10},{16,20},{18,... | collective-permute-start | bytes 1769480 | tf_op jit(solution)/shard_map/ppermute | solution.py:59
  348.3 54.8 %collective-permute-start.35 = (bf16[384,768]{1,0:T(8,128)(2,1)}, bf16[384,768]{1,0:T(8,128)(2,1)}, u32[]{:S(2)}, u32[]{:S(2)}) collective-permute-start(bf16[384,768]{1,0:T(8,128)(2,1)} %pad_maximum_fusion.4), channel_id=1, source_target_pairs={{0,4},{2,6},{4,0},{6,2},{8,12},{10,14},{12,8},{14,10},{16,20},{18,... | collective-permute-start | bytes 1769480 | tf_op jit(solution)/shard_map/ppermute | solution.py:59
  364.1 41.3 %collective-permute-start.33 = (bf16[384,768]{1,0:T(8,128)(2,1)}, bf16[384,768]{1,0:T(8,128)(2,1)S(1)}, u32[]{:S(2)}, u32[]{:S(2)}) collective-permute-start(bf16[384,768]{1,0:T(8,128)(2,1)} %get-tuple-element.155), channel_id=1, source_target_pairs={{0,2},{2,0},{4,6},{6,4},{8,10},{10,8},{12,14},{14,12},{16,18},{18,... | collective-permute-start | bytes 1769480 | tf_op jit(solution)/shard_map/ppermute | solution.py:59
  376.3 25.8 %collective-permute-start.45 = (bf16[48,3072]{1,0:T(8,128)(2,1)S(1)}, bf16[48,3072]{1,0:T(8,128)(2,1)S(1)}, u32[]{:S(2)}, u32[]{:S(2)}) collective-permute-start(bf16[48,3072]{1,0:T(8,128)(2,1)S(1)} %get-tuple-element.406), channel_id=1, source_target_pairs={{0,16},{2,18},{4,20},{6,22},{8,24},{10,26},{12,28},{14,30},{16,0},... | collective-permute-start | bytes 884744 | tf_op jit(solution)/shard_map/ppermute | solution.py:59
  384.2 23.7 %collective-permute-start.32 = (bf16[512,768]{1,0:T(8,128)(2,1)S(1)}, bf16[512,768]{1,0:T(8,128)(2,1)S(1)}, u32[]{:S(2)}, u32[]{:S(2)}) collective-permute-start(bf16[512,768]{1,0:T(8,128)(2,1)S(1)} %fusion.50), channel_id=1, source_target_pairs={{0,1},{1,0},{2,3},{3,2},{4,5},{5,4},{6,7},{7,6},{8,9},{9,8},{10,11... | collective-permute-start | bytes 2359304 | tf_op jit(solution)/shard_map/ppermute | solution.py:18
  404.9 17.8 %collective-permute-start.36 = (bf16[192,768]{1,0:T(8,128)(2,1)}, bf16[192,768]{1,0:T(8,128)(2,1)}, u32[]{:S(2)}, u32[]{:S(2)}) collective-permute-start(bf16[192,768]{1,0:T(8,128)(2,1)} %add_convert_fusion.10), channel_id=1, source_target_pairs={{0,2},{2,0},{4,6},{6,4},{8,10},{10,8},{12,14},{14,12},{16,18},{18,... | collective-permute-start | bytes 884744 | tf_op jit(solution)/shard_map/ppermute | solution.py:59
  406.4 17.4 %collective-permute-start.34 = (bf16[192,768]{1,0:T(8,128)(2,1)}, bf16[192,768]{1,0:T(8,128)(2,1)}, u32[]{:S(2)}, u32[]{:S(2)}) collective-permute-start(bf16[192,768]{1,0:T(8,128)(2,1)} %add_convert_fusion.11), channel_id=1, source_target_pairs={{0,4},{2,6},{4,0},{6,2},{8,12},{10,14},{12,8},{14,10},{16,20},{18,... | collective-permute-start | bytes 884744 | tf_op jit(solution)/shard_map/ppermute | solution.py:59
  (112 other events, 829.8 us)

commit v2 on v1

v2 whole, which is shorter than its diff:
```python
import jax
import jax.numpy as jnp
from jax import lax
from jax.experimental import pallas as pl
from jax.experimental.pallas import tpu as pltpu
from jax.sharding import PartitionSpec as P

HEAD_DIM = 64
PAIR = 2 * HEAD_DIM
LANES = 128
TILES = 4
SCALE = 0.125
LOG2E = 1.4426950408889634
WEIGHT = 4

epsilon = 1e-05
masked = -1e30

f32 = jnp.float32
bf16 = jnp.bfloat16
TRANSPOSED = (((1,), (1,)), ((), ()))
SMEM = pl.BlockSpec(memory_space=pltpu.SMEM)


def flip_partner(values):
    return lax.ppermute(values, "tensor", [(0, 1), (1, 0)])


def normal_of(values):
    center = jnp.mean(values, axis=-1, keepdims=True)
    spread = jnp.mean(values * values, axis=-1, keepdims=True) - center * center
    inverse = lax.rsqrt(spread + epsilon)
    return (values - center) * inverse, inverse


def normal_back(scaled, normal, inverse):
    return inverse * (
        scaled
        - jnp.mean(scaled, axis=-1, keepdims=True)
        - normal * jnp.mean(scaled * normal, axis=-1, keepdims=True)
    )


def widen(values):
    return values.astype(f32)


def after(values, *earlier):
    return lax.optimization_barrier((values, earlier))[0]


class Ring:
    def __init__(self, size):
        self.size = size
        rest, stride = size // 4, 4
        self.lines = []
        while rest > 1:
            factor = 4 if rest % 4 == 0 else 2 if rest % 2 == 0 else rest
            self.lines.append((factor, stride))
            rest, stride = rest // factor, stride * factor
        self.line_count = size // 4

    def shift(self, values, factor, stride, step):
        pairs = []
        for place in range(self.size):
            digit = place // stride % factor
            pairs.append((place, place + ((digit + step) % factor - digit) * stride))
        return lax.ppermute(values, "dp", pairs)

    def flip(self, values, stride):
        return self.shift(values, 2, stride, 1)

    def line_places(self, sign):
        own = lax.axis_index("dp")
        places = [jnp.int32(0)]
        for factor, stride in self.lines:
            digit = own // stride % factor
            places = [
                base + (digit + sign * step) % factor * stride
                for base in places
                for step in range(factor)
            ]
        return places

    def gather_order(self):
        own = lax.axis_index("dp")
        places = self.line_places_gather()
        return jnp.stack([base + (own % 4 ^ bits) for bits in (0, 1, 2, 3) for base in places])

    def line_places_gather(self):
        own = lax.axis_index("dp")
        places = [jnp.int32(0)]
        for factor, stride in self.lines:
            digit = own // stride % factor
            places = [
                base + (digit + factor - step) % factor * stride
                for step in range(factor)
                for base in places
            ]
        return places

    def along_lines(self, values):
        block = values
        for factor, stride in self.lines:
            block = jnp.concatenate(
                [block] + [self.shift(block, factor, stride, step) for step in range(1, factor)], 0
            )
        return block

    def to_sides(self, block):
        return self.flip(block, 1), self.flip(block, 2)

    def to_corner(self, from_x, from_y):
        half = from_x.shape[0] // 2
        return self.flip(from_x[:half], 2), self.flip(from_y[half:], 1)

    def scatter_order(self, first_bit):
        own = lax.axis_index("dp")
        other_bit = 3 - first_bit
        places = self.line_places(1)
        return jnp.stack(
            [
                base + (own % 4 ^ (cross + side))
                for cross in (0, first_bit)
                for side in (0, other_bit)
                for base in places
            ]
        )

    def sum_first(self, keep, got):
        half = keep.shape[0] // 2
        own = widen(keep[:half]) + widen(got[:half])
        return own, (widen(keep[half:]) + widen(got[half:])).astype(bf16)

    def sum_lines(self, total):
        for factor, stride in self.lines:
            rows = total.shape[0] // factor
            rounded = total.astype(bf16)
            running = total[:rows]
            for step in range(1, factor):
                got = self.shift(rounded[step * rows : (step + 1) * rows], factor, stride, step)
                running = running + widen(got)
            total = running
        return total

    def all_sum(self, values):
        stride = 1
        while stride < self.size:
            values = values + self.flip(values, stride)
            stride *= 2
        return values


def whole(shape):
    return pl.BlockSpec(shape, lambda i: (0,) * len(shape))


def rows_of(array, tiles=TILES):
    return pl.BlockSpec((array.shape[0] // tiles, array.shape[1]), lambda i: (i, 0))


def shape_of(shape, dtype):
    return jax.ShapeDtypeStruct(shape, dtype)


def cost(flops, moved, exponentials=0):
    return pl.CostEstimate(flops=WEIGHT * flops, bytes_accessed=moved, transcendentals=exponentials)


PARAMS = pltpu.CompilerParams(vmem_limit_bytes=60 * 2**20)


def place_rows(order_ref, pieces, outs, count):
    own, from_x, from_y, corner_a, corner_b = pieces
    rows = own.shape[0]
    shard = rows // (count // 4)
    for block in range(count):
        kind, inner = divmod(block, count // 4)
        start = inner * shard
        ref = (own, from_x, from_y, corner_a)[kind]
        if kind == 3 and start >= rows // 2:
            ref, start = corner_b, start - rows // 2
        place = pl.multiple_of(order_ref[block] * shard, 16)
        left = 0
        for out in outs:
            width = out.shape[1]
            out[pl.ds(place, shard), :] = ref[start : start + shard, left : left + width]
            left += width


def split_three(value):
    high = value.astype(bf16)
    rest = value - widen(high)
    middle = rest.astype(bf16)
    return high, middle, (rest - widen(middle)).astype(bf16)


def two_parts(row):
    high = row.astype(bf16)
    return high, (row - widen(high)).astype(bf16)


def pack_stats(center, spread):
    lane = lax.broadcasted_iota(jnp.int32, (1, LANES), 1)
    packed = jnp.zeros((center.shape[0], LANES), f32)
    for at, part in enumerate(split_three(center) + split_three(spread)):
        packed = jnp.where(lane == at, widen(part), packed)
    return packed.astype(bf16)


def unpack_stats(packed):
    lane = lax.broadcasted_iota(jnp.int32, (1, LANES), 1)
    values = widen(packed)
    center = jnp.sum(jnp.where(lane < 3, values, 0.0), axis=-1, keepdims=True)
    spread = jnp.sum(jnp.where((lane >= 3) & (lane < 6), values, 0.0), axis=-1, keepdims=True)
    return center, spread


def joined_product(one, two, side_one, side_two, features):
    center_one, spread_one = unpack_stats(one[:, features:])
    center_two, spread_two = unpack_stats(two[:, features:])
    center = 0.5 * (center_one + center_two)
    apart = 0.5 * (center_one - center_two)
    inverse = lax.rsqrt(0.5 * (spread_one + spread_two) + apart * apart + epsilon)
    product = inverse * (
        widen(one[:, :features])
        + widen(two[:, :features])
        + apart * (side_one[0:1, :] - side_two[0:1, :])
    )
    return center, inverse, product


def centered_product(values, gain, weight):
    center = jnp.mean(values, axis=-1, keepdims=True)
    away = values - center
    spread = jnp.mean(away * away, axis=-1, keepdims=True)
    product = lax.dot_general(
        (away * gain).astype(bf16), weight, TRANSPOSED, preferred_element_type=f32
    )
    return product.astype(bf16), pack_stats(center, spread)


def side_rows(gain, offset, weight):
    gain_high, gain_low = two_parts(gain)
    offset_high, offset_low = two_parts(offset)
    filler = jnp.zeros((4, gain.shape[1]), bf16)
    stacked = jnp.concatenate([gain_high, gain_low, offset_high, offset_low, filler], 0)
    rows = lax.dot_general(stacked, weight, TRANSPOSED, preferred_element_type=f32)
    return jnp.concatenate(
        [rows[0:1] + rows[1:2], rows[2:3] + rows[3:4], jnp.zeros((6, rows.shape[1]), f32)], 0
    )


def accumulate(ref, row, values):
    total = jnp.sum(values, axis=0, keepdims=True)
    first = pl.program_id(0) == 0
    ref[row : row + 1, :] = jnp.where(first, total, ref[row : row + 1, :] + total)


def prepare(core, tokens, tokens_other, cotangent, cotangent_other, model_vectors):
    rows, features = tokens.shape
    share = TILES // 2
    tile = rows // share

    def body(
        core_ref, x_own, x_other, g_own, g_other, model, inputs, grads, normal, turned, g_turned, sums
    ):
        here = pl.program_id(0) // share == core_ref[0]
        x = jnp.where(here, x_own[...], x_other[...])
        g = jnp.where(here, g_own[...], g_other[...])
        inputs[...] = x
        grads[...] = g
        n, _ = normal_of(widen(x))
        a = (n * model[0:1, :] + model[1:2, :]).astype(bf16)
        normal[...] = a
        turned[...] = a.T
        g_turned[...] = g.T
        accumulate(sums, 0, widen(g))

    own = pl.BlockSpec(
        (tile, features), lambda i, core: (jnp.clip(i - core[0] * share, 0, share - 1), 0)
    )
    other = pl.BlockSpec(
        (tile, features), lambda i, core: (jnp.clip(i - (1 - core[0]) * share, 0, share - 1), 0)
    )
    straight = pl.BlockSpec((tile, features), lambda i, core: (i, 0))
    across = pl.BlockSpec((features, tile), lambda i, core: (0, i))
    return pl.pallas_call(
        body,
        grid_spec=pltpu.PrefetchScalarGridSpec(
            num_scalar_prefetch=1,
            grid=(TILES,),
            in_specs=[own, other, own, other]
            + [pl.BlockSpec(model_vectors.shape, lambda i, core: (0, 0))],
            out_specs=[straight] * 3
            + [across] * 2
            + [pl.BlockSpec((8, features), lambda i, core: (0, 0))],
        ),
        out_shape=[shape_of((2 * rows, features), bf16)] * 3
        + [shape_of((features, 2 * rows), bf16)] * 2
        + [shape_of((8, features), f32)],
        compiler_params=PARAMS,
        cost_estimate=cost(20 * rows * features, 28 * rows * features),
        name="prepare",
    )(core, tokens, tokens_other, cotangent, cotangent_other, model_vectors)


def join(*parts):
    rows, width = parts[0].shape[0], sum(part.shape[1] for part in parts)

    def body(*refs):
        left = 0
        for ref in refs[:-1]:
            refs[-1][:, left : left + ref.shape[1]] = ref[...]
            left += ref.shape[1]

    return pl.pallas_call(
        body,
        out_shape=shape_of((rows, width), parts[0].dtype),
        in_specs=[pl.BlockSpec(memory_space=pltpu.VMEM)] * len(parts),
        out_specs=pl.BlockSpec(memory_space=pltpu.VMEM),
        name="join",
    )(*parts)


def project(order, pieces, attend_in, bias):
    length, features = attend_in.shape
    width = bias.shape[1]
    third = width // 3
    count = order.shape[0]

    def body(order_ref, *refs):
        pieces_in, (rows, bias_row, weight, *outs) = refs[:5], refs[5:]

        @pl.when(pl.program_id(0) == 0)
        def _():
            place_rows(order_ref, pieces_in, (weight,), count)

        states = jnp.dot(rows[...], weight[...], preferred_element_type=f32) + bias_row[...]
        for at, out in enumerate(outs):
            out[...] = states[:, at * third : (at + 1) * third].astype(bf16)

    return pl.pallas_call(
        body,
        grid=(TILES,),
        out_shape=[shape_of((features, width), bf16)] + [shape_of((length, third), bf16)] * 3,
        in_specs=[SMEM]
        + [whole(piece.shape) for piece in pieces]
        + [rows_of(attend_in), whole(bias.shape)],
        out_specs=[whole((features, width))]
        + [pl.BlockSpec((length // TILES, third), lambda i: (i, 0))] * 3,
        compiler_params=PARAMS,
        cost_estimate=cost(
            2 * length * features * width, 4 * features * width + 2 * length * (features + width)
        ),
        name="project",
    )(order, *pieces, attend_in, bias)


def attend_forward(prefix, queries, keys, values):
    length, width = queries.shape
    pairs = width // PAIR
    tile = length // 2

    def body(prefix_ref, query_ref, key_ref, value_ref, out_ref, log_ref, turned):
        turned[...] = value_ref[...].T
        first_half = lax.broadcasted_iota(jnp.int32, (1, PAIR), 1) < HEAD_DIM
        key_rows = key_ref[...]
        row_at = lax.broadcasted_iota(jnp.int32, (length, 1), 0)
        for start in range(0, length, tile):
            columns = slice(start, start + tile)
            places = lax.broadcasted_iota(jnp.int32, (1, tile), 1) + (start + 1)
            limit = jnp.maximum(places, prefix_ref[0])
            query_rows = query_ref[columns, :]
            parts = []
            for head in (0, 1):
                mine = jnp.where(
                    first_half == (head == 0), query_rows, jnp.zeros_like(query_rows)
                )
                scores = lax.dot_general(key_rows, mine, TRANSPOSED, preferred_element_type=f32)
                scores = jnp.where(row_at < limit, scores, masked)
                top = jnp.max(scores, axis=0, keepdims=True)
                raised = jnp.exp2((scores - top) * (SCALE * LOG2E))
                total = jnp.sum(raised, axis=0, keepdims=True)
                mixed = jnp.dot(
                    turned[head * HEAD_DIM : (head + 1) * HEAD_DIM, :],
                    raised.astype(bf16),
                    preferred_element_type=f32,
                )
                parts.append(mixed / total)
                log_ref[0, head : head + 1, columns] = top * (SCALE * LOG2E) + jnp.log2(total)
            out_ref[columns, :] = jnp.concatenate(parts, 0).T

    block = pl.BlockSpec((length, PAIR), lambda i: (0, i))
    return pl.pallas_call(
        body,
        grid=(pairs,),
        out_shape=[shape_of((length, width), f32), shape_of((pairs, 8, length), f32)],
        in_specs=[SMEM, block, block, block],
        out_specs=[block, pl.BlockSpec((1, 8, length), lambda i: (i, 0, 0))],
        scratch_shapes=[pltpu.VMEM((PAIR, length), bf16)],
        compiler_params=PARAMS,
        cost_estimate=cost(
            16 * length * length * width, 10 * length * width, 2 * pairs * length * length
        ),
        name="attend_forward",
    )(prefix, queries, keys, values)


def attend_backward(prefix, queries, keys, values, attended, grads, logs):
    length, width = queries.shape
    pairs = width // PAIR
    tile = length // 4

    def body(
        prefix_ref,
        query_ref,
        key_ref,
        value_ref,
        attended_ref,
        grad_ref,
        log_ref,
        query_out,
        key_out,
        value_out,
        turned,
        key_total,
        value_total,
    ):
        turned[...] = key_ref[...].T
        first_half = lax.broadcasted_iota(jnp.int32, (1, PAIR), 1) < HEAD_DIM
        key_rows, value_rows = key_ref[...], value_ref[...]
        row_at = lax.broadcasted_iota(jnp.int32, (length, 1), 0)
        for start in range(0, length, tile):
            columns = slice(start, start + tile)
            places = lax.broadcasted_iota(jnp.int32, (1, tile), 1) + (start + 1)
            limit = jnp.maximum(places, prefix_ref[0])
            query_rows, grad_rows = query_ref[columns, :], grad_ref[columns, :]
            crossed = (attended_ref[columns, :] * widen(grad_rows)).T
            parts = []
            key_part = value_part = 0.0
            for head in (0, 1):
                side = first_half == (head == 0)
                span = slice(head * HEAD_DIM, (head + 1) * HEAD_DIM)
                mine = jnp.where(side, query_rows, jnp.zeros_like(query_rows))
                grad = jnp.where(side, grad_rows, jnp.zeros_like(grad_rows))
                level = jnp.sum(crossed[span, :], axis=0, keepdims=True)
                scores = lax.dot_general(key_rows, mine, TRANSPOSED, preferred_element_type=f32)
                raised = jnp.exp2(
                    scores * (SCALE * LOG2E) - log_ref[0, head : head + 1, columns]
                )
                probs = jnp.where(row_at < limit, raised, 0.0)
                prob_grad = lax.dot_general(
                    value_rows, grad, TRANSPOSED, preferred_element_type=f32
                )
                score_grad = (probs * (prob_grad - level)).astype(bf16)
                value_part += jnp.dot(probs.astype(bf16), grad, preferred_element_type=f32)
                key_part += jnp.dot(score_grad, mine, preferred_element_type=f32)
                parts.append(jnp.dot(turned[span, :], score_grad, preferred_element_type=f32))
            query_out[columns, :] = (jnp.concatenate(parts, 0).T * SCALE).astype(bf16)
            if start == 0:
                key_total[...] = key_part
                value_total[...] = value_part
            else:
                key_total[...] += key_part
                value_total[...] += value_part
        key_out[...] = (key_total[...] * SCALE).astype(bf16)
        value_out[...] = value_total[...].astype(bf16)

    block = pl.BlockSpec((length, PAIR), lambda i: (0, i))
    return pl.pallas_call(
        body,
        grid=(pairs,),
        out_shape=[shape_of((length, width), bf16)] * 3,
        in_specs=[SMEM] + [block] * 5 + [pl.BlockSpec((1, 8, length), lambda i: (i, 0, 0))],
        out_specs=[block] * 3,
        scratch_shapes=[
            pltpu.VMEM((PAIR, length), bf16),
            pltpu.VMEM((length, PAIR), f32),
            pltpu.VMEM((length, PAIR), f32),
        ],
        compiler_params=PARAMS,
        cost_estimate=cost(
            40 * length * length * width, 18 * length * width, 2 * pairs * length * length
        ),
        name="attend_backward",
    )(prefix, queries, keys, values, attended, grads, logs)


def mix(order, pieces, attended, head_vectors, widths):
    length, width = attended.shape
    count = order.shape[0]
    features = pieces[0].shape[0] // (count // 4) * count

    def body(order_ref, *refs):
        pieces_in, (rows, vectors, weight, second, product, side) = refs[:5], refs[5:]

        @pl.when(pl.program_id(0) == 0)
        def _():
            place_rows(order_ref, pieces_in, (weight, second), count)
            side[...] = side_rows(vectors[2:3, :], vectors[3:4, :], weight[...])

        out, stats = centered_product(rows[...], vectors[2:3, :], weight[...])
        product[:, :features] = out
        product[:, features:] = stats

    return pl.pallas_call(
        body,
        grid=(TILES,),
        out_shape=[shape_of((features, each), bf16) for each in widths]
        + [shape_of((length, features + LANES), bf16), shape_of((8, features), f32)],
        in_specs=[SMEM]
        + [whole(piece.shape) for piece in pieces]
        + [rows_of(attended), whole(head_vectors.shape)],
        out_specs=[whole((features, each)) for each in widths]
        + [
            pl.BlockSpec((length // TILES, features + LANES), lambda i: (i, 0)),
            whole((8, features)),
        ],
        compiler_params=PARAMS,
        cost_estimate=cost(
            2 * length * features * width, 4 * features * sum(widths) + 6 * length * features
        ),
        name="mix",
    )(order, *pieces, attended, head_vectors)


def feed_up(product, product_other, side, side_other, inputs, weight, model_vectors, hidden_vectors):
    length, features = inputs.shape
    width = weight.shape[1]

    def body(one, two, side_one, side_two, x, weight_ref, model, hidden, middle, turned, kept, slope):
        _, _, branch = joined_product(one[...], two[...], side_one, side_two, features)
        offset = side_one[1:2, :] + side_two[1:2, :] + model[2:3, :]
        total = widen(x[...]) + (branch + offset)
        middle[...] = total
        normal, _ = normal_of(total)
        feed = (normal * model[3:4, :] + model[4:5, :]).astype(bf16)
        turned[...] = feed.T
        before = jnp.dot(feed, weight_ref[...], preferred_element_type=f32) + hidden[0:1, :]
        share = 0.5 + 0.5 * lax.erf(before * 0.7071067811865476)
        kept[...] = (before * share).astype(bf16)
        slope[...] = (
            share + before * (0.3989422804014327 * jnp.exp(-0.5 * before * before))
        ).astype(bf16)

    return pl.pallas_call(
        body,
        grid=(TILES,),
        out_shape=[
            shape_of((length, features), f32),
            shape_of((features, length), bf16),
            shape_of((length, width), bf16),
            shape_of((length, width), bf16),
        ],
        in_specs=[
            rows_of(product),
            rows_of(product),
            whole(side.shape),
            whole(side.shape),
            rows_of(inputs),
            whole(weight.shape),
            whole(model_vectors.shape),
            whole(hidden_vectors.shape),
        ],
        out_specs=[
            rows_of(inputs),
            pl.BlockSpec((features, length // TILES), lambda i: (0, i)),
            pl.BlockSpec((length // TILES, width), lambda i: (i, 0)),
            pl.BlockSpec((length // TILES, width), lambda i: (i, 0)),
        ],
        compiler_params=PARAMS,
        cost_estimate=cost(
            2 * length * features * width,
            2 * features * width + 12 * length * features + 4 * length * width,
            2 * length * width,
        ),
        name="feed_up",
    )(product, product_other, side, side_other, inputs, weight, model_vectors, hidden_vectors)


def feed_down(order, pieces, kept, hidden_vectors):
    length, width = kept.shape
    count = order.shape[0]
    features = pieces[0].shape[0] // (count // 4) * count

    def body(order_ref, *refs):
        pieces_in, (rows, vectors, weight, product, side) = refs[:5], refs[5:]

        @pl.when(pl.program_id(0) == 0)
        def _():
            place_rows(order_ref, pieces_in, (weight,), count)
            side[...] = side_rows(vectors[1:2, :], vectors[2:3, :], weight[...])

        out, stats = centered_product(widen(rows[...]), vectors[1:2, :], weight[...])
        product[:, :features] = out
        product[:, features:] = stats

    return pl.pallas_call(
        body,
        grid=(TILES,),
        out_shape=[
            shape_of((features, width), bf16),
            shape_of((length, features + LANES), bf16),
            shape_of((8, features), f32),
        ],
        in_specs=[SMEM]
        + [whole(piece.shape) for piece in pieces]
        + [rows_of(kept), whole(hidden_vectors.shape)],
        out_specs=[
            whole((features, width)),
            pl.BlockSpec((length // TILES, features + LANES), lambda i: (i, 0)),
            whole((8, features)),
        ],
        compiler_params=PARAMS,
        cost_estimate=cost(
            2 * length * features * width, 4 * features * width + 2 * length * (features + width)
        ),
        name="feed_down",
    )(order, *pieces, kept, hidden_vectors)


def feed_back(
    core,
    product,
    product_other,
    side,
    side_other,
    middle,
    cotangent,
    kept,
    slope,
    down,
    up,
    model_vectors,
    hidden_vectors,
):
    length, features = middle.shape
    width = kept.shape[1]
    joined = 2 * width
    share = TILES // 2

    def body(
        core_ref, one, two, side_one, side_two, mid, grad, kept_ref, slope_ref, down_ref, up_ref,
        model, hidden, output, norm_out, before_out, product_out, sums,
    ):
        center, inverse, branch = joined_product(one[...], two[...], side_one, side_two, features)
        offset = side_one[1:2, :] + side_two[1:2, :] + model[5:6, :]

        @pl.when(pl.program_id(0) // share == core_ref[0])
        def _():
            output[...] = (mid[...] + (branch + offset)).astype(bf16)

        rows = widen(grad[...])
        straight = side_one[0:1, :] + side_two[0:1, :]
        mean_scaled = jnp.sum(rows * straight, axis=-1, keepdims=True) / joined
        mean_crossed = jnp.sum(rows * branch, axis=-1, keepdims=True) / joined
        mid_grad = jnp.dot(grad[...], down_ref[...], preferred_element_type=f32)
        normal = (widen(kept_ref[...]) - center) * inverse
        norm_out[...] = (normal * hidden[1:2, :] + hidden[2:3, :]).astype(bf16)
        accumulate(sums, 1, mid_grad * normal)
        accumulate(sums, 2, mid_grad)
        hidden_grad = inverse * (
            mid_grad * hidden[1:2, :] - mean_scaled - normal * mean_crossed
        )
        before = (hidden_grad * widen(slope_ref[...])).astype(bf16)
        before_out[...] = before
        accumulate(sums, 0, widen(before))
        product_out[...] = lax.dot_general(
            before, up_ref[...], TRANSPOSED, preferred_element_type=f32
        ).astype(bf16)

    tile = length // TILES

    def at_rows(columns):
        return pl.BlockSpec((tile, columns), lambda i, core: (i, 0))

    def fixed(array):
        return pl.BlockSpec(array.shape, lambda i, core: (0, 0))

    return pl.pallas_call(
        body,
        grid_spec=pltpu.PrefetchScalarGridSpec(
            num_scalar_prefetch=1,
            grid=(TILES,),
            in_specs=[
                at_rows(features + LANES),
                at_rows(features + LANES),
                fixed(side),
                fixed(side),
                at_rows(features),
                at_rows(features),
                at_rows(width),
                at_rows(width),
                fixed(down),
                fixed(up),
                fixed(model_vectors),
                fixed(hidden_vectors),
            ],
            out_specs=[
                pl.BlockSpec(
                    (tile, features), lambda i, core: (jnp.clip(i - core[0] * share, 0, share - 1), 0)
                ),
                at_rows(width),
                at_rows(width),
                at_rows(features),
                pl.BlockSpec((8, width), lambda i, core: (0, 0)),
            ],
        ),
        out_shape=[
            shape_of((length // 2, features), bf16),
            shape_of((length, width), bf16),
            shape_of((length, width), bf16),
            shape_of((length, features), bf16),
            shape_of((8, width), f32),
        ],
        compiler_params=PARAMS,
        cost_estimate=cost(
            4 * length * features * width,
            4 * features * width + 12 * length * features + 8 * length * width,
        ),
        name="feed_back",
    )(
        core,
        product,
        product_other,
        side,
        side_other,
        middle,
        cotangent,
        kept,
        slope,
        down,
        up,
        model_vectors,
        hidden_vectors,
    )


def mix_back(
    passed,
    passed_other,
    product,
    product_other,
    side,
    side_other,
    middle,
    cotangent,
    attended,
    weight,
    model_vectors,
    head_vectors,
):
    length, features = middle.shape
    width = attended.shape[1]
    joined = 2 * width

    def body(
        back_one, back_two, one, two, side_one, side_two, mid, grad, attended_ref, weight_ref,
        model, head, middle_out, turned, mixed_out, attended_out, sums, head_sums,
    ):
        feed_grad = widen(back_one[...]) + widen(back_two[...])
        normal, inverse = normal_of(mid[...])
        accumulate(sums, 1, feed_grad * normal)
        accumulate(sums, 2, feed_grad)
        middle_grad = widen(grad[...]) + normal_back(feed_grad * model[3:4, :], normal, inverse)
        middle_out[...] = middle_grad
        branch_grad = middle_grad.astype(bf16)
        rows = widen(branch_grad)
        accumulate(sums, 0, rows)
        turned[...] = branch_grad.T
        center, inverse_two, branch = joined_product(
            one[...], two[...], side_one, side_two, features
        )
        straight = side_one[0:1, :] + side_two[0:1, :]
        mean_scaled = jnp.sum(rows * straight, axis=-1, keepdims=True) / joined
        mean_crossed = jnp.sum(rows * branch, axis=-1, keepdims=True) / joined
        mixed_grad = jnp.dot(branch_grad, weight_ref[...], preferred_element_type=f32)
        normal_two = (attended_ref[...] - center) * inverse_two
        mixed_out[...] = (normal_two * head[2:3, :] + head[3:4, :]).astype(bf16)
        accumulate(head_sums, 0, mixed_grad * normal_two)
        accumulate(head_sums, 1, mixed_grad)
        attended_out[...] = (
            inverse_two * (mixed_grad * head[2:3, :] - mean_scaled - normal_two * mean_crossed)
        ).astype(bf16)

    tile = length // TILES
    return pl.pallas_call(
        body,
        grid=(TILES,),
        out_shape=[
            shape_of((length, features), f32),
            shape_of((features, length), bf16),
            shape_of((length, width), bf16),
            shape_of((length, width), bf16),
            shape_of((8, features), f32),
            shape_of((8, width), f32),
        ],
        in_specs=[
            rows_of(passed),
            rows_of(passed),
            rows_of(product),
            rows_of(product),
            whole(side.shape),
            whole(side.shape),
            rows_of(middle),
            rows_of(cotangent),
            rows_of(attended),
            whole(weight.shape),
            whole(model_vectors.shape),
            whole(head_vectors.shape),
        ],
        out_specs=[
            rows_of(middle),
            pl.BlockSpec((features, tile), lambda i: (0, i)),
            rows_of(attended),
            rows_of(attended),
            whole((8, features)),
            whole((8, width)),
        ],
        compiler_params=PARAMS,
        cost_estimate=cost(
            2 * length * features * width, 2 * features * width + 24 * length * features
        ),
        name="mix_back",
    )(
        passed,
        passed_other,
        product,
        product_other,
        side,
        side_other,
        middle,
        cotangent,
        attended,
        weight,
        model_vectors,
        head_vectors,
    )


def project_back(core, parts, weight):
    length, third = parts[0].shape
    features = weight.shape[0]
    tile = length // TILES
    share = TILES // 2

    def body(core_ref, one, two, three, weight_ref, send, keep, sums):
        total = jnp.zeros((tile, features), f32)
        for at, part in enumerate((one, two, three)):
            total += lax.dot_general(
                part[...],
                weight_ref[:, at * third : (at + 1) * third],
                TRANSPOSED,
                preferred_element_type=f32,
            )
        accumulate(sums, 0, widen(one[...]))
        accumulate(sums, 1, widen(three[...]))

        @pl.when(pl.program_id(0) < share)
        def _():
            send[...] = total.astype(bf16)

        @pl.when(pl.program_id(0) >= share)
        def _():
            keep[...] = total

    moved = pl.BlockSpec((tile, third), lambda i, core: ((i + (1 - core[0]) * share) % TILES, 0))
    return pl.pallas_call(
        body,
        grid_spec=pltpu.PrefetchScalarGridSpec(
            num_scalar_prefetch=1,
            grid=(TILES,),
            in_specs=[moved, moved, moved, pl.BlockSpec(weight.shape, lambda i, core: (0, 0))],
            out_specs=[
                pl.BlockSpec((tile, features), lambda i, core: (jnp.minimum(i, share - 1), 0)),
                pl.BlockSpec((tile, features), lambda i, core: (jnp.maximum(i - share, 0), 0)),
                pl.BlockSpec((8, third), lambda i, core: (0, 0)),
            ],
        ),
        out_shape=[
            shape_of((length // 2, features), bf16),
            shape_of((length // 2, features), f32),
            shape_of((8, third), f32),
        ],
        compiler_params=PARAMS,
        cost_estimate=cost(
            6 * length * features * third, 6 * features * third + 6 * length * (features + third)
        ),
        name="project_back",
    )(core, *parts, weight)


def input_back(core, received, kept, middle_grad, tokens, model_vectors):
    rows, features = tokens.shape
    tiles = TILES // 2
    tile = rows // tiles

    def body(core_ref, got, own, mid, x, model, out, sums):
        grad = widen(got[...]) + own[...]
        normal, inverse = normal_of(widen(x[...]))
        accumulate(sums, 0, grad * normal)
        accumulate(sums, 1, grad)
        out[...] = mid[...] + normal_back(grad * model[0:1, :], normal, inverse)

    near = pl.BlockSpec((tile, features), lambda i, core: (i, 0))
    return pl.pallas_call(
        body,
        grid_spec=pltpu.PrefetchScalarGridSpec(
            num_scalar_prefetch=1,
            grid=(tiles,),
            in_specs=[
                near,
                near,
                pl.BlockSpec((tile, features), lambda i, core: (i + core[0] * tiles, 0)),
                near,
                pl.BlockSpec(model_vectors.shape, lambda i, core: (0, 0)),
            ],
            out_specs=[near, pl.BlockSpec((8, features), lambda i, core: (0, 0))],
        ),
        out_shape=[shape_of((rows, features), f32), shape_of((8, features), f32)],
        compiler_params=PARAMS,
        cost_estimate=cost(10 * rows * features, 16 * rows * features),
        name="input_back",
    )(core, received, kept, middle_grad, tokens, model_vectors)


def weight_grad(order, pairs, tile):
    features, tokens = pairs[0][0].shape
    width = sum(right.shape[1] for _, right in pairs)
    count = order.shape[0]
    shard = features // count
    lefts = []
    steps = []
    for left, right in pairs:
        if not any(left is known for known in lefts):
            lefts.append(left)
        at = [left is known for known in lefts].index(True)
        steps += [(at, len(steps), 0)] if right.shape[1] == tile else []
    rights = [right for _, right in pairs]
    single = len(pairs) == 1

    def body(order_ref, *refs):
        left_refs, right_refs = refs[: len(lefts)], refs[len(lefts) : -3]
        keep, send, total = refs[-3:]
        if single:
            total[...] = jnp.dot(left_refs[0][...], right_refs[0][...], preferred_element_type=f32)
        else:
            for at, step, _ in steps:

                @pl.when(pl.program_id(0) == step)
                def _(at=at, step=step):
                    total[...] = jnp.dot(
                        left_refs[at][...], right_refs[step][...], preferred_element_type=f32
                    )

        for block in range(count):
            place = pl.multiple_of(order_ref[block] * shard, 16)
            out, at = (keep, block) if block < count // 2 else (send, block - count // 2)
            out[at * shard : (at + 1) * shard, :] = total[pl.ds(place, shard), :].astype(bf16)

    return pl.pallas_call(
        body,
        grid=(width // tile,),
        out_shape=[shape_of((features // 2, width), bf16)] * 2,
        in_specs=[SMEM]
        + [whole(left.shape) for left in lefts]
        + (
            [pl.BlockSpec((tokens, tile), lambda i: (0, i))]
            if single
            else [whole(right.shape) for right in rights]
        ),
        out_specs=[pl.BlockSpec((features // 2, tile), lambda i: (0, i))] * 2,
        scratch_shapes=[pltpu.VMEM((features, tile), f32)],
        compiler_params=PARAMS,
        cost_estimate=cost(
            2 * tokens * features * width,
            2 * (tokens * (features + width) + features * width),
        ),
        name="weight_grad",
    )(order, *lefts, *rights)


def on_device(
    tokens,
    cotangent,
    prefix,
    query_weight,
    key_weight,
    value_weight,
    out_weight,
    up_weight,
    down_weight,
    model_vectors,
    head_vectors,
    hidden_vectors,
):
    ring = Ring(lax.axis_size("dp"))
    order = ring.gather_order()
    near, far = ring.scatter_order(1), ring.scatter_order(2)
    core = lax.axis_index("tensor").astype(jnp.int32)[None]
    half, full = query_weight.shape[1], up_weight.shape[1]
    features = tokens.shape[1]

    bias = jnp.concatenate([head_vectors[0], jnp.zeros_like(head_vectors[0]), head_vectors[1]])
    first_block = ring.along_lines(join(query_weight, key_weight, value_weight))
    second_block = ring.along_lines(after(join(out_weight, up_weight), first_block))
    third_block = ring.along_lines(after(down_weight, second_block))
    first_sides = ring.to_sides(first_block)
    first_pieces = (first_block, *first_sides, *ring.to_corner(*first_sides))

    inputs, grads, attend_in, attend_turned, grads_turned, grad_sums = prepare(
        core, tokens, flip_partner(tokens), cotangent, flip_partner(cotangent), model_vectors
    )

    second_block = after(second_block, first_pieces)
    second_sides = ring.to_sides(second_block)
    first_weight, queries, keys, values = project(order, first_pieces, attend_in, bias[None])
    attended, logs = attend_forward(prefix, queries, keys, values)
    second_pieces = (second_block, *second_sides, *ring.to_corner(*second_sides))
    third_block = after(third_block, second_sides)
    third_sides = ring.to_sides(third_block)
    out_full, up_full, mixed, mixed_side = mix(
        order, second_pieces, attended, head_vectors, (half, full)
    )
    mixed_other, mixed_side_other = flip_partner(mixed), flip_partner(mixed_side)
    middle, feed_turned, kept, slope = feed_up(
        after(mixed, third_sides),
        mixed_other,
        mixed_side,
        mixed_side_other,
        inputs,
        up_full,
        model_vectors,
        hidden_vectors,
    )
    third_pieces = (third_block, *third_sides, *ring.to_corner(*third_sides))
    down_full, fed, fed_side = feed_down(order, third_pieces, kept, hidden_vectors)
    fed_other, fed_side_other = flip_partner(fed), flip_partner(fed_side)
    output, feed_mid, before_grad, passed, hidden_sums = feed_back(
        core,
        fed,
        fed_other,
        fed_side,
        fed_side_other,
        middle,
        grads,
        kept,
        slope,
        down_full,
        up_full,
        model_vectors,
        hidden_vectors,
    )
    passed_other = flip_partner(passed)
    down_keep, down_send = weight_grad(far, [(grads_turned, feed_mid)], full // 2)
    up_keep, up_send = weight_grad(near, [(feed_turned, before_grad)], full // 2)
    down_got, up_got = ring.flip(down_send, 2), ring.flip(up_send, 1)

    middle_grad, branch_turned, mixed_in, attended_grad, model_sums, head_sums = mix_back(
        passed,
        passed_other,
        mixed,
        mixed_other,
        mixed_side,
        mixed_side_other,
        middle,
        grads,
        attended,
        out_full,
        model_vectors,
        head_vectors,
    )
    query_grad, key_grad, value_grad = attend_backward(
        prefix, queries, keys, values, attended, attended_grad, logs
    )
    down_own, down_away = ring.sum_first(down_keep, after(down_got, query_grad))
    up_own, up_away = ring.sum_first(up_keep, after(up_got, query_grad))
    down_second, up_second = ring.flip(down_away, 1), ring.flip(up_away, 2)
    parts = after((query_grad, key_grad, value_grad), down_away, up_away)
    send, keep, bias_sums = project_back(core, parts, first_weight)
    received = flip_partner(send)
    query_keep, query_send = weight_grad(
        near, [(attend_turned, query_grad), (attend_turned, after(value_grad, send))], half
    )
    wide = jnp.concatenate(
        [up_own + widen(up_second), down_own + widen(down_second)], axis=1
    )
    wide_grads = ring.sum_lines(after(wide, query_send))
    up_grad, down_grad = wide_grads[:, :full], wide_grads[:, full:]
    key_keep, key_send = weight_grad(
        far, [(attend_turned, after(key_grad, wide)), (branch_turned, mixed_in)], half
    )
    query_own, query_away = ring.sum_first(query_keep, ring.flip(query_send, 1))
    key_own, key_away = ring.sum_first(key_keep, ring.flip(key_send, 2))
    narrow = jnp.concatenate(
        [
            query_own + widen(ring.flip(query_away, 2)),
            key_own + widen(ring.flip(key_away, 1)),
        ],
        axis=1,
    )
    narrow = ring.sum_lines(narrow)
    query_weight_grad, value_weight_grad, key_weight_grad, out_grad = (
        narrow[:, at * half : (at + 1) * half] for at in range(4)
    )
    input_grad, first_sums = input_back(core, received, keep, middle_grad, tokens, model_vectors)
    first_sums = first_sums + flip_partner(first_sums)

    model_grads = jnp.concatenate([first_sums[:2], model_sums[:3], grad_sums[:1]], 0)
    head_grads = jnp.concatenate([bias_sums[:2], head_sums[:2]], 0)
    hidden_grads = hidden_sums[:3]
    sums = ring.all_sum(
        jnp.concatenate([g.reshape(-1, LANES) for g in (model_grads, head_grads, hidden_grads)], 0)
    )
    rows_one, rows_two = model_grads.size // LANES, head_grads.size // LANES
    model_sum = sums[:rows_one].reshape(model_grads.shape)
    head_sum = sums[rows_one : rows_one + rows_two].reshape(head_grads.shape)
    hidden_sum = sums[rows_one + rows_two :].reshape(hidden_grads.shape)
    return (
        output,
        input_grad,
        query_weight_grad,
        key_weight_grad,
        value_weight_grad,
        out_grad,
        up_grad,
        down_grad,
        model_sum,
        head_sum,
        hidden_sum,
    )


def solution(mesh):
    return jax.shard_map(
        on_device,
        mesh=mesh,
        in_specs=(
            P(("dp", "tensor"), None),
            P(("dp", "tensor"), None),
            P("dp"),
            P("dp", "tensor"),
            P("dp", "tensor"),
            P("dp", "tensor"),
            P("dp", "tensor"),
            P("dp", "tensor"),
            P("dp", "tensor"),
            P(),
            P(None, "tensor"),
            P(None, "tensor"),
        ),
        out_specs=(
            P(("dp", "tensor"), None),
            P(("dp", "tensor"), None),
            P("dp", "tensor"),
            P("dp", "tensor"),
            P("dp", "tensor"),
            P("dp", "tensor"),
            P("dp", "tensor"),
            P("dp", "tensor"),
            P(),
            P(None, "tensor"),
            P(None, "tensor"),
        ),
        check_vma=False,
    )
```

time: 455 us -> 305 us (0.67); the launches traced: 448 us -> 303 us
  matrix products: 108 us -> 0 us
  Pallas kernels: 37 us -> 132 us
  other arithmetic: 85.4 us -> 14.2 us
  local copies, waits for them, and re-layouts: 57.6 us -> 23.3 us
  waiting for transfers between devices: 102 us -> 81.5 us
    dot_general x26 -> x0, matrix products: 108 us -> none  [the longest x6 34.6 us: matmul(): return jnp.dot(left_side, right_side, preferred_element_type=jnp.float32)]
    pallas_call x8 -> x17, Pallas kernels: 37 us -> 132 us  [the longest x4 22.2 us: weight_grad(): pl.pallas_call(body, grid=(width // tile,), out_shape=[shape_of((features...]
    reduce_sum x11 -> x0, other arithmetic: 34.2 us -> none  [the longest x1 7.68 us: on_device(): up_bias_grad = jnp.sum(before_grad, axis=0, dtype=jnp.float32)]
    ppermute x39, waiting for transfers between devices: 99.5 us -> 80.5 us  [shift(): return lax.ppermute(values, 'dp', pairs)]
    convert_element_type x12 -> x5, other arithmetic: 22.1 us -> 4.79 us  [the longest x3 4.57 us: sum_first(): return (own, (widen(keep[half:]) + widen(got[half:])).astype(bf16))]
    while x38 -> x0, local copies, waits for them, and re-layouts: 9.48 us -> none
    select_n x4 -> x0, other arithmetic: 6.99 us -> none  [whole_sequence(): jnp.where(first, jnp.concatenate([values, other], 0), jnp.concatenate([ot...]
    convert_element_type x6 -> x0, local copies, waits for them, and re-layouts: 6.61 us -> none  [the longest x4 3.06 us: share_of_sum(): return mine + flip_partner(theirs.astype(jnp.bfloat16)).astype(jnp.float32)]
  transfers between devices with their start and end apart: 52 -> 48, of which waited for: 23 -> 18; matrix products, arithmetic and copies ran while one was open for 46% -> 8% of each run, Pallas kernels for 7% -> 34%
where the time goes in v2:
time: 305 us; the launch traced here: 303 us
  Pallas kernels  132 us (43%)
  waiting for transfers between devices  81.5 us (27%)
  starting transfers between devices  50.3 us (16%)
  local copies, waits for them, and re-layouts  23.3 us (8%)
  other arithmetic  14.2 us (5%)
    ppermute x39, waiting for transfers between devices, shift(): return lax.ppermute(values, 'dp', pairs)  80.5 us
    ppermute x39, starting transfers between devices, shift(): return lax.ppermute(values, 'dp', pairs)  49 us
    pallas_call x4, Pallas kernels, weight_grad(): pl.pallas_call(body, grid=(width // tile,), out_shape=[shape_of((features...  22.2 us
    pallas_call x1, Pallas kernels, attend_backward(): pl.pallas_call(body, grid=(pairs,), out_shape=[shape_of((length, width),...  20 us
    pallas_call x1, Pallas kernels, attend_forward(): pl.pallas_call(body, grid=(pairs,), out_shape=[shape_of((length, width),...  14.9 us
    pallas_call x1, Pallas kernels, feed_back(): pl.pallas_call(body, grid_spec=pltpu.PrefetchScalarGridSpec(num_scalar_pr...  14 us
    pallas_call x1, Pallas kernels, feed_up(): pl.pallas_call(body, grid=(TILES,), out_shape=[shape_of((length, features...  10.6 us
    pallas_call x1, Pallas kernels, mix_back(): pl.pallas_call(body, grid=(TILES,), out_shape=[shape_of((length, features...  10.2 us
  transfers between devices with their start and end apart: 48, of which 18 were waited for; matrix products, arithmetic and copies ran while one was open for 8% of the time, Pallas kernels for 34%

profile of v2, /device:TPU:0, one launch (start us, length us, event | category | flops | bytes accessed | tf_op | source)
XLA Modules:
  0.0 303.3 jit_solution(9876541279709569570)
XLA Ops:
  2.1 5.1 %collective-permute-start.2 = (bf16[48,1152]{1,0:T(8,128)(2,1)}, bf16[48,1152]{1,0:T(8,128)(2,1)S(1)}, u32[]{:S(2)}, u32[]{:S(2)}) collective-permute-start(bf16[48,1152]{1,0:T(8,128)(2,1)} %join.3), channel_id=1, source_target_pairs={{0,24},{2,26},{4,28},{6,30},{8,0},{10,2},{12,4},{14,6},{16,8},{18,... | collective-permute-start | bytes 331784 | tf_op jit(solution)/shard_map/ppermute | solution.py:68
  11.1 5.9 %collective-permute-done.1 = bf16[48,1152]{1,0:T(8,128)(2,1)S(1)} collective-permute-done((bf16[48,1152]{1,0:T(8,128)(2,1)}, bf16[48,1152]{1,0:T(8,128)(2,1)S(1)}, u32[]{:S(2)}, u32[]{:S(2)}) %collective-permute-start.1) | collective-permute-done | bytes 110624 | tf_op jit(solution)/shard_map/ppermute | solution.py:68
  23.6 5.5 %collective-permute-done.3 = bf16[48,1920]{1,0:T(8,128)(2,1)S(1)} collective-permute-done((bf16[48,1920]{1,0:T(8,128)(2,1)}, bf16[48,1920]{1,0:T(8,128)(2,1)S(1)}, u32[]{:S(2)}, u32[]{:S(2)}) %collective-permute-start.3) | collective-permute-done | bytes 184352 | tf_op jit(solution)/shard_map/ppermute | solution.py:68
  35.2 6.9 %collective-permute-done.9.refs_1_ = bf16[192,1152]{1,0:T(8,128)(2,1)S(1)} collective-permute-done((bf16[192,1152]{1,0:T(8,128)(2,1)S(1)}, bf16[192,1152]{1,0:T(8,128)(2,1)S(1)}, u32[]{:S(2)}, u32[]{:S(2)}) %collective-permute-start.9) | collective-permute-done | bytes 442400 | tf_op jit(solution)/shard_map/ppermute | solution.py:68
  45.7 4.1 %collective-permute-done.11.refs_3_ = bf16[96,1152]{1,0:T(8,128)(2,1)} collective-permute-done((bf16[96,1152]{1,0:T(8,128)(2,1)S(1)}, bf16[96,1152]{1,0:T(8,128)(2,1)}, u32[]{:S(2)}, u32[]{:S(2)}) %collective-permute-start.11) | collective-permute-done | bytes 221216 | tf_op jit(solution)/shard_map/ppermute | solution.py:68
  55.9 5.9 %prepare.1 = (bf16[1024,768]{1,0:T(8,128)(2,1)}, bf16[1024,768]{1,0:T(8,128)(2,1)}, bf16[1024,768]{1,0:T(8,128)(2,1)}, bf16[768,1024]{1,0:T(8,128)(2,1)}, bf16[768,1024]{1,0:T(8,128)(2,1)}, /*index=5*/f32[8,768]{1,0:T(8,128)}) custom-call(s32[1]{0:T(128)} %bitcast.core_ref, bf16[512,768]{1,0:T(8,128)(2,1)} %x.1, bf16[512,768]{1,0:T(8,128)(2,1)} %copy-done.5, ...), custom_call_target="tpu_custom_call" | custom-call | flops 31457280 | bytes 11010048 | tf_op jit(solution)/shard_map/prepare/pallas_call | solution.py:288
  61.8 5.8 %project.1 = (bf16[768,1152]{1,0:T(8,128)(2,1)}, bf16[1024,384]{1,0:T(8,128)(2,1)}, bf16[1024,384]{1,0:T(8,128)(2,1)}, bf16[1024,384]{1,0:T(8,128)(2,1)}) custom-call(s32[16]{0:T(128)} %stack.113.order_ref, bf16[192,1152]{1,0:T(8,128)(2,1)} %copy-done.10, bf16[192,1152]{1,0:T(8,128)(2,1)} %copy-done.18, bf16[192,1152]{1,0:T(8,128)(2,1)} %copy-done.17, ...), custom_call_target="tpu_custom_call" | custom-call | flops 7247757312 | bytes 7471104 | tf_op jit(solution)/shard_map/project/pallas_call | solution.py:343
  68.8 14.9 %attend_forward.1 = (f32[1024,384]{1,0:T(8,128)}, f32[3,8,1024]{2,1,0:T(8,128)}) custom-call(s32[1]{0:T(128)S(6)} %copy.26.prefix_ref, bf16[1024,384]{1,0:T(8,128)(2,1)} %get-tuple-element.79.query_ref, bf16[1024,384]{1,0:T(8,128)(2,1)} %get-tuple-element.80.key_ref, bf16[1024,384]{1,0:T(8,128)(2,1)} %get-tuple-element.81.value_ref), custom_call_target="tpu_custom_call" | custom-call | flops 25769803776 | bytes 3932160 | tf_op jit(solution)/shard_map/attend_forward/pallas_call | solution.py:395
  84.7 6.5 %mix.1 = (bf16[768,384]{1,0:T(8,128)(2,1)}, bf16[768,1536]{1,0:T(8,128)(2,1)}, bf16[1024,896]{1,0:T(8,128)(2,1)}, f32[8,768]{1,0:T(8,128)}) custom-call(s32[16]{0:T(128)} %stack.113.order_ref, bf16[192,1920]{1,0:T(8,128)(2,1)} %constant_dynamic-update-slice_fusion.refs_0_, bf16[192,1920]{1,0:T(8,128)(2,1)} %copy-done.13, bf16[192,1920]{1,0:T(8,128)(2,1)} %copy-done.12, ...), custom_call_target="tpu_custom_call" | custom-call | flops 2415919104 | bytes 10616832 | tf_op jit(solution)/shard_map/mix/pallas_call | solution.py:507
  97.9 10.8 %collective-permute-done.7 = bf16[48,1536]{1,0:T(8,128)(2,1)S(1)} collective-permute-done((bf16[48,1536]{1,0:T(8,128)(2,1)S(1)}, bf16[48,1536]{1,0:T(8,128)(2,1)S(1)}, u32[]{:S(2)}, u32[]{:S(2)}) %collective-permute-start.7) | collective-permute-done | bytes 147488 | tf_op jit(solution)/shard_map/ppermute | solution.py:68
  111.9 12.0 %collective-permute-done.16.refs_2_ = bf16[192,1536]{1,0:T(8,128)(2,1)S(1)} collective-permute-done((bf16[192,1536]{1,0:T(8,128)(2,1)S(1)}, bf16[192,1536]{1,0:T(8,128)(2,1)S(1)}, u32[]{:S(2)}, u32[]{:S(2)}) %collective-permute-start.16) | collective-permute-done | bytes 589856 | tf_op jit(solution)/shard_map/ppermute | solution.py:68
  128.4 10.6 %feed_up.1 = (f32[1024,768]{1,0:T(8,128)}, bf16[768,1024]{1,0:T(8,128)(2,1)}, bf16[1024,1536]{1,0:T(8,128)(2,1)}, bf16[1024,1536]{1,0:T(8,128)(2,1)}) custom-call(bf16[1024,896]{1,0:T(8,128)(2,1)} %get-tuple-element.84.one, bf16[1024,896]{1,0:T(8,128)(2,1)} %copy-done, f32[8,768]{1,0:T(8,128)} %get-tuple-element.85.side_one, f32[8,768]{1,0:T(8,128)} %copy-done.21, ...), custom_call_target="tpu_custom_call" | custom-call | flops 9663676416 | bytes 18087936 | tf_op jit(solution)/shard_map/feed_up/pallas_call | solution.py:547
  139.7 8.3 %feed_down.1 = (bf16[768,1536]{1,0:T(8,128)(2,1)}, bf16[1024,896]{1,0:T(8,128)(2,1)}, f32[8,768]{1,0:T(8,128)}) custom-call(s32[16]{0:T(128)} %stack.113.order_ref, bf16[192,1536]{1,0:T(8,128)(2,1)} %copy-done.9, bf16[192,1536]{1,0:T(8,128)(2,1)} %copy-done.16, bf16[192,1536]{1,0:T(8,128)(2,1)} %copy-done.15, ...), custom_call_target="tpu_custom_call" | custom-call | flops 9663676416 | bytes 9437184 | tf_op jit(solution)/shard_map/feed_down/pallas_call | solution.py:599
  153.3 14.0 %feed_back.1 = (bf16[512,768]{1,0:T(8,128)(2,1)}, bf16[1024,1536]{1,0:T(8,128)(2,1)}, bf16[1024,1536]{1,0:T(8,128)(2,1)}, bf16[1024,768]{1,0:T(8,128)(2,1)}, f32[8,1536]{1,0:T(8,128)}) custom-call(s32[1]{0:T(128)} %bitcast.core_ref, bf16[1024,896]{1,0:T(8,128)(2,1)} %get-tuple-element.89.one, bf16[1024,896]{1,0:T(8,128)(2,1)} %copy-done.24, ...), custom_call_target="tpu_custom_call" | custom-call | flops 19327352832 | bytes 26738688 | tf_op jit(solution)/shard_map/feed_back/pallas_call | solution.py:681
  168.9 6.0 %weight_grad.5 = (bf16[384,1536]{1,0:T(8,128)(2,1)}, bf16[384,1536]{1,0:T(8,128)(2,1)}) custom-call(s32[16]{0:T(128)} %stack.119.order_ref, bf16[768,1024]{1,0:T(8,128)(2,1)} %get-tuple-element.108.refs_0_, bf16[1024,1536]{1,0:T(8,128)(2,1)} %get-tuple-element.109.refs_1_), custom_call_target="tpu_custom_call" | custom-call | flops 9663676416 | bytes 7077888 | tf_op jit(solution)/shard_map/weight_grad/pallas_call | solution.py:962
  175.4 5.9 %weight_grad.4 = (bf16[384,1536]{1,0:T(8,128)(2,1)}, bf16[384,1536]{1,0:T(8,128)(2,1)}) custom-call(s32[16]{0:T(128)} %stack.118.order_ref, bf16[768,1024]{1,0:T(8,128)(2,1)} %get-tuple-element.103.refs_0_, bf16[1024,1536]{1,0:T(8,128)(2,1)} %get-tuple-element.104.refs_1_), custom_call_target="tpu_custom_call" | custom-call | flops 9663676416 | bytes 7077888 | tf_op jit(solution)/shard_map/weight_grad/pallas_call | solution.py:962
  183.6 10.2 %mix_back.1 = (f32[1024,768]{1,0:T(8,128)}, bf16[768,1024]{1,0:T(8,128)(2,1)}, bf16[1024,384]{1,0:T(8,128)(2,1)}, bf16[1024,384]{1,0:T(8,128)(2,1)}, f32[8,768]{1,0:T(8,128)}, /*index=5*/f32[8,384]{1,0:T(8,128)}) custom-call(bf16[1024,768]{1,0:T(8,128)(2,1)} %get-tuple-element.96.back_one, bf16[1024,768]{1,0:T(8,128)(2,1)} %copy-done.1, ...), custom_call_target="tpu_custom_call" | custom-call | flops 2415919104 | bytes 19464192 | tf_op jit(solution)/shard_map/mix_back/pallas_call | solution.py:788
  193.8 20.0 %attend_backward.1 = (bf16[1024,384]{1,0:T(8,128)(2,1)}, bf16[1024,384]{1,0:T(8,128)(2,1)}, bf16[1024,384]{1,0:T(8,128)(2,1)}) custom-call(s32[1]{0:T(128)S(6)} %copy.26.prefix_ref, bf16[1024,384]{1,0:T(8,128)(2,1)} %get-tuple-element.79.query_ref, bf16[1024,384]{1,0:T(8,128)(2,1)} %get-tuple-element.80.key_ref, ...), custom_call_target="tpu_custom_call" | custom-call | flops 64424509440 | bytes 7077888 | tf_op jit(solution)/shard_map/attend_backward/pallas_call | solution.py:471
  218.7 6.7 %project_back.1 = (bf16[512,768]{1,0:T(8,128)(2,1)}, f32[512,768]{1,0:T(8,128)}, f32[8,384]{1,0:T(8,128)}) custom-call(s32[1]{0:T(128)} %bitcast.core_ref, bf16[1024,384]{1,0:T(8,128)(2,1)} %get-tuple-element.113.one.refs_1_, bf16[1024,384]{1,0:T(8,128)(2,1)} %get-tuple-element.126.two.refs_2_, bf16[1024,384]{1,0:T(8,128)(2,1)} %get-tuple-element.122.three.refs_2_, ...), custom_call_target="tpu_custom_call" | custom-call | flops 7247757312 | bytes 8847360 | tf_op jit(solution)/shard_map/project_back/pallas_call | solution.py:869
  226.9 4.9 %weight_grad.6 = (bf16[384,768]{1,0:T(8,128)(2,1)}, bf16[384,768]{1,0:T(8,128)(2,1)}) custom-call(s32[16]{0:T(128)} %stack.119.order_ref, bf16[768,1024]{1,0:T(8,128)(2,1)} %get-tuple-element.121.refs_0_, bf16[1024,384]{1,0:T(8,128)(2,1)} %get-tuple-element.113.one.refs_1_, bf16[1024,384]{1,0:T(8,128)(2,1)} %get-tuple-element.122.three.refs_2_), custom_call_target="tpu_custom_call" | custom-call | flops 4831838208 | bytes 4325376 | tf_op jit(solution)/shard_map/weight_grad/pallas_call | solution.py:962
  235.8 5.3 %weight_grad.7 = (bf16[384,768]{1,0:T(8,128)(2,1)}, bf16[384,768]{1,0:T(8,128)(2,1)}) custom-call(s32[16]{0:T(128)} %stack.118.order_ref, bf16[768,1024]{1,0:T(8,128)(2,1)} %get-tuple-element.121.refs_0_, bf16[768,1024]{1,0:T(8,128)(2,1)} %get-tuple-element.125.refs_1_, bf16[1024,384]{1,0:T(8,128)(2,1)} %get-tuple-element.126.two.refs_2_, ...), custom_call_target="tpu_custom_call" | custom-call | flops 4831838208 | bytes 4325376 | tf_op jit(solution)/shard_map/weight_grad/pallas_call | solution.py:962
  260.2 5.4 %collective-permute-done.42 = bf16[48,3072]{1,0:T(8,128)(2,1)S(1)} collective-permute-done((bf16[48,3072]{1,0:T(8,128)(2,1)}, bf16[48,3072]{1,0:T(8,128)(2,1)S(1)}, u32[]{:S(2)}, u32[]{:S(2)}) %collective-permute-start.42) | collective-permute-done | bytes 294944 | tf_op jit(solution)/shard_map/ppermute | solution.py:68
  265.6 10.0 %collective-permute-done.41 = bf16[48,3072]{1,0:T(8,128)(2,1)} collective-permute-done((bf16[48,3072]{1,0:T(8,128)(2,1)}, bf16[48,3072]{1,0:T(8,128)(2,1)}, u32[]{:S(2)}, u32[]{:S(2)}) %collective-permute-start.41) | collective-permute-done | bytes 294944 | tf_op jit(solution)/shard_map/ppermute | solution.py:68
  296.3 6.2 %collective-permute-done.38 = bf16[48,1536]{1,0:T(8,128)(2,1)S(1)} collective-permute-done((bf16[48,1536]{1,0:T(8,128)(2,1)S(1)}, bf16[48,1536]{1,0:T(8,128)(2,1)S(1)}, u32[]{:S(2)}, u32[]{:S(2)}) %collective-permute-start.38) | collective-permute-done | bytes 147488 | tf_op jit(solution)/shard_map/ppermute | solution.py:68
  (205 shorter events, 104.4 us)
Async XLA Ops:
  8.2 46.6 %collective-permute-start.22 = (bf16[512,768]{1,0:T(8,128)(2,1)}, bf16[512,768]{1,0:T(8,128)(2,1)S(1)}, u32[]{:S(2)}, u32[]{:S(2)}) collective-permute-start(bf16[512,768]{1,0:T(8,128)(2,1)} %g_own.1), channel_id=1, source_target_pairs={{0,1},{1,0},{2,3},{3,2},{4,5},{5,4},{6,7},{7,6},{8,9},{9,8},{10,11... | collective-permute-start | bytes 2359304 | tf_op jit(solution)/shard_map/ppermute | solution.py:26
  8.2 46.6 %collective-permute-start.21 = (bf16[512,768]{1,0:T(8,128)(2,1)}, bf16[512,768]{1,0:T(8,128)(2,1)S(1)}, u32[]{:S(2)}, u32[]{:S(2)}) collective-permute-start(bf16[512,768]{1,0:T(8,128)(2,1)} %x.1), channel_id=1, source_target_pairs={{0,1},{1,0},{2,3},{3,2},{4,5},{5,4},{6,7},{7,6},{8,9},{9,8},{10,11... | collective-permute-start | bytes 2359304 | tf_op jit(solution)/shard_map/ppermute | solution.py:26
  18.0 14.9 %collective-permute-start.4 = (bf16[48,1920]{1,0:T(8,128)(2,1)}, bf16[48,1920]{1,0:T(8,128)(2,1)S(1)}, u32[]{:S(2)}, u32[]{:S(2)}) collective-permute-start(bf16[48,1920]{1,0:T(8,128)(2,1)} %join.2), channel_id=1, source_target_pairs={{0,16},{2,18},{4,20},{6,22},{8,24},{10,26},{12,28},{14,30},{16,0},... | collective-permute-start | bytes 552968 | tf_op jit(solution)/shard_map/ppermute | solution.py:68
  49.7 17.8 %collective-permute-start.14 = (bf16[192,1920]{1,0:T(8,128)(2,1)}, bf16[192,1920]{1,0:T(8,128)(2,1)S(1)}, u32[]{:S(2)}, u32[]{:S(2)}) collective-permute-start(bf16[192,1920]{1,0:T(8,128)(2,1)} %constant_dynamic-update-slice_fusion.refs_0_), channel_id=1, source_target_pairs={{0,4},{2,6},{4,0},{6,2},{8,12},{10,14},{12,8},{14,10},{16,20},{18,... | collective-permute-start | bytes 2211848 | tf_op jit(solution)/shard_map/ppermute | solution.py:68
  51.3 17.0 %collective-permute-start.13 = (bf16[192,1920]{1,0:T(8,128)(2,1)}, bf16[192,1920]{1,0:T(8,128)(2,1)S(1)}, u32[]{:S(2)}, u32[]{:S(2)}) collective-permute-start(bf16[192,1920]{1,0:T(8,128)(2,1)} %constant_dynamic-update-slice_fusion.refs_0_), channel_id=1, source_target_pairs={{0,2},{2,0},{4,6},{6,4},{8,10},{10,8},{12,14},{14,12},{16,18},{18,... | collective-permute-start | bytes 2211848 | tf_op jit(solution)/shard_map/ppermute | solution.py:68
  67.6 16.2 %collective-permute-start.20 = (bf16[96,1920]{1,0:T(8,128)(2,1)S(1)}, bf16[96,1920]{1,0:T(8,128)(2,1)S(1)}, u32[]{:S(2)}, u32[]{:S(2)}) collective-permute-start(bf16[96,1920]{1,0:T(8,128)(2,1)S(1)} %slice.193), channel_id=1, source_target_pairs={{0,2},{2,0},{4,6},{6,4},{8,10},{10,8},{12,14},{14,12},{16,18},{18,... | collective-permute-start | bytes 1105928 | tf_op jit(solution)/shard_map/ppermute | solution.py:68
  68.3 15.5 %collective-permute-start.19 = (bf16[96,1920]{1,0:T(8,128)(2,1)S(1)}, bf16[96,1920]{1,0:T(8,128)(2,1)S(1)}, u32[]{:S(2)}, u32[]{:S(2)}) collective-permute-start(bf16[96,1920]{1,0:T(8,128)(2,1)S(1)} %slice.192), channel_id=1, source_target_pairs={{0,4},{2,6},{4,0},{6,2},{8,12},{10,14},{12,8},{14,10},{16,20},{18,... | collective-permute-start | bytes 1105928 | tf_op jit(solution)/shard_map/ppermute | solution.py:68
  91.2 35.9 %collective-permute-start.23 = (bf16[1024,896]{1,0:T(8,128)(2,1)}, bf16[1024,896]{1,0:T(8,128)(2,1)S(1)}, u32[]{:S(2)}, u32[]{:S(2)}) collective-permute-start(bf16[1024,896]{1,0:T(8,128)(2,1)} %get-tuple-element.84.one), channel_id=1, source_target_pairs={{0,1},{1,0},{2,3},{3,2},{4,5},{5,4},{6,7},{7,6},{8,9},{9,8},{10,11... | collective-permute-start | bytes 5505032 | tf_op jit(solution)/shard_map/ppermute | solution.py:26
  91.3 17.4 %collective-permute-start.7 = (bf16[48,1536]{1,0:T(8,128)(2,1)S(1)}, bf16[48,1536]{1,0:T(8,128)(2,1)S(1)}, u32[]{:S(2)}, u32[]{:S(2)}) collective-permute-start(bf16[48,1536]{1,0:T(8,128)(2,1)S(1)} %copy-done.14), channel_id=1, source_target_pairs={{0,16},{2,18},{4,20},{6,22},{8,24},{10,26},{12,28},{14,30},{16,0},... | collective-permute-start | bytes 442376 | tf_op jit(solution)/shard_map/ppermute | solution.py:68
  108.8 15.0 %collective-permute-start.16 = (bf16[192,1536]{1,0:T(8,128)(2,1)S(1)}, bf16[192,1536]{1,0:T(8,128)(2,1)S(1)}, u32[]{:S(2)}, u32[]{:S(2)}) collective-permute-start(bf16[192,1536]{1,0:T(8,128)(2,1)S(1)} %pad_maximum_fusion.2.refs_0_), channel_id=1, source_target_pairs={{0,4},{2,6},{4,0},{6,2},{8,12},{10,14},{12,8},{14,10},{16,20},{18,... | collective-permute-start | bytes 1769480 | tf_op jit(solution)/shard_map/ppermute | solution.py:68
  110.4 15.1 %collective-permute-start.15 = (bf16[192,1536]{1,0:T(8,128)(2,1)S(1)}, bf16[192,1536]{1,0:T(8,128)(2,1)S(1)}, u32[]{:S(2)}, u32[]{:S(2)}) collective-permute-start(bf16[192,1536]{1,0:T(8,128)(2,1)S(1)} %pad_maximum_fusion.2.refs_0_), channel_id=1, source_target_pairs={{0,2},{2,0},{4,6},{6,4},{8,10},{10,8},{12,14},{14,12},{16,18},{18,... | collective-permute-start | bytes 1769480 | tf_op jit(solution)/shard_map/ppermute | solution.py:68
  111.9 15.2 %collective-permute-start.24 = (f32[8,768]{1,0:T(8,128)S(1)}, f32[8,768]{1,0:T(8,128)S(1)}, u32[]{:S(2)}, u32[]{:S(2)}) collective-permute-start(f32[8,768]{1,0:T(8,128)S(1)} %copy-done.20), channel_id=1, source_target_pairs={{0,1},{1,0},{2,3},{3,2},{4,5},{5,4},{6,7},{7,6},{8,9},{9,8},{10,11... | collective-permute-start | bytes 73736 | tf_op jit(solution)/shard_map/ppermute | solution.py:26
  123.9 15.1 %collective-permute-start.18 = (bf16[96,1536]{1,0:T(8,128)(2,1)S(1)}, bf16[96,1536]{1,0:T(8,128)(2,1)S(1)}, u32[]{:S(2)}, u32[]{:S(2)}) collective-permute-start(bf16[96,1536]{1,0:T(8,128)(2,1)S(1)} %slice.191), channel_id=1, source_target_pairs={{0,2},{2,0},{4,6},{6,4},{8,10},{10,8},{12,14},{14,12},{16,18},{18,... | collective-permute-start | bytes 884744 | tf_op jit(solution)/shard_map/ppermute | solution.py:68
  174.9 39.0 %collective-permute-start.29 = (bf16[384,1536]{1,0:T(8,128)(2,1)}, bf16[384,1536]{1,0:T(8,128)(2,1)S(1)}, u32[]{:S(2)}, u32[]{:S(2)}) collective-permute-start(bf16[384,1536]{1,0:T(8,128)(2,1)} %get-tuple-element.111), channel_id=1, source_target_pairs={{0,2},{2,0},{4,6},{6,4},{8,10},{10,8},{12,14},{14,12},{16,18},{18,... | collective-permute-start | bytes 3538952 | tf_op jit(solution)/shard_map/ppermute | solution.py:68
  181.3 32.5 %collective-permute-start.28 = (bf16[384,1536]{1,0:T(8,128)(2,1)}, bf16[384,1536]{1,0:T(8,128)(2,1)}, u32[]{:S(2)}, u32[]{:S(2)}) collective-permute-start(bf16[384,1536]{1,0:T(8,128)(2,1)} %get-tuple-element.106), channel_id=1, source_target_pairs={{0,4},{2,6},{4,0},{6,2},{8,12},{10,14},{12,8},{14,10},{16,20},{18,... | collective-permute-start | bytes 3538952 | tf_op jit(solution)/shard_map/ppermute | solution.py:68
  216.3 16.7 %collective-permute-start.33 = (bf16[192,1536]{1,0:T(8,128)(2,1)}, bf16[192,1536]{1,0:T(8,128)(2,1)}, u32[]{:S(2)}, u32[]{:S(2)}) collective-permute-start(bf16[192,1536]{1,0:T(8,128)(2,1)} %get-tuple-element.153), channel_id=1, source_target_pairs={{0,4},{2,6},{4,0},{6,2},{8,12},{10,14},{12,8},{14,10},{16,20},{18,... | collective-permute-start | bytes 1769480 | tf_op jit(solution)/shard_map/ppermute | solution.py:68
  217.2 17.0 %collective-permute-start.34 = (bf16[192,1536]{1,0:T(8,128)(2,1)}, bf16[192,1536]{1,0:T(8,128)(2,1)}, u32[]{:S(2)}, u32[]{:S(2)}) collective-permute-start(bf16[192,1536]{1,0:T(8,128)(2,1)} %get-tuple-element.154), channel_id=1, source_target_pairs={{0,2},{2,0},{4,6},{6,4},{8,10},{10,8},{12,14},{14,12},{16,18},{18,... | collective-permute-start | bytes 1769480 | tf_op jit(solution)/shard_map/ppermute | solution.py:68
  225.4 17.0 %collective-permute-start.30 = (bf16[512,768]{1,0:T(8,128)(2,1)}, bf16[512,768]{1,0:T(8,128)(2,1)}, u32[]{:S(2)}, u32[]{:S(2)}) collective-permute-start(bf16[512,768]{1,0:T(8,128)(2,1)} %get-tuple-element.117), channel_id=1, source_target_pairs={{0,1},{1,0},{2,3},{3,2},{4,5},{5,4},{6,7},{7,6},{8,9},{9,8},{10,11... | collective-permute-start | bytes 2359304 | tf_op jit(solution)/shard_map/ppermute | solution.py:26
  232.4 20.3 %collective-permute-start.31 = (bf16[384,768]{1,0:T(8,128)(2,1)}, bf16[384,768]{1,0:T(8,128)(2,1)}, u32[]{:S(2)}, u32[]{:S(2)}) collective-permute-start(bf16[384,768]{1,0:T(8,128)(2,1)} %get-tuple-element.124), channel_id=1, source_target_pairs={{0,2},{2,0},{4,6},{6,4},{8,10},{10,8},{12,14},{14,12},{16,18},{18,... | collective-permute-start | bytes 1769480 | tf_op jit(solution)/shard_map/ppermute | solution.py:68
  241.1 35.6 %collective-permute-start.35 = (bf16[384,768]{1,0:T(8,128)(2,1)}, bf16[384,768]{1,0:T(8,128)(2,1)}, u32[]{:S(2)}, u32[]{:S(2)}) collective-permute-start(bf16[384,768]{1,0:T(8,128)(2,1)} %get-tuple-element.129), channel_id=1, source_target_pairs={{0,4},{2,6},{4,0},{6,2},{8,12},{10,14},{12,8},{14,10},{16,20},{18,... | collective-permute-start | bytes 1769480 | tf_op jit(solution)/shard_map/ppermute | solution.py:68
  247.3 18.2 %collective-permute-start.42 = (bf16[48,3072]{1,0:T(8,128)(2,1)}, bf16[48,3072]{1,0:T(8,128)(2,1)S(1)}, u32[]{:S(2)}, u32[]{:S(2)}) collective-permute-start(bf16[48,3072]{1,0:T(8,128)(2,1)} %get-tuple-element.140), channel_id=1, source_target_pairs={{0,24},{2,26},{4,28},{6,30},{8,0},{10,2},{12,4},{14,6},{16,8},{18,... | collective-permute-start | bytes 884744 | tf_op jit(solution)/shard_map/ppermute | solution.py:68
  251.2 24.4 %collective-permute-start.41 = (bf16[48,3072]{1,0:T(8,128)(2,1)}, bf16[48,3072]{1,0:T(8,128)(2,1)}, u32[]{:S(2)}, u32[]{:S(2)}) collective-permute-start(bf16[48,3072]{1,0:T(8,128)(2,1)} %get-tuple-element.141), channel_id=1, source_target_pairs={{0,16},{2,18},{4,20},{6,22},{8,24},{10,26},{12,28},{14,30},{16,0},... | collective-permute-start | bytes 884744 | tf_op jit(solution)/shard_map/ppermute | solution.py:68
  256.8 24.7 %collective-permute-start.32 = (bf16[192,768]{1,0:T(8,128)(2,1)S(1)}, bf16[192,768]{1,0:T(8,128)(2,1)S(1)}, u32[]{:S(2)}, u32[]{:S(2)}) collective-permute-start(bf16[192,768]{1,0:T(8,128)(2,1)S(1)} %add_convert_fusion.3), channel_id=1, source_target_pairs={{0,4},{2,6},{4,0},{6,2},{8,12},{10,14},{12,8},{14,10},{16,20},{18,... | collective-permute-start | bytes 884744 | tf_op jit(solution)/shard_map/ppermute | solution.py:68
  259.3 17.4 %collective-permute-start.45 = (f32[84,128]{1,0:T(8,128)S(1)}, f32[84,128]{1,0:T(8,128)S(1)}, u32[]{:S(2)}, u32[]{:S(2)}) collective-permute-start(f32[84,128]{1,0:T(8,128)S(1)} %fusion.10), channel_id=1, source_target_pairs={{0,4},{2,6},{4,0},{6,2},{8,12},{10,14},{12,8},{14,10},{16,20},{18,... | collective-permute-start | bytes 129032 | tf_op jit(solution)/shard_map/ppermute | solution.py:68
  (54 other events, 495.3 us)

commit v3 on v2

--- a/solution.py
+++ b/solution.py
@@ -99,12 +99,11 @@
             ]
         return places
 
-    def along_lines(self, values):
+    def along_lines(self, values, meanwhile=lambda got: got):
         block = values
         for factor, stride in self.lines:
-            block = jnp.concatenate(
-                [block] + [self.shift(block, factor, stride, step) for step in range(1, factor)], 0
-            )
+            got = [self.shift(block, factor, stride, step) for step in range(1, factor)]
+            block = jnp.concatenate([block] + meanwhile(got), 0)
         return block
 
     def to_sides(self, block):
@@ -132,23 +131,24 @@
         own = widen(keep[:half]) + widen(got[:half])
         return own, (widen(keep[half:]) + widen(got[half:])).astype(bf16)
 
-    def sum_lines(self, total):
-        for factor, stride in self.lines:
-            rows = total.shape[0] // factor
-            rounded = total.astype(bf16)
-            running = total[:rows]
-            for step in range(1, factor):
-                got = self.shift(rounded[step * rows : (step + 1) * rows], factor, stride, step)
-                running = running + widen(got)
-            total = running
+    def sum_lines(self, own, seconds, meanwhile):
+        parts = square_end(own, seconds, self.lines[0][0])
+        for at, (factor, stride) in enumerate(self.lines):
+            got = [self.shift(parts[step], factor, stride, step) for step in range(1, factor)]
+            total = parts[0]
+            for piece in meanwhile(got, parts):
+                total = total + widen(piece)
+            if at + 1 < len(self.lines):
+                pieces = jnp.split(total, self.lines[at + 1][0])
+                parts = [pieces[0]] + [piece.astype(bf16) for piece in pieces[1:]]
         return total
 
-    def all_sum(self, values):
-        stride = 1
+    def sum_strides(self):
+        stride, strides = 1, []
         while stride < self.size:
-            values = values + self.flip(values, stride)
+            strides.append(stride)
             stride *= 2
-        return values
+        return strides
 
 
 def whole(shape):
@@ -257,6 +257,71 @@
     ref[row : row + 1, :] = jnp.where(first, total, ref[row : row + 1, :] + total)
 
 
+def square_end(own, seconds, factor):
+    rows = own[0].shape[0] // factor
+    width = sum(each.shape[1] for each in own)
+
+    def body(*refs):
+        ins, outs = refs[: 2 * len(own)], refs[2 * len(own) :]
+        for at, out in enumerate(outs):
+            left = 0
+            for mine, theirs in zip(ins[: len(own)], ins[len(own) :]):
+                span = slice(at * rows, (at + 1) * rows)
+                total = mine[span, :] + widen(theirs[span, :])
+                out[:, left : left + mine.shape[1]] = total.astype(out.dtype)
+                left += mine.shape[1]
+
+    return pl.pallas_call(
+        body,
+        out_shape=[shape_of((rows, width), f32)] + [shape_of((rows, width), bf16)] * (factor - 1),
+        in_specs=[pl.BlockSpec(memory_space=pltpu.VMEM)] * (2 * len(own)),
+        out_specs=[pl.BlockSpec(memory_space=pltpu.VMEM)] * factor,
+        name="square_end",
+    )(*own, *seconds)
+
+
+def pack(first_sums, first_other, model_sums, grad_sums, bias_sums, head_sums, hidden_sums):
+    def body(first, other, model, grad, bias, head, hidden, out):
+        at = 0
+        rows = [first[0:1, :] + other[0:1, :], first[1:2, :] + other[1:2, :]]
+        rows += [model[0:1, :], model[1:2, :], model[2:3, :], grad[0:1, :]]
+        rows += [bias[0:1, :], bias[1:2, :], head[0:1, :], head[1:2, :]]
+        rows += [hidden[0:1, :], hidden[1:2, :], hidden[2:3, :]]
+        for row in rows:
+            for left in range(0, row.shape[1], LANES):
+                out[at : at + 1, :] = row[:, left : left + LANES]
+                at += 1
+
+    parts = (first_sums, first_other, model_sums, grad_sums, bias_sums, head_sums, hidden_sums)
+    count = 6 * model_sums.shape[1] + 4 * head_sums.shape[1] + 3 * hidden_sums.shape[1]
+    return pl.pallas_call(
+        body,
+        out_shape=shape_of((count // LANES, LANES), f32),
+        in_specs=[pl.BlockSpec(memory_space=pltpu.VMEM)] * len(parts),
+        out_specs=pl.BlockSpec(memory_space=pltpu.VMEM),
+        name="pack",
+    )(*parts)
+
+
+def unpack(one, two, shapes):
+    def body(one_ref, two_ref, *outs):
+        total = one_ref[...] + two_ref[...]
+        at = 0
+        for out in outs:
+            for row in range(out.shape[0]):
+                for left in range(0, out.shape[1], LANES):
+                    out[row : row + 1, left : left + LANES] = total[at : at + 1, :]
+                    at += 1
+
+    return pl.pallas_call(
+        body,
+        out_shape=[shape_of(shape, f32) for shape in shapes],
+        in_specs=[pl.BlockSpec(memory_space=pltpu.VMEM)] * 2,
+        out_specs=[pl.BlockSpec(memory_space=pltpu.VMEM)] * len(shapes),
+        name="unpack",
+    )(one, two)
+
+
 def prepare(core, tokens, tokens_other, cotangent, cotangent_other, model_vectors):
     rows, features = tokens.shape
     share = TILES // 2
@@ -357,9 +422,8 @@
     )(order, *pieces, attend_in, bias)
 
 
-def attend_forward(prefix, queries, keys, values):
-    length, width = queries.shape
-    pairs = width // PAIR
+def attend_forward(pair, prefix, queries, keys, values):
+    length = queries.shape[0]
     tile = length // 2
 
     def body(prefix_ref, query_ref, key_ref, value_ref, out_ref, log_ref, turned):
@@ -388,28 +452,27 @@
                     preferred_element_type=f32,
                 )
                 parts.append(mixed / total)
-                log_ref[0, head : head + 1, columns] = top * (SCALE * LOG2E) + jnp.log2(total)
+                log_ref[head : head + 1, columns] = top * (SCALE * LOG2E) + jnp.log2(total)
             out_ref[columns, :] = jnp.concatenate(parts, 0).T
 
-    block = pl.BlockSpec((length, PAIR), lambda i: (0, i))
-    return pl.pallas_call(
-        body,
-        grid=(pairs,),
-        out_shape=[shape_of((length, width), f32), shape_of((pairs, 8, length), f32)],
+    block = pl.BlockSpec((length, PAIR), lambda i: (0, pair))
+    return pl.pallas_call(
+        body,
+        grid=(1,),
+        out_shape=[shape_of((length, PAIR), f32), shape_of((8, length), f32)],
         in_specs=[SMEM, block, block, block],
-        out_specs=[block, pl.BlockSpec((1, 8, length), lambda i: (i, 0, 0))],
+        out_specs=[whole((length, PAIR)), whole((8, length))],
         scratch_shapes=[pltpu.VMEM((PAIR, length), bf16)],
         compiler_params=PARAMS,
         cost_estimate=cost(
-            16 * length * length * width, 10 * length * width, 2 * pairs * length * length
+            16 * length * length * PAIR, 10 * length * PAIR, 2 * length * length
         ),
         name="attend_forward",
     )(prefix, queries, keys, values)
 
 
-def attend_backward(prefix, queries, keys, values, attended, grads, logs):
-    length, width = queries.shape
-    pairs = width // PAIR
+def attend_backward(pair, prefix, queries, keys, values, attended, grads, logs):
+    length = queries.shape[0]
     tile = length // 4
 
     def body(
@@ -447,7 +510,7 @@
                 level = jnp.sum(crossed[span, :], axis=0, keepdims=True)
                 scores = lax.dot_general(key_rows, mine, TRANSPOSED, preferred_element_type=f32)
                 raised = jnp.exp2(
-                    scores * (SCALE * LOG2E) - log_ref[0, head : head + 1, columns]
+                    scores * (SCALE * LOG2E) - log_ref[head : head + 1, columns]
                 )
                 probs = jnp.where(row_at < limit, raised, 0.0)
                 prob_grad = lax.dot_general(
@@ -467,13 +530,13 @@
         key_out[...] = (key_total[...] * SCALE).astype(bf16)
         value_out[...] = value_total[...].astype(bf16)
 
-    block = pl.BlockSpec((length, PAIR), lambda i: (0, i))
-    return pl.pallas_call(
-        body,
-        grid=(pairs,),
-        out_shape=[shape_of((length, width), bf16)] * 3,
-        in_specs=[SMEM] + [block] * 5 + [pl.BlockSpec((1, 8, length), lambda i: (i, 0, 0))],
-        out_specs=[block] * 3,
+    block = pl.BlockSpec((length, PAIR), lambda i: (0, pair))
+    return pl.pallas_call(
+        body,
+        grid=(1,),
+        out_shape=[shape_of((length, PAIR), bf16)] * 3,
+        in_specs=[SMEM] + [block] * 3 + [whole((length, PAIR)), block, whole((8, length))],
+        out_specs=[whole((length, PAIR))] * 3,
         scratch_shapes=[
             pltpu.VMEM((PAIR, length), bf16),
             pltpu.VMEM((length, PAIR), f32),
@@ -481,26 +544,28 @@
         ],
         compiler_params=PARAMS,
         cost_estimate=cost(
-            40 * length * length * width, 18 * length * width, 2 * pairs * length * length
+            40 * length * length * PAIR, 18 * length * PAIR, 2 * length * length
         ),
         name="attend_backward",
     )(prefix, queries, keys, values, attended, grads, logs)
 
 
 def mix(order, pieces, attended, head_vectors, widths):
-    length, width = attended.shape
+    length = attended[0].shape[0]
+    width = PAIR * len(attended)
     count = order.shape[0]
     features = pieces[0].shape[0] // (count // 4) * count
 
     def body(order_ref, *refs):
-        pieces_in, (rows, vectors, weight, second, product, side) = refs[:5], refs[5:]
+        pieces_in, rows, (vectors, weight, second, product, side) = refs[:5], refs[5:-5], refs[-5:]
 
         @pl.when(pl.program_id(0) == 0)
         def _():
             place_rows(order_ref, pieces_in, (weight, second), count)
             side[...] = side_rows(vectors[2:3, :], vectors[3:4, :], weight[...])
 
-        out, stats = centered_product(rows[...], vectors[2:3, :], weight[...])
+        out, stats = centered_product(
+            jnp.concatenate([part[...] for part in rows], 1), vectors[2:3, :], weight[...])
         product[:, :features] = out
         product[:, features:] = stats
 
@@ -511,7 +576,8 @@
         + [shape_of((length, features + LANES), bf16), shape_of((8, features), f32)],
         in_specs=[SMEM]
         + [whole(piece.shape) for piece in pieces]
-        + [rows_of(attended), whole(head_vectors.shape)],
+        + [rows_of(part) for part in attended]
+        + [whole(head_vectors.shape)],
         out_specs=[whole((features, each)) for each in widths]
         + [
             pl.BlockSpec((length // TILES, features + LANES), lambda i: (i, 0)),
@@ -522,7 +588,7 @@
             2 * length * features * width, 4 * features * sum(widths) + 6 * length * features
         ),
         name="mix",
-    )(order, *pieces, attended, head_vectors)
+    )(order, *pieces, *attended, head_vectors)
 
 
 def feed_up(product, product_other, side, side_other, inputs, weight, model_vectors, hidden_vectors):
@@ -752,13 +818,13 @@
     head_vectors,
 ):
     length, features = middle.shape
-    width = attended.shape[1]
+    width = PAIR * len(attended)
     joined = 2 * width
 
     def body(
-        back_one, back_two, one, two, side_one, side_two, mid, grad, attended_ref, weight_ref,
-        model, head, middle_out, turned, mixed_out, attended_out, sums, head_sums,
+        back_one, back_two, one, two, side_one, side_two, mid, grad, *refs
     ):
+        attended_refs, (weight_ref, model, head, middle_out, turned, mixed_out, attended_out, sums, head_sums) = refs[:-9], refs[-9:]
         feed_grad = widen(back_one[...]) + widen(back_two[...])
         normal, inverse = normal_of(mid[...])
         accumulate(sums, 1, feed_grad * normal)
@@ -776,7 +842,8 @@
         mean_scaled = jnp.sum(rows * straight, axis=-1, keepdims=True) / joined
         mean_crossed = jnp.sum(rows * branch, axis=-1, keepdims=True) / joined
         mixed_grad = jnp.dot(branch_grad, weight_ref[...], preferred_element_type=f32)
-        normal_two = (attended_ref[...] - center) * inverse_two
+        attended_rows = jnp.concatenate([part[...] for part in attended_refs], 1)
+        normal_two = (attended_rows - center) * inverse_two
         mixed_out[...] = (normal_two * head[2:3, :] + head[3:4, :]).astype(bf16)
         accumulate(head_sums, 0, mixed_grad * normal_two)
         accumulate(head_sums, 1, mixed_grad)
@@ -805,7 +872,7 @@
             whole(side.shape),
             rows_of(middle),
             rows_of(cotangent),
-            rows_of(attended),
+            *[rows_of(part) for part in attended],
             whole(weight.shape),
             whole(model_vectors.shape),
             whole(head_vectors.shape),
@@ -813,8 +880,8 @@
         out_specs=[
             rows_of(middle),
             pl.BlockSpec((features, tile), lambda i: (0, i)),
-            rows_of(attended),
-            rows_of(attended),
+            pl.BlockSpec((tile, width), lambda i: (i, 0)),
+            pl.BlockSpec((tile, width), lambda i: (i, 0)),
             whole((8, features)),
             whole((8, width)),
         ],
@@ -832,30 +899,33 @@
         side_other,
         middle,
         cotangent,
-        attended,
+        *attended,
         weight,
         model_vectors,
         head_vectors,
     )
 
 
-def project_back(core, parts, weight):
-    length, third = parts[0].shape
-    features = weight.shape[0]
+def project_back(core, groups, weight):
+    length = groups[0][0].shape[0]
+    parts = [part for group in groups for part in group]
+    features, width = weight.shape
+    third = width // 3
     tile = length // TILES
     share = TILES // 2
-
-    def body(core_ref, one, two, three, weight_ref, send, keep, sums):
-        total = jnp.zeros((tile, features), f32)
-        for at, part in enumerate((one, two, three)):
-            total += lax.dot_general(
-                part[...],
-                weight_ref[:, at * third : (at + 1) * third],
-                TRANSPOSED,
-                preferred_element_type=f32,
-            )
-        accumulate(sums, 0, widen(one[...]))
-        accumulate(sums, 1, widen(three[...]))
+    each = len(groups[0])
+
+    def body(core_ref, *refs):
+        weight_ref, send, keep, sums = refs[-4:]
+        grads = [
+            jnp.concatenate([ref[...] for ref in refs[at * each : (at + 1) * each]], 1)
+            for at in range(3)
+        ]
+        total = lax.dot_general(
+            jnp.concatenate(grads, 1), weight_ref[...], TRANSPOSED, preferred_element_type=f32
+        )
+        accumulate(sums, 0, widen(grads[0]))
+        accumulate(sums, 1, widen(grads[2]))
 
         @pl.when(pl.program_id(0) < share)
         def _():
@@ -865,13 +935,13 @@
         def _():
             keep[...] = total
 
-    moved = pl.BlockSpec((tile, third), lambda i, core: ((i + (1 - core[0]) * share) % TILES, 0))
+    moved = pl.BlockSpec((tile, PAIR), lambda i, core: ((i + (1 - core[0]) * share) % TILES, 0))
     return pl.pallas_call(
         body,
         grid_spec=pltpu.PrefetchScalarGridSpec(
             num_scalar_prefetch=1,
             grid=(TILES,),
-            in_specs=[moved, moved, moved, pl.BlockSpec(weight.shape, lambda i, core: (0, 0))],
+            in_specs=[moved] * len(parts) + [pl.BlockSpec(weight.shape, lambda i, core: (0, 0))],
             out_specs=[
                 pl.BlockSpec((tile, features), lambda i, core: (jnp.minimum(i, share - 1), 0)),
                 pl.BlockSpec((tile, features), lambda i, core: (jnp.maximum(i - share, 0), 0)),
@@ -885,7 +955,7 @@
         ],
         compiler_params=PARAMS,
         cost_estimate=cost(
-            6 * length * features * third, 6 * features * third + 6 * length * (features + third)
+            2 * length * features * width, 2 * features * width + 6 * length * (features + third)
         ),
         name="project_back",
     )(core, *parts, weight)
@@ -927,18 +997,16 @@
 
 def weight_grad(order, pairs, tile):
     features, tokens = pairs[0][0].shape
-    width = sum(right.shape[1] for _, right in pairs)
+    lefts, groups = [], []
+    for left, group in pairs:
+        if not any(left is known for known in lefts):
+            lefts.append(left)
+        groups.append(([left is known for known in lefts].index(True), len(group)))
+    rights = [right for _, group in pairs for right in group]
+    width = sum(right.shape[1] for right in rights)
     count = order.shape[0]
     shard = features // count
-    lefts = []
-    steps = []
-    for left, right in pairs:
-        if not any(left is known for known in lefts):
-            lefts.append(left)
-        at = [left is known for known in lefts].index(True)
-        steps += [(at, len(steps), 0)] if right.shape[1] == tile else []
-    rights = [right for _, right in pairs]
-    single = len(pairs) == 1
+    single = len(rights) == 1
 
     def body(order_ref, *refs):
         left_refs, right_refs = refs[: len(lefts)], refs[len(lefts) : -3]
@@ -946,13 +1014,19 @@
         if single:
             total[...] = jnp.dot(left_refs[0][...], right_refs[0][...], preferred_element_type=f32)
         else:
-            for at, step, _ in steps:
+            first = 0
+            for step, (at, size) in enumerate(groups):
 
                 @pl.when(pl.program_id(0) == step)
-                def _(at=at, step=step):
+                def _(at=at, first=first, size=size):
+                    right = [ref[...] for ref in right_refs[first : first + size]]
                     total[...] = jnp.dot(
-                        left_refs[at][...], right_refs[step][...], preferred_element_type=f32
+                        left_refs[at][...],
+                        jnp.concatenate(right, 1) if size > 1 else right[0],
+                        preferred_element_type=f32,
                     )
+
+                first += size
 
         for block in range(count):
             place = pl.multiple_of(order_ref[block] * shard, 16)
@@ -1003,30 +1077,40 @@
     features = tokens.shape[1]
 
     bias = jnp.concatenate([head_vectors[0], jnp.zeros_like(head_vectors[0]), head_vectors[1]])
+    pair_count = half // PAIR
+    tokens_other, cotangent_other = flip_partner(tokens), flip_partner(cotangent)
     first_block = ring.along_lines(join(query_weight, key_weight, value_weight))
-    second_block = ring.along_lines(after(join(out_weight, up_weight), first_block))
-    third_block = ring.along_lines(after(down_weight, second_block))
     first_sides = ring.to_sides(first_block)
+    second = after(join(out_weight, up_weight), first_block)
+    whole_rows = after((tokens, tokens_other, cotangent, cotangent_other), first_block)
+    inputs, grads, attend_in, attend_turned, grads_turned, grad_sums = prepare(
+        core, *whole_rows, model_vectors
+    )
+    second_block = ring.along_lines(second, lambda got: after(got, attend_in))
+    first_sides = after(first_sides, attend_in)
     first_pieces = (first_block, *first_sides, *ring.to_corner(*first_sides))
 
-    inputs, grads, attend_in, attend_turned, grads_turned, grad_sums = prepare(
-        core, tokens, flip_partner(tokens), cotangent, flip_partner(cotangent), model_vectors
-    )
-
-    second_block = after(second_block, first_pieces)
-    second_sides = ring.to_sides(second_block)
+    second_sides = ring.to_sides(after(second_block, first_pieces))
+    third = after(down_weight, second_block)
     first_weight, queries, keys, values = project(order, first_pieces, attend_in, bias[None])
-    attended, logs = attend_forward(prefix, queries, keys, values)
+    states = (prefix, queries, keys, values)
+    attended, logs = zip(*[attend_forward(pair, *states) for pair in range(pair_count - 1)])
+    third_block = ring.along_lines(third, lambda got: after(got, attended))
+    second_sides = after(second_sides, attended)
     second_pieces = (second_block, *second_sides, *ring.to_corner(*second_sides))
-    third_block = after(third_block, second_sides)
-    third_sides = ring.to_sides(third_block)
+    third_sides = ring.to_sides(after(third_block, second_sides))
+    last, last_logs = attend_forward(pair_count - 1, *after(states, second_sides, third_block))
+    attended, logs = (*attended, last), (*logs, last_logs)
+    second_pieces = (second_block, *second_sides, *after(second_pieces[3:], last))
     out_full, up_full, mixed, mixed_side = mix(
         order, second_pieces, attended, head_vectors, (half, full)
     )
     mixed_other, mixed_side_other = flip_partner(mixed), flip_partner(mixed_side)
+    third_sides = after(third_sides, mixed)
+    third_corner = ring.to_corner(*third_sides)
     middle, feed_turned, kept, slope = feed_up(
-        after(mixed, third_sides),
-        mixed_other,
+        mixed,
+        after(mixed_other, third_sides),
         mixed_side,
         mixed_side_other,
         inputs,
@@ -1034,7 +1118,7 @@
         model_vectors,
         hidden_vectors,
     )
-    third_pieces = (third_block, *third_sides, *ring.to_corner(*third_sides))
+    third_pieces = (third_block, *third_sides, *after(third_corner, kept))
     down_full, fed, fed_side = feed_down(order, third_pieces, kept, hidden_vectors)
     fed_other, fed_side_other = flip_partner(fed), flip_partner(fed_side)
     output, feed_mid, before_grad, passed, hidden_sums = feed_back(
@@ -1053,8 +1137,8 @@
         hidden_vectors,
     )
     passed_other = flip_partner(passed)
-    down_keep, down_send = weight_grad(far, [(grads_turned, feed_mid)], full // 2)
-    up_keep, up_send = weight_grad(near, [(feed_turned, before_grad)], full // 2)
+    down_keep, down_send = weight_grad(far, [(grads_turned, [feed_mid])], full // 2)
+    up_keep, up_send = weight_grad(near, [(feed_turned, [before_grad])], full // 2)
     down_got, up_got = ring.flip(down_send, 2), ring.flip(up_send, 1)
 
     middle_grad, branch_turned, mixed_in, attended_grad, model_sums, head_sums = mix_back(
@@ -1071,52 +1155,67 @@
         model_vectors,
         head_vectors,
     )
-    query_grad, key_grad, value_grad = attend_backward(
-        prefix, queries, keys, values, attended, attended_grad, logs
-    )
-    down_own, down_away = ring.sum_first(down_keep, after(down_got, query_grad))
-    up_own, up_away = ring.sum_first(up_keep, after(up_got, query_grad))
-    down_second, up_second = ring.flip(down_away, 1), ring.flip(up_away, 2)
-    parts = after((query_grad, key_grad, value_grad), down_away, up_away)
-    send, keep, bias_sums = project_back(core, parts, first_weight)
+    def pair_back(pair, grad):
+        return attend_backward(pair, *states, attended[pair], grad, logs[pair])
+
+    pair_grads = [pair_back(pair, attended_grad) for pair in range(pair_count - 1)]
+    down_own, down_away = ring.sum_first(down_keep, after(down_got, pair_grads))
+    up_own, up_away = ring.sum_first(up_keep, after(up_got, pair_grads))
+    up_second, down_second = ring.flip(up_away, 2), ring.flip(down_away, 1)
+    pair_grads.append(pair_back(pair_count - 1, after(attended_grad, down_away, up_away)))
+    query_grad, key_grad, value_grad = ([pair[at] for pair in pair_grads] for at in range(3))
+    wide_seconds = after((up_second, down_second), pair_grads)
+
+    progress = {}
+
+    def during_wide(got, parts):
+        tied_query, tied_value = after((query_grad, value_grad), parts)
+        query_keep, query_send = weight_grad(
+            near, [(attend_turned, tied_query), (attend_turned, tied_value)], half
+        )
+        query_got = ring.flip(query_send, 1)
+        key_keep, key_send = weight_grad(
+            far, [(attend_turned, after(key_grad, query_send)), (branch_turned, [mixed_in])], half
+        )
+        key_got = ring.flip(key_send, 2)
+        sums = project_back(
+            core, after((query_grad, key_grad, value_grad), key_send), first_weight
+        )
+        progress["narrow"] = (query_keep, query_got, key_keep, key_got)
+        progress["project"] = sums
+        return after(got, sums)
+
+    if len(ring.lines) > 1:
+        during_wide([], [])
+        wide_grads = ring.sum_lines((up_own, down_own), wide_seconds, lambda got, parts: got)
+    else:
+        wide_grads = ring.sum_lines((up_own, down_own), wide_seconds, during_wide)
+    up_grad, down_grad = wide_grads[:, :full], wide_grads[:, full:]
+    query_keep, query_got, key_keep, key_got = progress["narrow"]
+    send, keep, bias_sums = progress["project"]
     received = flip_partner(send)
-    query_keep, query_send = weight_grad(
-        near, [(attend_turned, query_grad), (attend_turned, after(value_grad, send))], half
-    )
-    wide = jnp.concatenate(
-        [up_own + widen(up_second), down_own + widen(down_second)], axis=1
-    )
-    wide_grads = ring.sum_lines(after(wide, query_send))
-    up_grad, down_grad = wide_grads[:, :full], wide_grads[:, full:]
-    key_keep, key_send = weight_grad(
-        far, [(attend_turned, after(key_grad, wide)), (branch_turned, mixed_in)], half
-    )
-    query_own, query_away = ring.sum_first(query_keep, ring.flip(query_send, 1))
-    key_own, key_away = ring.sum_first(key_keep, ring.flip(key_send, 2))
-    narrow = jnp.concatenate(
-        [
-            query_own + widen(ring.flip(query_away, 2)),
-            key_own + widen(ring.flip(key_away, 1)),
-        ],
-        axis=1,
-    )
-    narrow = ring.sum_lines(narrow)
+    query_own, query_away = ring.sum_first(query_keep, after(query_got, send))
+    key_own, key_away = ring.sum_first(key_keep, after(key_got, send))
+    narrow_seconds = ring.flip(query_away, 2), ring.flip(key_away, 1)
+    input_grad, first_sums = input_back(
+        core, received, after(keep, query_away, key_away), middle_grad, tokens, model_vectors
+    )
+    narrow_seconds = after(narrow_seconds, input_grad)
+    packed = pack(
+        first_sums, flip_partner(first_sums), model_sums, grad_sums, bias_sums, head_sums, hidden_sums
+    )
+    strides = ring.sum_strides()
+    for stride in strides[:-1]:
+        packed = packed + ring.flip(packed, stride)
+    model_sum, head_sum, hidden_sum = unpack(
+        packed, ring.flip(packed, strides[-1]), ((6, features), (4, half), (3, full))
+    )
+    narrow = ring.sum_lines(
+        (query_own, key_own), after(narrow_seconds, wide_grads), lambda got, parts: got
+    )
     query_weight_grad, value_weight_grad, key_weight_grad, out_grad = (
         narrow[:, at * half : (at + 1) * half] for at in range(4)
     )
-    input_grad, first_sums = input_back(core, received, keep, middle_grad, tokens, model_vectors)
-    first_sums = first_sums + flip_partner(first_sums)
-
-    model_grads = jnp.concatenate([first_sums[:2], model_sums[:3], grad_sums[:1]], 0)
-    head_grads = jnp.concatenate([bias_sums[:2], head_sums[:2]], 0)
-    hidden_grads = hidden_sums[:3]
-    sums = ring.all_sum(
-        jnp.concatenate([g.reshape(-1, LANES) for g in (model_grads, head_grads, hidden_grads)], 0)
-    )
-    rows_one, rows_two = model_grads.size // LANES, head_grads.size // LANES
-    model_sum = sums[:rows_one].reshape(model_grads.shape)
-    head_sum = sums[rows_one : rows_one + rows_two].reshape(head_grads.shape)
-    hidden_sum = sums[rows_one + rows_two :].reshape(hidden_grads.shape)
     return (
         output,
         input_grad,

time: 305 us -> 297 us (0.974)
  waiting for transfers between devices: 81.5 us -> 54 us
  Pallas kernels: 132 us -> 150 us
  starting transfers between devices: 50.3 us -> 60.1 us
  other arithmetic: 14.2 us -> 7.1 us
    ppermute x39, waiting for transfers between devices: 80.5 us -> 50.4 us  [shift(): return lax.ppermute(values, 'dp', pairs)]
    pallas_call x2 -> x10, Pallas kernels: 35 us -> 51.4 us  [the longest x3 24.3 us: attend_backward(): pl.pallas_call(body, grid=(1,), out_shape=[shape_of((length, PAIR), bf16)...]
    ppermute x39, starting transfers between devices: 49 us -> 58.7 us  [shift(): return lax.ppermute(values, 'dp', pairs)]
    slice x9 -> x0, local copies, waits for them, and re-layouts: 5.11 us -> none  [the longest x2 1.42 us: on_device(): head_grads = jnp.concatenate([bias_sums[:2], head_sums[:2]], 0)]
    convert_element_type x5 -> x0, other arithmetic: 4.79 us -> none  [the longest x3 4.57 us: sum_first(): return (own, (widen(keep[half:]) + widen(got[half:])).astype(bf16))]
    unnamed x63 -> x76, local copies, waits for them, and re-layouts: 10.1 us -> 14 us
    add x11 -> x8, other arithmetic: 7.54 us -> 6.16 us  [the longest x3 4.01 us: sum_first(): own = widen(keep[:half]) + widen(got[:half])]
  transfers between devices with their start and end apart: 48 -> 48, of which waited for: 18 -> 15; matrix products, arithmetic and copies ran while one was open for 8% -> 6% of each run, Pallas kernels for 34% -> 37%
where the time goes in v3:
time: 297 us; the launch traced here: 293 us
  Pallas kernels  150 us (51%)
  starting transfers between devices  60.1 us (20%)
  waiting for transfers between devices  54 us (18%)
  local copies, waits for them, and re-layouts  20.3 us (7%)
  other arithmetic  7.1 us (2%)
    ppermute x39, starting transfers between devices, shift(): return lax.ppermute(values, 'dp', pairs)  58.7 us
    ppermute x39, waiting for transfers between devices, shift(): return lax.ppermute(values, 'dp', pairs)  50.4 us
    pallas_call x3, Pallas kernels, attend_backward(): pl.pallas_call(body, grid=(1,), out_shape=[shape_of((length, PAIR), bf16)...  24.3 us
    pallas_call x4, Pallas kernels, weight_grad(): pl.pallas_call(body, grid=(width // tile,), out_shape=[shape_of((features...  22.1 us
    pallas_call x3, Pallas kernels, attend_forward(): pl.pallas_call(body, grid=(1,), out_shape=[shape_of((length, PAIR), f32),...  18.8 us
    unnamed x76, local copies, waits for them, and re-layouts  14 us
    pallas_call x1, Pallas kernels, feed_back(): pl.pallas_call(body, grid_spec=pltpu.PrefetchScalarGridSpec(num_scalar_pr...  14 us
    pallas_call x1, Pallas kernels, feed_up(): pl.pallas_call(body, grid=(TILES,), out_shape=[shape_of((length, features...  10.6 us
  transfers between devices with their start and end apart: 48, of which 15 were waited for; matrix products, arithmetic and copies ran while one was open for 6% of the time, Pallas kernels for 37%

profile of v3, /device:TPU:0, one launch (start us, length us, event | category | flops | bytes accessed | tf_op | source)
XLA Modules:
  0.0 293.2 jit_solution(8122642717483144619)
XLA Ops:
  2.7 5.0 %collective-permute-start.2 = (bf16[48,1152]{1,0:T(8,128)(2,1)}, bf16[48,1152]{1,0:T(8,128)(2,1)S(1)}, u32[]{:S(2)}, u32[]{:S(2)}) collective-permute-start(bf16[48,1152]{1,0:T(8,128)(2,1)} %join.3), channel_id=1, source_target_pairs={{0,24},{2,26},{4,28},{6,30},{8,0},{10,2},{12,4},{14,6},{16,8},{18,... | collective-permute-start | bytes 331784 | tf_op jit(solution)/shard_map/ppermute | solution.py:68
  13.0 5.0 %collective-permute-done.1 = bf16[48,1152]{1,0:T(8,128)(2,1)S(1)} collective-permute-done((bf16[48,1152]{1,0:T(8,128)(2,1)}, bf16[48,1152]{1,0:T(8,128)(2,1)S(1)}, u32[]{:S(2)}, u32[]{:S(2)}) %collective-permute-start.1) | collective-permute-done | bytes 110624 | tf_op jit(solution)/shard_map/ppermute | solution.py:68
  28.0 5.9 %prepare.1 = (bf16[1024,768]{1,0:T(8,128)(2,1)}, bf16[1024,768]{1,0:T(8,128)(2,1)}, bf16[1024,768]{1,0:T(8,128)(2,1)}, bf16[768,1024]{1,0:T(8,128)(2,1)}, bf16[768,1024]{1,0:T(8,128)(2,1)}, /*index=5*/f32[8,768]{1,0:T(8,128)}) custom-call(s32[1]{0:T(128)} %bitcast.core_ref, bf16[512,768]{1,0:T(8,128)(2,1)} %x.1, bf16[512,768]{1,0:T(8,128)(2,1)} %copy-done.6, ...), custom_call_target="tpu_custom_call" | custom-call | flops 31457280 | bytes 11010048 | tf_op jit(solution)/shard_map/prepare/pallas_call | solution.py:353
  52.6 6.2 %project.1 = (bf16[768,1152]{1,0:T(8,128)(2,1)}, bf16[1024,384]{1,0:T(8,128)(2,1)}, bf16[1024,384]{1,0:T(8,128)(2,1)}, bf16[1024,384]{1,0:T(8,128)(2,1)}) custom-call(s32[16]{0:T(128)} %stack.113.order_ref, bf16[192,1152]{1,0:T(8,128)(2,1)} %copy-done.12, bf16[192,1152]{1,0:T(8,128)(2,1)} %copy-done.24, bf16[192,1152]{1,0:T(8,128)(2,1)} %copy-done.23, ...), custom_call_target="tpu_custom_call" | custom-call | flops 7247757312 | bytes 7471104 | tf_op jit(solution)/shard_map/project/pallas_call | solution.py:408
  58.8 6.2 %attend_forward.4 = (f32[1024,128]{1,0:T(8,128)}, f32[8,1024]{1,0:T(8,128)}) custom-call(s32[1]{0:T(128)S(6)} %copy.29.prefix_ref, bf16[1024,384]{1,0:T(8,128)(2,1)} %get-tuple-element.169.query_ref, bf16[1024,384]{1,0:T(8,128)(2,1)} %get-tuple-element.170.key_ref, bf16[1024,384]{1,0:T(8,128)(2,1)} %get-tuple-element.171.value_ref), custom_call_target="tpu_custom_call" | custom-call | flops 8589934592 | bytes 1310720 | tf_op jit(solution)/shard_map/attend_forward/pallas_call | solution.py:459
  65.0 6.2 %attend_forward.3 = (f32[1024,128]{1,0:T(8,128)}, f32[8,1024]{1,0:T(8,128)}) custom-call(s32[1]{0:T(128)S(6)} %copy.29.prefix_ref, bf16[1024,384]{1,0:T(8,128)(2,1)} %get-tuple-element.169.query_ref, bf16[1024,384]{1,0:T(8,128)(2,1)} %get-tuple-element.170.key_ref, bf16[1024,384]{1,0:T(8,128)(2,1)} %get-tuple-element.171.value_ref), custom_call_target="tpu_custom_call" | custom-call | flops 8589934592 | bytes 1310720 | tf_op jit(solution)/shard_map/attend_forward/pallas_call | solution.py:459
  75.4 6.4 %attend_forward.5 = (f32[1024,128]{1,0:T(8,128)}, f32[8,1024]{1,0:T(8,128)}) custom-call(s32[1]{0:T(128)S(6)} %copy.29.prefix_ref, bf16[1024,384]{1,0:T(8,128)(2,1)} %get-tuple-element.169.query_ref, bf16[1024,384]{1,0:T(8,128)(2,1)} %get-tuple-element.170.key_ref, bf16[1024,384]{1,0:T(8,128)(2,1)} %get-tuple-element.171.value_ref), custom_call_target="tpu_custom_call" | custom-call | flops 8589934592 | bytes 1310720 | tf_op jit(solution)/shard_map/attend_forward/pallas_call | solution.py:459
  83.3 6.6 %mix.1 = (bf16[768,384]{1,0:T(8,128)(2,1)}, bf16[768,1536]{1,0:T(8,128)(2,1)}, bf16[1024,896]{1,0:T(8,128)(2,1)}, f32[8,768]{1,0:T(8,128)}) custom-call(s32[16]{0:T(128)} %stack.113.order_ref, bf16[192,1920]{1,0:T(8,128)(2,1)} %constant_dynamic-update-slice_fusion.refs_0_, bf16[192,1920]{1,0:T(8,128)(2,1)} %copy-done.18, bf16[192,1920]{1,0:T(8,128)(2,1)} %copy-done.17, ...), custom_call_target="tpu_custom_call" | custom-call | flops 2415919104 | bytes 10616832 | tf_op jit(solution)/shard_map/mix/pallas_call | solution.py:572
  91.4 14.5 %collective-permute-done.18.refs_2_ = bf16[192,1536]{1,0:T(8,128)(2,1)S(1)} collective-permute-done((bf16[192,1536]{1,0:T(8,128)(2,1)}, bf16[192,1536]{1,0:T(8,128)(2,1)S(1)}, u32[]{:S(2)}, u32[]{:S(2)}) %collective-permute-start.18) | collective-permute-done | bytes 589856 | tf_op jit(solution)/shard_map/ppermute | solution.py:68
  109.7 10.6 %feed_up.1 = (f32[1024,768]{1,0:T(8,128)}, bf16[768,1024]{1,0:T(8,128)(2,1)}, bf16[1024,1536]{1,0:T(8,128)(2,1)}, bf16[1024,1536]{1,0:T(8,128)(2,1)}) custom-call(bf16[1024,896]{1,0:T(8,128)(2,1)} %get-tuple-element.175.one, bf16[1024,896]{1,0:T(8,128)(2,1)} %copy-done, f32[8,768]{1,0:T(8,128)} %get-tuple-element.179.side_one, f32[8,768]{1,0:T(8,128)} %copy-done.26, ...), custom_call_target="tpu_custom_call" | custom-call | flops 9663676416 | bytes 18087936 | tf_op jit(solution)/shard_map/feed_up/pallas_call | solution.py:613
  121.1 8.4 %feed_down.1 = (bf16[768,1536]{1,0:T(8,128)(2,1)}, bf16[1024,896]{1,0:T(8,128)(2,1)}, f32[8,768]{1,0:T(8,128)}) custom-call(s32[16]{0:T(128)} %stack.113.order_ref, bf16[192,1536]{1,0:T(8,128)(2,1)} %constant_dynamic-update-slice_fusion.4.refs_0_, bf16[192,1536]{1,0:T(8,128)(2,1)} %copy-done.21, bf16[192,1536]{1,0:T(8,128)(2,1)} %copy-done.20, ...), custom_call_target="tpu_custom_call" | custom-call | flops 9663676416 | bytes 9437184 | tf_op jit(solution)/shard_map/feed_down/pallas_call | solution.py:665
  134.7 14.0 %feed_back.1 = (bf16[512,768]{1,0:T(8,128)(2,1)}, bf16[1024,1536]{1,0:T(8,128)(2,1)}, bf16[1024,1536]{1,0:T(8,128)(2,1)}, bf16[1024,768]{1,0:T(8,128)(2,1)}, f32[8,1536]{1,0:T(8,128)}) custom-call(s32[1]{0:T(128)} %bitcast.core_ref, bf16[1024,896]{1,0:T(8,128)(2,1)} %get-tuple-element.185.one, bf16[1024,896]{1,0:T(8,128)(2,1)} %copy-done.28, ...), custom_call_target="tpu_custom_call" | custom-call | flops 19327352832 | bytes 26738688 | tf_op jit(solution)/shard_map/feed_back/pallas_call | solution.py:747
  148.9 5.9 %weight_grad.5 = (bf16[384,1536]{1,0:T(8,128)(2,1)}, bf16[384,1536]{1,0:T(8,128)(2,1)}) custom-call(s32[16]{0:T(128)} %stack.119.order_ref, bf16[768,1024]{1,0:T(8,128)(2,1)} %get-tuple-element.208.refs_0_, bf16[1024,1536]{1,0:T(8,128)(2,1)} %get-tuple-element.209.refs_1_), custom_call_target="tpu_custom_call" | custom-call | flops 9663676416 | bytes 7077888 | tf_op jit(solution)/shard_map/weight_grad/pallas_call | solution.py:1036
  156.2 6.0 %weight_grad.4 = (bf16[384,1536]{1,0:T(8,128)(2,1)}, bf16[384,1536]{1,0:T(8,128)(2,1)}) custom-call(s32[16]{0:T(128)} %stack.118.order_ref, bf16[768,1024]{1,0:T(8,128)(2,1)} %get-tuple-element.199.refs_0_, bf16[1024,1536]{1,0:T(8,128)(2,1)} %get-tuple-element.200.refs_1_), custom_call_target="tpu_custom_call" | custom-call | flops 9663676416 | bytes 7077888 | tf_op jit(solution)/shard_map/weight_grad/pallas_call | solution.py:1036
  164.1 10.4 %mix_back.1 = (f32[1024,768]{1,0:T(8,128)}, bf16[768,1024]{1,0:T(8,128)(2,1)}, bf16[1024,384]{1,0:T(8,128)(2,1)}, bf16[1024,384]{1,0:T(8,128)(2,1)}, f32[8,768]{1,0:T(8,128)}, /*index=5*/f32[8,384]{1,0:T(8,128)}) custom-call(bf16[1024,768]{1,0:T(8,128)(2,1)} %get-tuple-element.192.back_one, bf16[1024,768]{1,0:T(8,128)(2,1)} %copy-done.1, ...), custom_call_target="tpu_custom_call" | custom-call | flops 2415919104 | bytes 19464192 | tf_op jit(solution)/shard_map/mix_back/pallas_call | solution.py:855
  174.6 8.0 %attend_backward.4 = (bf16[1024,128]{1,0:T(8,128)(2,1)}, bf16[1024,128]{1,0:T(8,128)(2,1)}, bf16[1024,128]{1,0:T(8,128)(2,1)}) custom-call(s32[1]{0:T(128)S(6)} %copy.29.prefix_ref, bf16[1024,384]{1,0:T(8,128)(2,1)} %get-tuple-element.169.query_ref, bf16[1024,384]{1,0:T(8,128)(2,1)} %get-tuple-element.170.key_ref, ...), custom_call_target="tpu_custom_call" | custom-call | flops 21474836480 | bytes 2359296 | tf_op jit(solution)/shard_map/attend_backward/pallas_call | solution.py:534
  182.5 8.1 %attend_backward.3 = (bf16[1024,128]{1,0:T(8,128)(2,1)}, bf16[1024,128]{1,0:T(8,128)(2,1)}, bf16[1024,128]{1,0:T(8,128)(2,1)}) custom-call(s32[1]{0:T(128)S(6)} %copy.29.prefix_ref, bf16[1024,384]{1,0:T(8,128)(2,1)} %get-tuple-element.169.query_ref, bf16[1024,384]{1,0:T(8,128)(2,1)} %get-tuple-element.170.key_ref, ...), custom_call_target="tpu_custom_call" | custom-call | flops 21474836480 | bytes 2359296 | tf_op jit(solution)/shard_map/attend_backward/pallas_call | solution.py:534
  195.2 8.2 %attend_backward.5 = (bf16[1024,128]{1,0:T(8,128)(2,1)}, bf16[1024,128]{1,0:T(8,128)(2,1)}, bf16[1024,128]{1,0:T(8,128)(2,1)}) custom-call(s32[1]{0:T(128)S(6)} %copy.29.prefix_ref, bf16[1024,384]{1,0:T(8,128)(2,1)} %get-tuple-element.169.query_ref, bf16[1024,384]{1,0:T(8,128)(2,1)} %get-tuple-element.170.key_ref, ...), custom_call_target="tpu_custom_call" | custom-call | flops 21474836480 | bytes 2359296 | tf_op jit(solution)/shard_map/attend_backward/pallas_call | solution.py:534
  212.6 4.8 %weight_grad.6 = (bf16[384,768]{1,0:T(8,128)(2,1)}, bf16[384,768]{1,0:T(8,128)(2,1)}) custom-call(s32[16]{0:T(128)} %stack.119.order_ref, bf16[768,1024]{1,0:T(8,128)(2,1)} %get-tuple-element.218.refs_0_, bf16[1024,128]{1,0:T(8,128)(2,1)} %get-tuple-element.238.refs_1_.refs_0_, bf16[1024,128]{1,0:T(8,128)(2,1)} %get-tuple-element.239.refs_2_.refs_1_, ...), custom_call_target="tpu_custom_call" | custom-call | flops 4831838208 | bytes 4325376 | tf_op jit(solution)/shard_map/weight_grad/pallas_call | solution.py:1036
  217.5 5.4 %weight_grad.7 = (bf16[384,768]{1,0:T(8,128)(2,1)}, bf16[384,768]{1,0:T(8,128)(2,1)}) custom-call(s32[16]{0:T(128)} %stack.118.order_ref, bf16[768,1024]{1,0:T(8,128)(2,1)} %get-tuple-element.218.refs_0_, bf16[768,1024]{1,0:T(8,128)(2,1)} %get-tuple-element.219.refs_1_, bf16[1024,128]{1,0:T(8,128)(2,1)} %get-tuple-element.241.refs_2_.refs_3_, ...), custom_call_target="tpu_custom_call" | custom-call | flops 4831838208 | bytes 4325376 | tf_op jit(solution)/shard_map/weight_grad/pallas_call | solution.py:1036
  225.5 6.8 %project_back.1 = (bf16[512,768]{1,0:T(8,128)(2,1)}, f32[512,768]{1,0:T(8,128)}, f32[8,384]{1,0:T(8,128)}) custom-call(s32[1]{0:T(128)} %bitcast.core_ref, bf16[1024,128]{1,0:T(8,128)(2,1)} %get-tuple-element.238.refs_1_.refs_0_, bf16[1024,128]{1,0:T(8,128)(2,1)} %get-tuple-element.239.refs_2_.refs_1_, bf16[1024,128]{1,0:T(8,128)(2,1)} %get-tuple-element.240.refs_3_.refs_2_, ...), custom_call_target="tpu_custom_call" | custom-call | flops 7247757312 | bytes 8847360 | tf_op jit(solution)/shard_map/project_back/pallas_call | solution.py:939
  258.0 6.1 %collective-permute-start.46 = (f32[84,128]{1,0:T(8,128)S(1)}, f32[84,128]{1,0:T(8,128)S(1)}, u32[]{:S(2)}, u32[]{:S(2)}) collective-permute-start(f32[84,128]{1,0:T(8,128)S(1)} %add.282), channel_id=1, source_target_pairs={{0,8},{2,10},{4,12},{6,14},{8,0},{10,2},{12,4},{14,6},{16,24},{18,... | collective-permute-start | bytes 129032 | tf_op jit(solution)/shard_map/ppermute | solution.py:68
  268.5 5.8 %collective-permute-start.40 = (bf16[48,1536]{1,0:T(8,128)(2,1)}, bf16[48,1536]{1,0:T(8,128)(2,1)S(1)}, u32[]{:S(2)}, u32[]{:S(2)}) collective-permute-start(bf16[48,1536]{1,0:T(8,128)(2,1)} %get-tuple-element.266), channel_id=1, source_target_pairs={{0,8},{2,10},{4,12},{6,14},{8,16},{10,18},{12,20},{14,22},{16,24},... | collective-permute-start | bytes 442376 | tf_op jit(solution)/shard_map/ppermute | solution.py:68
  278.7 11.2 %collective-permute-done.47.two_ref = f32[84,128]{1,0:T(8,128)S(1)} collective-permute-done((f32[84,128]{1,0:T(8,128)S(1)}, f32[84,128]{1,0:T(8,128)S(1)}, u32[]{:S(2)}, u32[]{:S(2)}) %collective-permute-start.47) | collective-permute-done | bytes 43040 | tf_op jit(solution)/shard_map/ppermute | solution.py:68
  (199 shorter events, 109.3 us)
Async XLA Ops:
  0.6 24.3 %collective-permute-start.7 = (bf16[512,768]{1,0:T(8,128)(2,1)}, bf16[512,768]{1,0:T(8,128)(2,1)S(1)}, u32[]{:S(2)}, u32[]{:S(2)}) collective-permute-start(bf16[512,768]{1,0:T(8,128)(2,1)} %g_own), channel_id=1, source_target_pairs={{0,1},{1,0},{2,3},{3,2},{4,5},{5,4},{6,7},{7,6},{8,9},{9,8},{10,11... | collective-permute-start | bytes 2359304 | tf_op jit(solution)/shard_map/ppermute | solution.py:26
  1.2 25.3 %collective-permute-start.6 = (bf16[512,768]{1,0:T(8,128)(2,1)}, bf16[512,768]{1,0:T(8,128)(2,1)S(1)}, u32[]{:S(2)}, u32[]{:S(2)}) collective-permute-start(bf16[512,768]{1,0:T(8,128)(2,1)} %x.1), channel_id=1, source_target_pairs={{0,1},{1,0},{2,3},{3,2},{4,5},{5,4},{6,7},{7,6},{8,9},{9,8},{10,11... | collective-permute-start | bytes 2359304 | tf_op jit(solution)/shard_map/ppermute | solution.py:26
  20.6 16.8 %collective-permute-start.4 = (bf16[48,1920]{1,0:T(8,128)(2,1)}, bf16[48,1920]{1,0:T(8,128)(2,1)S(1)}, u32[]{:S(2)}, u32[]{:S(2)}) collective-permute-start(bf16[48,1920]{1,0:T(8,128)(2,1)} %join.2), channel_id=1, source_target_pairs={{0,16},{2,18},{4,20},{6,22},{8,24},{10,26},{12,28},{14,30},{16,0},... | collective-permute-start | bytes 552968 | tf_op jit(solution)/shard_map/ppermute | solution.py:68
  21.4 16.1 %collective-permute-start.3 = (bf16[48,1920]{1,0:T(8,128)(2,1)}, bf16[48,1920]{1,0:T(8,128)(2,1)S(1)}, u32[]{:S(2)}, u32[]{:S(2)}) collective-permute-start(bf16[48,1920]{1,0:T(8,128)(2,1)} %join.2), channel_id=1, source_target_pairs={{0,8},{2,10},{4,12},{6,14},{8,16},{10,18},{12,20},{14,22},{16,24},... | collective-permute-start | bytes 552968 | tf_op jit(solution)/shard_map/ppermute | solution.py:68
  25.0 17.6 %collective-permute-start.12 = (bf16[192,1152]{1,0:T(8,128)(2,1)S(1)}, bf16[192,1152]{1,0:T(8,128)(2,1)S(1)}, u32[]{:S(2)}, u32[]{:S(2)}) collective-permute-start(bf16[192,1152]{1,0:T(8,128)(2,1)S(1)} %pad_maximum_fusion.refs_0_), channel_id=1, source_target_pairs={{0,4},{2,6},{4,0},{6,2},{8,12},{10,14},{12,8},{14,10},{16,20},{18,... | collective-permute-start | bytes 1327112 | tf_op jit(solution)/shard_map/ppermute | solution.py:68
  26.5 16.1 %collective-permute-start.11 = (bf16[192,1152]{1,0:T(8,128)(2,1)S(1)}, bf16[192,1152]{1,0:T(8,128)(2,1)S(1)}, u32[]{:S(2)}, u32[]{:S(2)}) collective-permute-start(bf16[192,1152]{1,0:T(8,128)(2,1)S(1)} %pad_maximum_fusion.refs_0_), channel_id=1, source_target_pairs={{0,2},{2,0},{4,6},{6,4},{8,10},{10,8},{12,14},{14,12},{16,18},{18,... | collective-permute-start | bytes 1327112 | tf_op jit(solution)/shard_map/ppermute | solution.py:68
  39.5 31.7 %collective-permute-start.10 = (bf16[48,1536]{1,0:T(8,128)(2,1)S(1)}, bf16[48,1536]{1,0:T(8,128)(2,1)S(1)}, u32[]{:S(2)}, u32[]{:S(2)}) collective-permute-start(bf16[48,1536]{1,0:T(8,128)(2,1)S(1)} %copy-done.22), channel_id=1, source_target_pairs={{0,24},{2,26},{4,28},{6,30},{8,0},{10,2},{12,4},{14,6},{16,8},{18,... | collective-permute-start | bytes 442376 | tf_op jit(solution)/shard_map/ppermute | solution.py:68
  39.5 31.7 %collective-permute-start.9 = (bf16[48,1536]{1,0:T(8,128)(2,1)S(1)}, bf16[48,1536]{1,0:T(8,128)(2,1)S(1)}, u32[]{:S(2)}, u32[]{:S(2)}) collective-permute-start(bf16[48,1536]{1,0:T(8,128)(2,1)S(1)} %copy-done.22), channel_id=1, source_target_pairs={{0,16},{2,18},{4,20},{6,22},{8,24},{10,26},{12,28},{14,30},{16,0},... | collective-permute-start | bytes 442376 | tf_op jit(solution)/shard_map/ppermute | solution.py:68
  40.6 30.6 %collective-permute-start.8 = (bf16[48,1536]{1,0:T(8,128)(2,1)S(1)}, bf16[48,1536]{1,0:T(8,128)(2,1)S(1)}, u32[]{:S(2)}, u32[]{:S(2)}) collective-permute-start(bf16[48,1536]{1,0:T(8,128)(2,1)S(1)} %copy-done.22), channel_id=1, source_target_pairs={{0,8},{2,10},{4,12},{6,14},{8,16},{10,18},{12,20},{14,22},{16,24},... | collective-permute-start | bytes 442376 | tf_op jit(solution)/shard_map/ppermute | solution.py:68
  50.5 22.7 %collective-permute-start.16 = (bf16[192,1920]{1,0:T(8,128)(2,1)}, bf16[192,1920]{1,0:T(8,128)(2,1)S(1)}, u32[]{:S(2)}, u32[]{:S(2)}) collective-permute-start(bf16[192,1920]{1,0:T(8,128)(2,1)} %constant_dynamic-update-slice_fusion.refs_0_), channel_id=1, source_target_pairs={{0,4},{2,6},{4,0},{6,2},{8,12},{10,14},{12,8},{14,10},{16,20},{18,... | collective-permute-start | bytes 2211848 | tf_op jit(solution)/shard_map/ppermute | solution.py:68
  52.0 21.2 %collective-permute-start.15 = (bf16[192,1920]{1,0:T(8,128)(2,1)}, bf16[192,1920]{1,0:T(8,128)(2,1)S(1)}, u32[]{:S(2)}, u32[]{:S(2)}) collective-permute-start(bf16[192,1920]{1,0:T(8,128)(2,1)} %constant_dynamic-update-slice_fusion.refs_0_), channel_id=1, source_target_pairs={{0,2},{2,0},{4,6},{6,4},{8,10},{10,8},{12,14},{14,12},{16,18},{18,... | collective-permute-start | bytes 2211848 | tf_op jit(solution)/shard_map/ppermute | solution.py:68
  89.9 18.5 %collective-permute-start.23 = (bf16[1024,896]{1,0:T(8,128)(2,1)}, bf16[1024,896]{1,0:T(8,128)(2,1)S(1)}, u32[]{:S(2)}, u32[]{:S(2)}) collective-permute-start(bf16[1024,896]{1,0:T(8,128)(2,1)} %get-tuple-element.175.one), channel_id=1, source_target_pairs={{0,1},{1,0},{2,3},{3,2},{4,5},{5,4},{6,7},{7,6},{8,9},{9,8},{10,11... | collective-permute-start | bytes 5505032 | tf_op jit(solution)/shard_map/ppermute | solution.py:26
  89.9 15.9 %collective-permute-start.18 = (bf16[192,1536]{1,0:T(8,128)(2,1)}, bf16[192,1536]{1,0:T(8,128)(2,1)S(1)}, u32[]{:S(2)}, u32[]{:S(2)}) collective-permute-start(bf16[192,1536]{1,0:T(8,128)(2,1)} %constant_dynamic-update-slice_fusion.4.refs_0_), channel_id=1, source_target_pairs={{0,4},{2,6},{4,0},{6,2},{8,12},{10,14},{12,8},{14,10},{16,20},{18,... | collective-permute-start | bytes 1769480 | tf_op jit(solution)/shard_map/ppermute | solution.py:68
  90.8 15.6 %collective-permute-start.17 = (bf16[192,1536]{1,0:T(8,128)(2,1)}, bf16[192,1536]{1,0:T(8,128)(2,1)S(1)}, u32[]{:S(2)}, u32[]{:S(2)}) collective-permute-start(bf16[192,1536]{1,0:T(8,128)(2,1)} %constant_dynamic-update-slice_fusion.4.refs_0_), channel_id=1, source_target_pairs={{0,2},{2,0},{4,6},{6,4},{8,10},{10,8},{12,14},{14,12},{16,18},{18,... | collective-permute-start | bytes 1769480 | tf_op jit(solution)/shard_map/ppermute | solution.py:68
  91.4 17.0 %collective-permute-start.24 = (f32[8,768]{1,0:T(8,128)}, f32[8,768]{1,0:T(8,128)S(1)}, u32[]{:S(2)}, u32[]{:S(2)}) collective-permute-start(f32[8,768]{1,0:T(8,128)} %get-tuple-element.179.side_one), channel_id=1, source_target_pairs={{0,1},{1,0},{2,3},{3,2},{4,5},{5,4},{6,7},{7,6},{8,9},{9,8},{10,11... | collective-permute-start | bytes 73736 | tf_op jit(solution)/shard_map/ppermute | solution.py:26
  154.8 35.8 %collective-permute-start.29 = (bf16[384,1536]{1,0:T(8,128)(2,1)}, bf16[384,1536]{1,0:T(8,128)(2,1)S(1)}, u32[]{:S(2)}, u32[]{:S(2)}) collective-permute-start(bf16[384,1536]{1,0:T(8,128)(2,1)} %get-tuple-element.211), channel_id=1, source_target_pairs={{0,2},{2,0},{4,6},{6,4},{8,10},{10,8},{12,14},{14,12},{16,18},{18,... | collective-permute-start | bytes 3538952 | tf_op jit(solution)/shard_map/ppermute | solution.py:68
  162.2 28.5 %collective-permute-start.28 = (bf16[384,1536]{1,0:T(8,128)(2,1)}, bf16[384,1536]{1,0:T(8,128)(2,1)S(1)}, u32[]{:S(2)}, u32[]{:S(2)}) collective-permute-start(bf16[384,1536]{1,0:T(8,128)(2,1)} %get-tuple-element.202), channel_id=1, source_target_pairs={{0,4},{2,6},{4,0},{6,2},{8,12},{10,14},{12,8},{14,10},{16,20},{18,... | collective-permute-start | bytes 3538952 | tf_op jit(solution)/shard_map/ppermute | solution.py:68
  232.5 22.9 %collective-permute-start.37 = (bf16[48,3072]{1,0:T(8,128)(2,1)}, bf16[48,3072]{1,0:T(8,128)(2,1)}, u32[]{:S(2)}, u32[]{:S(2)}) collective-permute-start(bf16[48,3072]{1,0:T(8,128)(2,1)} %get-tuple-element.223), channel_id=1, source_target_pairs={{0,8},{2,10},{4,12},{6,14},{8,16},{10,18},{12,20},{14,22},{16,24},... | collective-permute-start | bytes 884744 | tf_op jit(solution)/shard_map/ppermute | solution.py:68
  232.7 23.8 %collective-permute-start.38 = (bf16[48,3072]{1,0:T(8,128)(2,1)}, bf16[48,3072]{1,0:T(8,128)(2,1)}, u32[]{:S(2)}, u32[]{:S(2)}) collective-permute-start(bf16[48,3072]{1,0:T(8,128)(2,1)} %get-tuple-element.224), channel_id=1, source_target_pairs={{0,16},{2,18},{4,20},{6,22},{8,24},{10,26},{12,28},{14,30},{16,0},... | collective-permute-start | bytes 884744 | tf_op jit(solution)/shard_map/ppermute | solution.py:68
  236.9 19.5 %collective-permute-start.39 = (bf16[48,3072]{1,0:T(8,128)(2,1)}, bf16[48,3072]{1,0:T(8,128)(2,1)}, u32[]{:S(2)}, u32[]{:S(2)}) collective-permute-start(bf16[48,3072]{1,0:T(8,128)(2,1)} %get-tuple-element.225), channel_id=1, source_target_pairs={{0,24},{2,26},{4,28},{6,30},{8,0},{10,2},{12,4},{14,6},{16,8},{18,... | collective-permute-start | bytes 884744 | tf_op jit(solution)/shard_map/ppermute | solution.py:68
  258.0 18.8 %collective-permute-start.46 = (f32[84,128]{1,0:T(8,128)S(1)}, f32[84,128]{1,0:T(8,128)S(1)}, u32[]{:S(2)}, u32[]{:S(2)}) collective-permute-start(f32[84,128]{1,0:T(8,128)S(1)} %add.282), channel_id=1, source_target_pairs={{0,8},{2,10},{4,12},{6,14},{8,0},{10,2},{12,4},{14,6},{16,24},{18,... | collective-permute-start | bytes 129032 | tf_op jit(solution)/shard_map/ppermute | solution.py:68
  268.5 23.4 %collective-permute-start.40 = (bf16[48,1536]{1,0:T(8,128)(2,1)}, bf16[48,1536]{1,0:T(8,128)(2,1)S(1)}, u32[]{:S(2)}, u32[]{:S(2)}) collective-permute-start(bf16[48,1536]{1,0:T(8,128)(2,1)} %get-tuple-element.266), channel_id=1, source_target_pairs={{0,8},{2,10},{4,12},{6,14},{8,16},{10,18},{12,20},{14,22},{16,24},... | collective-permute-start | bytes 442376 | tf_op jit(solution)/shard_map/ppermute | solution.py:68
  274.4 17.6 %collective-permute-start.41 = (bf16[48,1536]{1,0:T(8,128)(2,1)}, bf16[48,1536]{1,0:T(8,128)(2,1)S(1)}, u32[]{:S(2)}, u32[]{:S(2)}) collective-permute-start(bf16[48,1536]{1,0:T(8,128)(2,1)} %get-tuple-element.267), channel_id=1, source_target_pairs={{0,16},{2,18},{4,20},{6,22},{8,24},{10,26},{12,28},{14,30},{16,0},... | collective-permute-start | bytes 442376 | tf_op jit(solution)/shard_map/ppermute | solution.py:68
  276.2 15.7 %collective-permute-start.42 = (bf16[48,1536]{1,0:T(8,128)(2,1)}, bf16[48,1536]{1,0:T(8,128)(2,1)S(1)}, u32[]{:S(2)}, u32[]{:S(2)}) collective-permute-start(bf16[48,1536]{1,0:T(8,128)(2,1)} %get-tuple-element.268), channel_id=1, source_target_pairs={{0,24},{2,26},{4,28},{6,30},{8,0},{10,2},{12,4},{14,6},{16,8},{18,... | collective-permute-start | bytes 442376 | tf_op jit(solution)/shard_map/ppermute | solution.py:68
  (59 other events, 477.0 us)

commit v4 on v3

--- a/solution.py
+++ b/solution.py
@@ -99,11 +99,16 @@
             ]
         return places
 
-    def along_lines(self, values, meanwhile=lambda got: got):
-        block = values
-        for factor, stride in self.lines:
-            got = [self.shift(block, factor, stride, step) for step in range(1, factor)]
-            block = jnp.concatenate([block] + meanwhile(got), 0)
+    def start_gather(self, values):
+        factor, stride = self.lines[0]
+        return [self.shift(values, factor, stride, step) for step in range(1, factor)]
+
+    def end_gather(self, values, got):
+        block = jnp.concatenate([values, *got], 0)
+        for factor, stride in self.lines[1:]:
+            block = jnp.concatenate(
+                [block] + [self.shift(block, factor, stride, step) for step in range(1, factor)], 0
+            )
         return block
 
     def to_sides(self, block):
@@ -131,24 +136,34 @@
         own = widen(keep[:half]) + widen(got[:half])
         return own, (widen(keep[half:]) + widen(got[half:])).astype(bf16)
 
-    def sum_lines(self, own, seconds, meanwhile):
-        parts = square_end(own, seconds, self.lines[0][0])
-        for at, (factor, stride) in enumerate(self.lines):
-            got = [self.shift(parts[step], factor, stride, step) for step in range(1, factor)]
-            total = parts[0]
-            for piece in meanwhile(got, parts):
-                total = total + widen(piece)
-            if at + 1 < len(self.lines):
-                pieces = jnp.split(total, self.lines[at + 1][0])
-                parts = [pieces[0]] + [piece.astype(bf16) for piece in pieces[1:]]
-        return total
-
-    def sum_strides(self):
-        stride, strides = 1, []
-        while stride < self.size:
-            strides.append(stride)
-            stride *= 2
-        return strides
+    def start_lines(self, parts):
+        factor, stride = self.lines[0]
+        return [self.shift(parts[step], factor, stride, step) for step in range(1, factor)]
+
+    def last_terms(self, parts, got):
+        terms = [parts[0], *got]
+        for factor, stride in self.lines[1:]:
+            total = add_up(terms)
+            pieces = jnp.split(total, factor)
+            terms = [pieces[0]] + [
+                self.shift(pieces[step].astype(bf16), factor, stride, step)
+                for step in range(1, factor)
+            ]
+        return terms
+
+    def around(self, values, factor, stride):
+        return [self.shift(values, factor, stride, step) for step in range(1, factor)]
+
+    def around_square(self, values):
+        pairs = [(place, place ^ 3) for place in range(self.size)]
+        return [self.flip(values, 1), self.flip(values, 2), lax.ppermute(values, "dp", pairs)]
+
+
+def add_up(terms):
+    total = widen(terms[0])
+    for term in terms[1:]:
+        total = total + widen(term)
+    return total
 
 
 def whole(shape):
@@ -303,11 +318,11 @@
     )(*parts)
 
 
-def unpack(one, two, shapes):
-    def body(one_ref, two_ref, *outs):
-        total = one_ref[...] + two_ref[...]
+def unpack(terms, shapes):
+    def body(*refs):
+        total = add_up([ref[...] for ref in refs[: len(terms)]])
         at = 0
-        for out in outs:
+        for out in refs[len(terms) :]:
             for row in range(out.shape[0]):
                 for left in range(0, out.shape[1], LANES):
                     out[row : row + 1, left : left + LANES] = total[at : at + 1, :]
@@ -316,10 +331,38 @@
     return pl.pallas_call(
         body,
         out_shape=[shape_of(shape, f32) for shape in shapes],
-        in_specs=[pl.BlockSpec(memory_space=pltpu.VMEM)] * 2,
+        in_specs=[pl.BlockSpec(memory_space=pltpu.VMEM)] * len(terms),
         out_specs=[pl.BlockSpec(memory_space=pltpu.VMEM)] * len(shapes),
         name="unpack",
-    )(one, two)
+    )(*terms)
+
+
+def finish(groups, layout):
+    sizes = [len(terms) for terms in groups]
+    terms = [term for group in groups for term in group]
+    rows = groups[0][0].shape[0]
+
+    def body(*refs):
+        ins, outs = refs[: len(terms)], refs[len(terms) :]
+        for out, columns in zip(outs, layout):
+            left = 0
+            for group, start, width in columns:
+                first = sum(sizes[:group])
+                span = slice(start, start + width)
+                out[:, left : left + width] = add_up(
+                    [ref[:, span] for ref in ins[first : first + sizes[group]]]
+                )
+                left += width
+
+    return pl.pallas_call(
+        body,
+        out_shape=[
+            shape_of((rows, sum(width for _, _, width in columns)), f32) for columns in layout
+        ],
+        in_specs=[pl.BlockSpec(memory_space=pltpu.VMEM)] * len(terms),
+        out_specs=[pl.BlockSpec(memory_space=pltpu.VMEM)] * len(layout),
+        name="finish",
+    )(*terms)
 
 
 def prepare(core, tokens, tokens_other, cotangent, cotangent_other, model_vectors):
@@ -1079,38 +1122,46 @@
     bias = jnp.concatenate([head_vectors[0], jnp.zeros_like(head_vectors[0]), head_vectors[1]])
     pair_count = half // PAIR
     tokens_other, cotangent_other = flip_partner(tokens), flip_partner(cotangent)
-    first_block = ring.along_lines(join(query_weight, key_weight, value_weight))
+    first = join(query_weight, key_weight, value_weight)
+    first_got = ring.start_gather(first)
+    inputs, grads, attend_in, attend_turned, grads_turned, grad_sums = prepare(
+        core, tokens, tokens_other, cotangent, cotangent_other, model_vectors
+    )
+    first_block = ring.end_gather(first, after(first_got, attend_in))
     first_sides = ring.to_sides(first_block)
     second = after(join(out_weight, up_weight), first_block)
-    whole_rows = after((tokens, tokens_other, cotangent, cotangent_other), first_block)
-    inputs, grads, attend_in, attend_turned, grads_turned, grad_sums = prepare(
-        core, *whole_rows, model_vectors
-    )
-    second_block = ring.along_lines(second, lambda got: after(got, attend_in))
-    first_sides = after(first_sides, attend_in)
+    second_got = ring.start_gather(second)
     first_pieces = (first_block, *first_sides, *ring.to_corner(*first_sides))
-
-    second_sides = ring.to_sides(after(second_block, first_pieces))
+    first_weight, queries, keys, values = project(
+        order, first_pieces, attend_in, bias[None]
+    )
+    states = (prefix, queries, keys, values)
+    second_block = ring.end_gather(second, after(second_got, queries))
+    second_sides = ring.to_sides(second_block)
     third = after(down_weight, second_block)
-    first_weight, queries, keys, values = project(order, first_pieces, attend_in, bias[None])
-    states = (prefix, queries, keys, values)
-    attended, logs = zip(*[attend_forward(pair, *states) for pair in range(pair_count - 1)])
-    third_block = ring.along_lines(third, lambda got: after(got, attended))
-    second_sides = after(second_sides, attended)
-    second_pieces = (second_block, *second_sides, *ring.to_corner(*second_sides))
-    third_sides = ring.to_sides(after(third_block, second_sides))
-    last, last_logs = attend_forward(pair_count - 1, *after(states, second_sides, third_block))
-    attended, logs = (*attended, last), (*logs, last_logs)
-    second_pieces = (second_block, *second_sides, *after(second_pieces[3:], last))
+    third_got = ring.start_gather(third)
+    attended, logs = [], []
+    for pair in range(pair_count):
+        out, log = attend_forward(pair, *states)
+        attended.append(out)
+        logs.append(log)
+        states = after(states, out, third_got[0], third_got[-1])
+        if pair == pair_count - 2:
+            second_sides = after(second_sides, out)
+            second_corner = ring.to_corner(*second_sides)
+            states = after(states, second_sides, third_got)
+    second_pieces = (second_block, *second_sides, *after(second_corner, attended[-1]))
+    third_block = ring.end_gather(third, after(third_got, second_corner, attended[-1]))
+    third_sides = ring.to_sides(third_block)
     out_full, up_full, mixed, mixed_side = mix(
-        order, second_pieces, attended, head_vectors, (half, full)
-    )
+        order, second_pieces, after(attended, third_block), head_vectors, (half, full)
+    )
+    mixed, mixed_side, third_sides = after((mixed, mixed_side, third_sides), mixed)
     mixed_other, mixed_side_other = flip_partner(mixed), flip_partner(mixed_side)
-    third_sides = after(third_sides, mixed)
     third_corner = ring.to_corner(*third_sides)
     middle, feed_turned, kept, slope = feed_up(
         mixed,
-        after(mixed_other, third_sides),
+        mixed_other,
         mixed_side,
         mixed_side_other,
         inputs,
@@ -1155,66 +1206,74 @@
         model_vectors,
         head_vectors,
     )
+
     def pair_back(pair, grad):
         return attend_backward(pair, *states, attended[pair], grad, logs[pair])
 
-    pair_grads = [pair_back(pair, attended_grad) for pair in range(pair_count - 1)]
+    last_pair = pair_count - 1
+    pair_grads = [pair_back(pair, attended_grad) for pair in range(last_pair)]
     down_own, down_away = ring.sum_first(down_keep, after(down_got, pair_grads))
     up_own, up_away = ring.sum_first(up_keep, after(up_got, pair_grads))
     up_second, down_second = ring.flip(up_away, 2), ring.flip(down_away, 1)
-    pair_grads.append(pair_back(pair_count - 1, after(attended_grad, down_away, up_away)))
+    early_grads = after(pair_grads, down_away, up_away)
+    early_keep, early_send = weight_grad(
+        near,
+        [(attend_turned, [pair[at] for pair in early_grads]) for at in range(3)],
+        last_pair * PAIR,
+    )
+    early_got = ring.flip(early_send, 1)
+    out_keep, out_send = weight_grad(
+        far, [(branch_turned, [after(mixed_in, early_send)])], half
+    )
+    out_got = ring.flip(out_send, 2)
+    pair_grads.append(pair_back(last_pair, after(attended_grad, out_send)))
     query_grad, key_grad, value_grad = ([pair[at] for pair in pair_grads] for at in range(3))
-    wide_seconds = after((up_second, down_second), pair_grads)
-
-    progress = {}
-
-    def during_wide(got, parts):
-        tied_query, tied_value = after((query_grad, value_grad), parts)
-        query_keep, query_send = weight_grad(
-            near, [(attend_turned, tied_query), (attend_turned, tied_value)], half
-        )
-        query_got = ring.flip(query_send, 1)
-        key_keep, key_send = weight_grad(
-            far, [(attend_turned, after(key_grad, query_send)), (branch_turned, [mixed_in])], half
-        )
-        key_got = ring.flip(key_send, 2)
-        sums = project_back(
-            core, after((query_grad, key_grad, value_grad), key_send), first_weight
-        )
-        progress["narrow"] = (query_keep, query_got, key_keep, key_got)
-        progress["project"] = sums
-        return after(got, sums)
-
-    if len(ring.lines) > 1:
-        during_wide([], [])
-        wide_grads = ring.sum_lines((up_own, down_own), wide_seconds, lambda got, parts: got)
-    else:
-        wide_grads = ring.sum_lines((up_own, down_own), wide_seconds, during_wide)
-    up_grad, down_grad = wide_grads[:, :full], wide_grads[:, full:]
-    query_keep, query_got, key_keep, key_got = progress["narrow"]
-    send, keep, bias_sums = progress["project"]
+    wide_parts = square_end(
+        (up_own, down_own), after((up_second, down_second), pair_grads), ring.lines[0][0]
+    )
+    wide_got = ring.start_lines(wide_parts)
+    send, keep, bias_sums = project_back(
+        core, after((query_grad, key_grad, value_grad), wide_parts), first_weight
+    )
     received = flip_partner(send)
-    query_own, query_away = ring.sum_first(query_keep, after(query_got, send))
-    key_own, key_away = ring.sum_first(key_keep, after(key_got, send))
-    narrow_seconds = ring.flip(query_away, 2), ring.flip(key_away, 1)
+    late_keep, late_send = weight_grad(
+        near, [(attend_turned, after(list(pair_grads[last_pair]), send))], 3 * PAIR
+    )
+    late_got = ring.flip(late_send, 1)
+    early_got, out_got = after((early_got, out_got), late_send, wide_got[0], wide_got[-1])
+    early_own, early_away = ring.sum_first(early_keep, early_got)
+    out_own, out_away = ring.sum_first(out_keep, out_got)
+    early_second, out_second = ring.flip(early_away, 2), ring.flip(out_away, 1)
     input_grad, first_sums = input_back(
-        core, received, after(keep, query_away, key_away), middle_grad, tokens, model_vectors
-    )
-    narrow_seconds = after(narrow_seconds, input_grad)
+        core, received, after(keep, early_away, out_away), middle_grad, tokens, model_vectors
+    )
+    late_own, late_away = ring.sum_first(late_keep, after(late_got, input_grad))
+    late_second = ring.flip(late_away, 2)
     packed = pack(
         first_sums, flip_partner(first_sums), model_sums, grad_sums, bias_sums, head_sums, hidden_sums
     )
-    strides = ring.sum_strides()
-    for stride in strides[:-1]:
-        packed = packed + ring.flip(packed, stride)
+    for factor, stride in [*ring.lines[1:][::-1], ring.lines[0]]:
+        packed = add_up([packed, *ring.around(packed, factor, stride)])
     model_sum, head_sum, hidden_sum = unpack(
-        packed, ring.flip(packed, strides[-1]), ((6, features), (4, half), (3, full))
-    )
-    narrow = ring.sum_lines(
-        (query_own, key_own), after(narrow_seconds, wide_grads), lambda got, parts: got
-    )
-    query_weight_grad, value_weight_grad, key_weight_grad, out_grad = (
-        narrow[:, at * half : (at + 1) * half] for at in range(4)
+        [packed, *ring.around_square(packed)], ((6, features), (4, half), (3, full))
+    )
+    early_parts = square_end(
+        (early_own, out_own),
+        after((early_second, out_second), input_grad),
+        ring.lines[0][0],
+    )
+    early_got = ring.start_lines(early_parts)
+    late_parts = square_end((late_own,), (late_second,), ring.lines[0][0])
+    late_got = ring.start_lines(late_parts)
+    wide_terms = ring.last_terms(wide_parts, wide_got)
+    early_terms = ring.last_terms(early_parts, early_got)
+    late_terms = ring.last_terms(late_parts, late_got)
+    up_grad, down_grad = finish([wide_terms], [[(0, 0, full)], [(0, full, full)]])
+    early = last_pair * PAIR
+    query_weight_grad, key_weight_grad, value_weight_grad, out_grad = finish(
+        [early_terms, late_terms],
+        [[(0, at * early, early), (1, at * PAIR, PAIR)] for at in range(3)]
+        + [[(0, 3 * early, half)]],
     )
     return (
         output,

time: 297 us -> 275 us (0.926)
  waiting for transfers between devices: 54 us -> 21.7 us
  starting transfers between devices: 60.1 us -> 68.3 us
  Pallas kernels: 150 us -> 156 us
  local copies, waits for them, and re-layouts: 20.3 us -> 16.7 us
    ppermute x39 -> x45, waiting for transfers between devices: 50.4 us -> 18.3 us  [shift(): return lax.ppermute(values, 'dp', pairs)]
    ppermute x39 -> x45, starting transfers between devices: 58.7 us -> 64.7 us  [shift(): return lax.ppermute(values, 'dp', pairs)]
    pallas_call x0 -> x2, Pallas kernels: none -> 4.09 us  [finish(): pl.pallas_call(body, out_shape=[shape_of((rows, sum((width for _, _, widt...]
    pallas_call x4 -> x5, Pallas kernels: 22.1 us -> 23.7 us  [weight_grad(): pl.pallas_call(body, grid=(width // tile,), out_shape=[shape_of((features...]
    pallas_call x2 -> x3, Pallas kernels: 5.4 us -> 6.95 us  [square_end(): pl.pallas_call(body, out_shape=[shape_of((rows, width), f32)] + [shape_of...]
    unnamed x76 -> x104, local copies, waits for them, and re-layouts: 14 us -> 13.3 us
  transfers between devices with their start and end apart: 48 -> 55, of which waited for: 15 -> 15; matrix products, arithmetic and copies ran while one was open for 6% -> 3% of each run, Pallas kernels for 37% -> 49%
where the time goes in v4:
time: 275 us; the launch traced here: 271 us
  Pallas kernels  156 us (57%)
  starting transfers between devices  68.3 us (25%)
  waiting for transfers between devices  21.7 us (8%)
  local copies, waits for them, and re-layouts  16.7 us (6%)
  other arithmetic  6.2 us (2%)
    ppermute x45, starting transfers between devices, shift(): return lax.ppermute(values, 'dp', pairs)  64.7 us
    pallas_call x3, Pallas kernels, attend_backward(): pl.pallas_call(body, grid=(1,), out_shape=[shape_of((length, PAIR), bf16)...  24 us
    pallas_call x5, Pallas kernels, weight_grad(): pl.pallas_call(body, grid=(width // tile,), out_shape=[shape_of((features...  23.7 us
    pallas_call x3, Pallas kernels, attend_forward(): pl.pallas_call(body, grid=(1,), out_shape=[shape_of((length, PAIR), f32),...  18.8 us
    ppermute x45, waiting for transfers between devices, shift(): return lax.ppermute(values, 'dp', pairs)  18.3 us
    pallas_call x1, Pallas kernels, feed_back(): pl.pallas_call(body, grid_spec=pltpu.PrefetchScalarGridSpec(num_scalar_pr...  14 us
    unnamed x104, local copies, waits for them, and re-layouts  13.3 us
    pallas_call x1, Pallas kernels, mix_back(): pl.pallas_call(body, grid=(TILES,), out_shape=[shape_of((length, features...  10.7 us
  transfers between devices with their start and end apart: 55, of which 15 were waited for; matrix products, arithmetic and copies ran while one was open for 3% of the time, Pallas kernels for 49%

profile of v4, /device:TPU:0, one launch (start us, length us, event | category | flops | bytes accessed | tf_op | source)
XLA Modules:
  0.0 271.0 jit_solution(5598281447975215694)
XLA Ops:
  2.7 5.0 %collective-permute-start.2 = (bf16[48,1152]{1,0:T(8,128)(2,1)}, bf16[48,1152]{1,0:T(8,128)(2,1)S(1)}, u32[]{:S(2)}, u32[]{:S(2)}) collective-permute-start(bf16[48,1152]{1,0:T(8,128)(2,1)} %join.3), channel_id=1, source_target_pairs={{0,24},{2,26},{4,28},{6,30},{8,0},{10,2},{12,4},{14,6},{16,8},{18,... | collective-permute-start | bytes 331784 | tf_op jit(solution)/shard_map/ppermute | solution.py:68
  9.9 5.9 %prepare.1 = (bf16[1024,768]{1,0:T(8,128)(2,1)}, bf16[1024,768]{1,0:T(8,128)(2,1)}, bf16[1024,768]{1,0:T(8,128)(2,1)}, bf16[768,1024]{1,0:T(8,128)(2,1)}, bf16[768,1024]{1,0:T(8,128)(2,1)}, /*index=5*/f32[8,768]{1,0:T(8,128)}) custom-call(s32[1]{0:T(128)} %bitcast.core_ref, bf16[512,768]{1,0:T(8,128)(2,1)} %x.1, bf16[512,768]{1,0:T(8,128)(2,1)} %copy-done.6, ...), custom_call_target="tpu_custom_call" | custom-call | flops 31457280 | bytes 11010048 | tf_op jit(solution)/shard_map/prepare/pallas_call | solution.py:396
  38.0 5.7 %project.1 = (bf16[768,1152]{1,0:T(8,128)(2,1)}, bf16[1024,384]{1,0:T(8,128)(2,1)}, bf16[1024,384]{1,0:T(8,128)(2,1)}, bf16[1024,384]{1,0:T(8,128)(2,1)}) custom-call(s32[16]{0:T(128)} %stack.113.order_ref, bf16[192,1152]{1,0:T(8,128)(2,1)} %copy-done.10, bf16[192,1152]{1,0:T(8,128)(2,1)} %copy-done.27, bf16[192,1152]{1,0:T(8,128)(2,1)} %copy-done.26, ...), custom_call_target="tpu_custom_call" | custom-call | flops 7247757312 | bytes 7471104 | tf_op jit(solution)/shard_map/project/pallas_call | solution.py:451
  50.5 6.2 %attend_forward.3 = (f32[1024,128]{1,0:T(8,128)}, f32[8,1024]{1,0:T(8,128)}) custom-call(s32[1]{0:T(128)S(6)} %copy.29.prefix_ref, bf16[1024,384]{1,0:T(8,128)(2,1)} %get-tuple-element.220.query_ref, bf16[1024,384]{1,0:T(8,128)(2,1)} %get-tuple-element.221.key_ref, bf16[1024,384]{1,0:T(8,128)(2,1)} %get-tuple-element.222.value_ref), custom_call_target="tpu_custom_call" | custom-call | flops 8589934592 | bytes 1310720 | tf_op jit(solution)/shard_map/attend_forward/pallas_call | solution.py:502
  57.4 6.2 %attend_forward.4 = (f32[1024,128]{1,0:T(8,128)}, f32[8,1024]{1,0:T(8,128)}) custom-call(s32[1]{0:T(128)S(6)} %copy.29.prefix_ref, bf16[1024,384]{1,0:T(8,128)(2,1)} %get-tuple-element.220.query_ref, bf16[1024,384]{1,0:T(8,128)(2,1)} %get-tuple-element.221.key_ref, bf16[1024,384]{1,0:T(8,128)(2,1)} %get-tuple-element.222.value_ref), custom_call_target="tpu_custom_call" | custom-call | flops 8589934592 | bytes 1310720 | tf_op jit(solution)/shard_map/attend_forward/pallas_call | solution.py:502
  67.8 6.4 %attend_forward.5 = (f32[1024,128]{1,0:T(8,128)}, f32[8,1024]{1,0:T(8,128)}) custom-call(s32[1]{0:T(128)S(6)} %copy.29.prefix_ref, bf16[1024,384]{1,0:T(8,128)(2,1)} %get-tuple-element.220.query_ref, bf16[1024,384]{1,0:T(8,128)(2,1)} %get-tuple-element.221.key_ref, bf16[1024,384]{1,0:T(8,128)(2,1)} %get-tuple-element.222.value_ref), custom_call_target="tpu_custom_call" | custom-call | flops 8589934592 | bytes 1310720 | tf_op jit(solution)/shard_map/attend_forward/pallas_call | solution.py:502
  80.1 6.6 %mix.1 = (bf16[768,384]{1,0:T(8,128)(2,1)}, bf16[768,1536]{1,0:T(8,128)(2,1)}, bf16[1024,896]{1,0:T(8,128)(2,1)}, f32[8,768]{1,0:T(8,128)}) custom-call(s32[16]{0:T(128)} %stack.113.order_ref, bf16[192,1920]{1,0:T(8,128)(2,1)} %copy-done.31, bf16[192,1920]{1,0:T(8,128)(2,1)} %copy-done.19, bf16[192,1920]{1,0:T(8,128)(2,1)} %copy-done.18, ...), custom_call_target="tpu_custom_call" | custom-call | flops 2415919104 | bytes 10616832 | tf_op jit(solution)/shard_map/mix/pallas_call | solution.py:615
  93.8 10.6 %feed_up.1 = (f32[1024,768]{1,0:T(8,128)}, bf16[768,1024]{1,0:T(8,128)(2,1)}, bf16[1024,1536]{1,0:T(8,128)(2,1)}, bf16[1024,1536]{1,0:T(8,128)(2,1)}) custom-call(bf16[1024,896]{1,0:T(8,128)(2,1)} %get-tuple-element.205.one, bf16[1024,896]{1,0:T(8,128)(2,1)} %copy-done, f32[8,768]{1,0:T(8,128)} %get-tuple-element.206.side_one, f32[8,768]{1,0:T(8,128)} %copy-done.38, ...), custom_call_target="tpu_custom_call" | custom-call | flops 9663676416 | bytes 18087936 | tf_op jit(solution)/shard_map/feed_up/pallas_call | solution.py:656
  105.1 8.3 %feed_down.1 = (bf16[768,1536]{1,0:T(8,128)(2,1)}, bf16[1024,896]{1,0:T(8,128)(2,1)}, f32[8,768]{1,0:T(8,128)}) custom-call(s32[16]{0:T(128)} %stack.113.order_ref, bf16[192,1536]{1,0:T(8,128)(2,1)} %constant_dynamic-update-slice_fusion.4.refs_0_, bf16[192,1536]{1,0:T(8,128)(2,1)} %copy-done.23, bf16[192,1536]{1,0:T(8,128)(2,1)} %copy-done.22, ...), custom_call_target="tpu_custom_call" | custom-call | flops 9663676416 | bytes 9437184 | tf_op jit(solution)/shard_map/feed_down/pallas_call | solution.py:708
  118.7 14.0 %feed_back.1 = (bf16[512,768]{1,0:T(8,128)(2,1)}, bf16[1024,1536]{1,0:T(8,128)(2,1)}, bf16[1024,1536]{1,0:T(8,128)(2,1)}, bf16[1024,768]{1,0:T(8,128)(2,1)}, f32[8,1536]{1,0:T(8,128)}) custom-call(s32[1]{0:T(128)} %bitcast.core_ref, bf16[1024,896]{1,0:T(8,128)(2,1)} %get-tuple-element.212.one, bf16[1024,896]{1,0:T(8,128)(2,1)} %copy-done.41, ...), custom_call_target="tpu_custom_call" | custom-call | flops 19327352832 | bytes 26738688 | tf_op jit(solution)/shard_map/feed_back/pallas_call | solution.py:790
  132.9 6.0 %weight_grad.6 = (bf16[384,1536]{1,0:T(8,128)(2,1)}, bf16[384,1536]{1,0:T(8,128)(2,1)}) custom-call(s32[16]{0:T(128)} %stack.119.order_ref, bf16[768,1024]{1,0:T(8,128)(2,1)} %get-tuple-element.242.refs_0_, bf16[1024,1536]{1,0:T(8,128)(2,1)} %get-tuple-element.243.refs_1_), custom_call_target="tpu_custom_call" | custom-call | flops 9663676416 | bytes 7077888 | tf_op jit(solution)/shard_map/weight_grad/pallas_call | solution.py:1079
  140.7 5.9 %weight_grad.5 = (bf16[384,1536]{1,0:T(8,128)(2,1)}, bf16[384,1536]{1,0:T(8,128)(2,1)}) custom-call(s32[16]{0:T(128)} %stack.118.order_ref, bf16[768,1024]{1,0:T(8,128)(2,1)} %get-tuple-element.237.refs_0_, bf16[1024,1536]{1,0:T(8,128)(2,1)} %get-tuple-element.238.refs_1_), custom_call_target="tpu_custom_call" | custom-call | flops 9663676416 | bytes 7077888 | tf_op jit(solution)/shard_map/weight_grad/pallas_call | solution.py:1079
  148.2 10.7 %mix_back.1 = (f32[1024,768]{1,0:T(8,128)}, bf16[768,1024]{1,0:T(8,128)(2,1)}, bf16[1024,384]{1,0:T(8,128)(2,1)}, bf16[1024,384]{1,0:T(8,128)(2,1)}, f32[8,768]{1,0:T(8,128)}, /*index=5*/f32[8,384]{1,0:T(8,128)}) custom-call(bf16[1024,768]{1,0:T(8,128)(2,1)} %get-tuple-element.223.back_one, bf16[1024,768]{1,0:T(8,128)(2,1)} %copy-done.1, ...), custom_call_target="tpu_custom_call" | custom-call | flops 2415919104 | bytes 19464192 | tf_op jit(solution)/shard_map/mix_back/pallas_call | solution.py:898
  158.9 8.0 %attend_backward.4 = (bf16[1024,128]{1,0:T(8,128)(2,1)}, bf16[1024,128]{1,0:T(8,128)(2,1)}, bf16[1024,128]{1,0:T(8,128)(2,1)}) custom-call(s32[1]{0:T(128)S(6)} %copy.29.prefix_ref, bf16[1024,384]{1,0:T(8,128)(2,1)} %get-tuple-element.220.query_ref, bf16[1024,384]{1,0:T(8,128)(2,1)} %get-tuple-element.221.key_ref, ...), custom_call_target="tpu_custom_call" | custom-call | flops 21474836480 | bytes 2359296 | tf_op jit(solution)/shard_map/attend_backward/pallas_call | solution.py:577
  166.9 8.1 %attend_backward.3 = (bf16[1024,128]{1,0:T(8,128)(2,1)}, bf16[1024,128]{1,0:T(8,128)(2,1)}, bf16[1024,128]{1,0:T(8,128)(2,1)}) custom-call(s32[1]{0:T(128)S(6)} %copy.29.prefix_ref, bf16[1024,384]{1,0:T(8,128)(2,1)} %get-tuple-element.220.query_ref, bf16[1024,384]{1,0:T(8,128)(2,1)} %get-tuple-element.221.key_ref, ...), custom_call_target="tpu_custom_call" | custom-call | flops 21474836480 | bytes 2359296 | tf_op jit(solution)/shard_map/attend_backward/pallas_call | solution.py:577
  179.8 4.9 %weight_grad.7 = (bf16[384,768]{1,0:T(8,128)(2,1)}, bf16[384,768]{1,0:T(8,128)(2,1)}) custom-call(s32[16]{0:T(128)} %stack.119.order_ref, bf16[768,1024]{1,0:T(8,128)(2,1)} %get-tuple-element.232.refs_0_, bf16[1024,128]{1,0:T(8,128)(2,1)} %get-tuple-element.267.refs_1_.refs_0_, bf16[1024,128]{1,0:T(8,128)(2,1)} %get-tuple-element.268.refs_2_.refs_1_, ...), custom_call_target="tpu_custom_call" | custom-call | flops 4831838208 | bytes 4325376 | tf_op jit(solution)/shard_map/weight_grad/pallas_call | solution.py:1079
  184.7 3.4 %weight_grad.8 = (bf16[384,384]{1,0:T(8,128)(2,1)}, bf16[384,384]{1,0:T(8,128)(2,1)}) custom-call(s32[16]{0:T(128)} %stack.118.order_ref, bf16[768,1024]{1,0:T(8,128)(2,1)} %get-tuple-element.230.refs_0_, bf16[1024,384]{1,0:T(8,128)(2,1)} %get-tuple-element.254.refs_1_), custom_call_target="tpu_custom_call" | custom-call | flops 2415919104 | bytes 2949120 | tf_op jit(solution)/shard_map/weight_grad/pallas_call | solution.py:1079
  190.1 8.0 %attend_backward.5 = (bf16[1024,128]{1,0:T(8,128)(2,1)}, bf16[1024,128]{1,0:T(8,128)(2,1)}, bf16[1024,128]{1,0:T(8,128)(2,1)}) custom-call(s32[1]{0:T(128)S(6)} %copy.29.prefix_ref, bf16[1024,384]{1,0:T(8,128)(2,1)} %get-tuple-element.220.query_ref, bf16[1024,384]{1,0:T(8,128)(2,1)} %get-tuple-element.221.key_ref, ...), custom_call_target="tpu_custom_call" | custom-call | flops 21474836480 | bytes 2359296 | tf_op jit(solution)/shard_map/attend_backward/pallas_call | solution.py:577
  202.3 3.8 %collective-permute-start.36 = (bf16[48,3072]{1,0:T(8,128)(2,1)}, bf16[48,3072]{1,0:T(8,128)(2,1)S(1)}, u32[]{:S(2)}, u32[]{:S(2)}) collective-permute-start(bf16[48,3072]{1,0:T(8,128)(2,1)} %get-tuple-element.266), channel_id=1, source_target_pairs={{0,24},{2,26},{4,28},{6,30},{8,0},{10,2},{12,4},{14,6},{16,8},{18,... | collective-permute-start | bytes 884744 | tf_op jit(solution)/shard_map/ppermute | solution.py:68
  206.1 6.6 %project_back.1 = (bf16[512,768]{1,0:T(8,128)(2,1)}, f32[512,768]{1,0:T(8,128)}, f32[8,384]{1,0:T(8,128)}) custom-call(s32[1]{0:T(128)} %bitcast.core_ref, bf16[1024,128]{1,0:T(8,128)(2,1)} %get-tuple-element.267.refs_1_.refs_0_, bf16[1024,128]{1,0:T(8,128)(2,1)} %get-tuple-element.268.refs_2_.refs_1_, bf16[1024,128]{1,0:T(8,128)(2,1)} %get-tuple-element.280.refs_2_.refs_1_, ...), custom_call_target="tpu_custom_call" | custom-call | flops 7247757312 | bytes 8847360 | tf_op jit(solution)/shard_map/project_back/pallas_call | solution.py:982
  212.9 3.5 %weight_grad.9 = (bf16[384,384]{1,0:T(8,128)(2,1)}, bf16[384,384]{1,0:T(8,128)(2,1)}) custom-call(s32[16]{0:T(128)} %stack.119.order_ref, bf16[768,1024]{1,0:T(8,128)(2,1)} %get-tuple-element.232.refs_0_, bf16[1024,128]{1,0:T(8,128)(2,1)} %get-tuple-element.280.refs_2_.refs_1_, bf16[1024,128]{1,0:T(8,128)(2,1)} %get-tuple-element.281.refs_5_.refs_2_, ...), custom_call_target="tpu_custom_call" | custom-call | flops 2415919104 | bytes 2949120 | tf_op jit(solution)/shard_map/weight_grad/pallas_call | solution.py:1079
  222.7 3.9 %input_back.1 = (f32[512,768]{1,0:T(8,128)}, f32[8,768]{1,0:T(8,128)}) custom-call(s32[1]{0:T(128)} %bitcast.core_ref, bf16[512,768]{1,0:T(8,128)(2,1)} %copy-done.4, f32[512,768]{1,0:T(8,128)} %get-tuple-element.287.own, f32[1024,768]{1,0:T(8,128)} %get-tuple-element.288.mid, bf16[512,768]{1,0:T(8,128)(2,1)} %x.1, f32[6,768]{1,0:T(8,128)} %model.7), custom_call_target="tpu_custom_call" | custom-call | flops 15728640 | bytes 6291456 | tf_op jit(solution)/shard_map/input_back/pallas_call | solution.py:1020
  234.2 3.8 %collective-permute-start.51 = (f32[84,128]{1,0:T(8,128)}, f32[84,128]{1,0:T(8,128)S(1)}, u32[]{:S(2)}, u32[]{:S(2)}) collective-permute-start(f32[84,128]{1,0:T(8,128)} %pack.1), channel_id=1, source_target_pairs={{0,24},{2,26},{4,28},{6,30},{8,0},{10,2},{12,4},{14,6},{16,8},{18,... | collective-permute-start | bytes 129032 | tf_op jit(solution)/shard_map/ppermute | solution.py:68
  240.7 7.3 %collective-permute-start.40 = (bf16[48,1152]{1,0:T(8,128)(2,1)}, bf16[48,1152]{1,0:T(8,128)(2,1)S(1)}, u32[]{:S(2)}, u32[]{:S(2)}) collective-permute-start(bf16[48,1152]{1,0:T(8,128)(2,1)} %get-tuple-element.294), channel_id=1, source_target_pairs={{0,16},{2,18},{4,20},{6,22},{8,24},{10,26},{12,28},{14,30},{16,0},... | collective-permute-start | bytes 331784 | tf_op jit(solution)/shard_map/ppermute | solution.py:68
  (241 shorter events, 110.0 us)
Async XLA Ops:
  2.7 13.1 %collective-permute-start.2 = (bf16[48,1152]{1,0:T(8,128)(2,1)}, bf16[48,1152]{1,0:T(8,128)(2,1)S(1)}, u32[]{:S(2)}, u32[]{:S(2)}) collective-permute-start(bf16[48,1152]{1,0:T(8,128)(2,1)} %join.3), channel_id=1, source_target_pairs={{0,24},{2,26},{4,28},{6,30},{8,0},{10,2},{12,4},{14,6},{16,8},{18,... | collective-permute-start | bytes 331784 | tf_op jit(solution)/shard_map/ppermute | solution.py:68
  24.7 19.0 %collective-permute-start.7 = (bf16[48,1920]{1,0:T(8,128)(2,1)}, bf16[48,1920]{1,0:T(8,128)(2,1)S(1)}, u32[]{:S(2)}, u32[]{:S(2)}) collective-permute-start(bf16[48,1920]{1,0:T(8,128)(2,1)} %join.2), channel_id=1, source_target_pairs={{0,24},{2,26},{4,28},{6,30},{8,0},{10,2},{12,4},{14,6},{16,8},{18,... | collective-permute-start | bytes 552968 | tf_op jit(solution)/shard_map/ppermute | solution.py:68
  26.3 17.4 %collective-permute-start.6 = (bf16[48,1920]{1,0:T(8,128)(2,1)}, bf16[48,1920]{1,0:T(8,128)(2,1)S(1)}, u32[]{:S(2)}, u32[]{:S(2)}) collective-permute-start(bf16[48,1920]{1,0:T(8,128)(2,1)} %join.2), channel_id=1, source_target_pairs={{0,16},{2,18},{4,20},{6,22},{8,24},{10,26},{12,28},{14,30},{16,0},... | collective-permute-start | bytes 552968 | tf_op jit(solution)/shard_map/ppermute | solution.py:68
  27.0 16.8 %collective-permute-start.5 = (bf16[48,1920]{1,0:T(8,128)(2,1)}, bf16[48,1920]{1,0:T(8,128)(2,1)S(1)}, u32[]{:S(2)}, u32[]{:S(2)}) collective-permute-start(bf16[48,1920]{1,0:T(8,128)(2,1)} %join.2), channel_id=1, source_target_pairs={{0,8},{2,10},{4,12},{6,14},{8,16},{10,18},{12,20},{14,22},{16,24},... | collective-permute-start | bytes 552968 | tf_op jit(solution)/shard_map/ppermute | solution.py:68
  43.8 13.5 %collective-permute-start.14 = (bf16[48,1536]{1,0:T(8,128)(2,1)S(1)}, bf16[48,1536]{1,0:T(8,128)(2,1)S(1)}, u32[]{:S(2)}, u32[]{:S(2)}) collective-permute-start(bf16[48,1536]{1,0:T(8,128)(2,1)S(1)} %copy-done.24), channel_id=1, source_target_pairs={{0,24},{2,26},{4,28},{6,30},{8,0},{10,2},{12,4},{14,6},{16,8},{18,... | collective-permute-start | bytes 442376 | tf_op jit(solution)/shard_map/ppermute | solution.py:68
  44.6 21.4 %collective-permute-start.13 = (bf16[48,1536]{1,0:T(8,128)(2,1)S(1)}, bf16[48,1536]{1,0:T(8,128)(2,1)S(1)}, u32[]{:S(2)}, u32[]{:S(2)}) collective-permute-start(bf16[48,1536]{1,0:T(8,128)(2,1)S(1)} %copy-done.24), channel_id=1, source_target_pairs={{0,16},{2,18},{4,20},{6,22},{8,24},{10,26},{12,28},{14,30},{16,0},... | collective-permute-start | bytes 442376 | tf_op jit(solution)/shard_map/ppermute | solution.py:68
  48.4 16.2 %collective-permute-start.16 = (bf16[192,1920]{1,0:T(8,128)(2,1)S(1)}, bf16[192,1920]{1,0:T(8,128)(2,1)S(1)}, u32[]{:S(2)}, u32[]{:S(2)}) collective-permute-start(bf16[192,1920]{1,0:T(8,128)(2,1)S(1)} %constant_dynamic-update-slice_fusion.refs_0_), channel_id=1, source_target_pairs={{0,4},{2,6},{4,0},{6,2},{8,12},{10,14},{12,8},{14,10},{16,20},{18,... | collective-permute-start | bytes 2211848 | tf_op jit(solution)/shard_map/ppermute | solution.py:68
  50.0 16.0 %collective-permute-start.15 = (bf16[192,1920]{1,0:T(8,128)(2,1)S(1)}, bf16[192,1920]{1,0:T(8,128)(2,1)S(1)}, u32[]{:S(2)}, u32[]{:S(2)}) collective-permute-start(bf16[192,1920]{1,0:T(8,128)(2,1)S(1)} %constant_dynamic-update-slice_fusion.refs_0_), channel_id=1, source_target_pairs={{0,2},{2,0},{4,6},{6,4},{8,10},{10,8},{12,14},{14,12},{16,18},{18,... | collective-permute-start | bytes 2211848 | tf_op jit(solution)/shard_map/ppermute | solution.py:68
  89.0 15.4 %collective-permute-start.22 = (bf16[96,1536]{1,0:T(8,128)(2,1)S(1)}, bf16[96,1536]{1,0:T(8,128)(2,1)S(1)}, u32[]{:S(2)}, u32[]{:S(2)}) collective-permute-start(bf16[96,1536]{1,0:T(8,128)(2,1)S(1)} %slice.91), channel_id=1, source_target_pairs={{0,2},{2,0},{4,6},{6,4},{8,10},{10,8},{12,14},{14,12},{16,18},{18,... | collective-permute-start | bytes 884744 | tf_op jit(solution)/shard_map/ppermute | solution.py:68
  90.8 13.6 %collective-permute-start.21 = (bf16[96,1536]{1,0:T(8,128)(2,1)S(1)}, bf16[96,1536]{1,0:T(8,128)(2,1)}, u32[]{:S(2)}, u32[]{:S(2)}) collective-permute-start(bf16[96,1536]{1,0:T(8,128)(2,1)S(1)} %slice.90), channel_id=1, source_target_pairs={{0,4},{2,6},{4,0},{6,2},{8,12},{10,14},{12,8},{14,10},{16,20},{18,... | collective-permute-start | bytes 884744 | tf_op jit(solution)/shard_map/ppermute | solution.py:68
  132.7 14.4 %collective-permute-start.27 = (bf16[1024,768]{1,0:T(8,128)(2,1)}, bf16[1024,768]{1,0:T(8,128)(2,1)S(1)}, u32[]{:S(2)}, u32[]{:S(2)}) collective-permute-start(bf16[1024,768]{1,0:T(8,128)(2,1)} %get-tuple-element.223.back_one), channel_id=1, source_target_pairs={{0,1},{1,0},{2,3},{3,2},{4,5},{5,4},{6,7},{7,6},{8,9},{9,8},{10,11... | collective-permute-start | bytes 4718600 | tf_op jit(solution)/shard_map/ppermute | solution.py:26
  138.9 36.0 %collective-permute-start.29 = (bf16[384,1536]{1,0:T(8,128)(2,1)}, bf16[384,1536]{1,0:T(8,128)(2,1)S(1)}, u32[]{:S(2)}, u32[]{:S(2)}) collective-permute-start(bf16[384,1536]{1,0:T(8,128)(2,1)} %get-tuple-element.245), channel_id=1, source_target_pairs={{0,2},{2,0},{4,6},{6,4},{8,10},{10,8},{12,14},{14,12},{16,18},{18,... | collective-permute-start | bytes 3538952 | tf_op jit(solution)/shard_map/ppermute | solution.py:68
  146.6 28.4 %collective-permute-start.28 = (bf16[384,1536]{1,0:T(8,128)(2,1)}, bf16[384,1536]{1,0:T(8,128)(2,1)S(1)}, u32[]{:S(2)}, u32[]{:S(2)}) collective-permute-start(bf16[384,1536]{1,0:T(8,128)(2,1)} %get-tuple-element.240), channel_id=1, source_target_pairs={{0,4},{2,6},{4,0},{6,2},{8,12},{10,14},{12,8},{14,10},{16,20},{18,... | collective-permute-start | bytes 3538952 | tf_op jit(solution)/shard_map/ppermute | solution.py:68
  176.5 21.6 %collective-permute-start.31 = (bf16[192,1536]{1,0:T(8,128)(2,1)}, bf16[192,1536]{1,0:T(8,128)(2,1)S(1)}, u32[]{:S(2)}, u32[]{:S(2)}) collective-permute-start(bf16[192,1536]{1,0:T(8,128)(2,1)} %get-tuple-element.320), channel_id=1, source_target_pairs={{0,2},{2,0},{4,6},{6,4},{8,10},{10,8},{12,14},{14,12},{16,18},{18,... | collective-permute-start | bytes 1769480 | tf_op jit(solution)/shard_map/ppermute | solution.py:68
  179.5 18.6 %collective-permute-start.30 = (bf16[192,1536]{1,0:T(8,128)(2,1)S(1)}, bf16[192,1536]{1,0:T(8,128)(2,1)S(1)}, u32[]{:S(2)}, u32[]{:S(2)}) collective-permute-start(bf16[192,1536]{1,0:T(8,128)(2,1)S(1)} %get-tuple-element.322), channel_id=1, source_target_pairs={{0,4},{2,6},{4,0},{6,2},{8,12},{10,14},{12,8},{14,10},{16,20},{18,... | collective-permute-start | bytes 1769480 | tf_op jit(solution)/shard_map/ppermute | solution.py:68
  188.1 28.3 %collective-permute-start.34 = (bf16[384,384]{1,0:T(8,128)(2,1)}, bf16[384,384]{1,0:T(8,128)(2,1)S(1)}, u32[]{:S(2)}, u32[]{:S(2)}) collective-permute-start(bf16[384,384]{1,0:T(8,128)(2,1)} %get-tuple-element.255), channel_id=1, source_target_pairs={{0,4},{2,6},{4,0},{6,2},{8,12},{10,14},{12,8},{14,10},{16,20},{18,... | collective-permute-start | bytes 884744 | tf_op jit(solution)/shard_map/ppermute | solution.py:68
  189.9 28.3 %collective-permute-start.33 = (bf16[384,768]{1,0:T(8,128)(2,1)}, bf16[384,768]{1,0:T(8,128)(2,1)S(1)}, u32[]{:S(2)}, u32[]{:S(2)}) collective-permute-start(bf16[384,768]{1,0:T(8,128)(2,1)} %get-tuple-element.253), channel_id=1, source_target_pairs={{0,2},{2,0},{4,6},{6,4},{8,10},{10,8},{12,14},{14,12},{16,18},{18,... | collective-permute-start | bytes 1769480 | tf_op jit(solution)/shard_map/ppermute | solution.py:68
  202.3 15.9 %collective-permute-start.35 = (bf16[48,3072]{1,0:T(8,128)(2,1)}, bf16[48,3072]{1,0:T(8,128)(2,1)S(1)}, u32[]{:S(2)}, u32[]{:S(2)}) collective-permute-start(bf16[48,3072]{1,0:T(8,128)(2,1)} %get-tuple-element.264), channel_id=1, source_target_pairs={{0,8},{2,10},{4,12},{6,14},{8,16},{10,18},{12,20},{14,22},{16,24},... | collective-permute-start | bytes 884744 | tf_op jit(solution)/shard_map/ppermute | solution.py:68
  202.3 15.9 %collective-permute-start.36 = (bf16[48,3072]{1,0:T(8,128)(2,1)}, bf16[48,3072]{1,0:T(8,128)(2,1)S(1)}, u32[]{:S(2)}, u32[]{:S(2)}) collective-permute-start(bf16[48,3072]{1,0:T(8,128)(2,1)} %get-tuple-element.266), channel_id=1, source_target_pairs={{0,24},{2,26},{4,28},{6,30},{8,0},{10,2},{12,4},{14,6},{16,8},{18,... | collective-permute-start | bytes 884744 | tf_op jit(solution)/shard_map/ppermute | solution.py:68
  226.8 26.7 %collective-permute-start.47 = (bf16[48,3072]{1,0:T(8,128)(2,1)S(1)}, bf16[48,3072]{1,0:T(8,128)(2,1)S(1)}, u32[]{:S(2)}, u32[]{:S(2)}) collective-permute-start(bf16[48,3072]{1,0:T(8,128)(2,1)S(1)} %copy-done.44), channel_id=1, source_target_pairs={{0,16},{2,18},{4,20},{6,22},{8,24},{10,26},{12,28},{14,30},{16,0},... | collective-permute-start | bytes 884744 | tf_op jit(solution)/shard_map/ppermute | solution.py:68
  232.0 23.0 %collective-permute-start.39 = (bf16[48,1152]{1,0:T(8,128)(2,1)}, bf16[48,1152]{1,0:T(8,128)(2,1)S(1)}, u32[]{:S(2)}, u32[]{:S(2)}) collective-permute-start(bf16[48,1152]{1,0:T(8,128)(2,1)} %get-tuple-element.293), channel_id=1, source_target_pairs={{0,8},{2,10},{4,12},{6,14},{8,16},{10,18},{12,20},{14,22},{16,24},... | collective-permute-start | bytes 331784 | tf_op jit(solution)/shard_map/ppermute | solution.py:68
  238.0 13.3 %collective-permute-start.49 = (f32[84,128]{1,0:T(8,128)}, f32[84,128]{1,0:T(8,128)S(1)}, u32[]{:S(2)}, u32[]{:S(2)}) collective-permute-start(f32[84,128]{1,0:T(8,128)} %pack.1), channel_id=1, source_target_pairs={{0,8},{2,10},{4,12},{6,14},{8,16},{10,18},{12,20},{14,22},{16,24},... | collective-permute-start | bytes 129032 | tf_op jit(solution)/shard_map/ppermute | solution.py:68
  240.7 27.4 %collective-permute-start.40 = (bf16[48,1152]{1,0:T(8,128)(2,1)}, bf16[48,1152]{1,0:T(8,128)(2,1)S(1)}, u32[]{:S(2)}, u32[]{:S(2)}) collective-permute-start(bf16[48,1152]{1,0:T(8,128)(2,1)} %get-tuple-element.294), channel_id=1, source_target_pairs={{0,16},{2,18},{4,20},{6,22},{8,24},{10,26},{12,28},{14,30},{16,0},... | collective-permute-start | bytes 331784 | tf_op jit(solution)/shard_map/ppermute | solution.py:68
  249.3 18.8 %collective-permute-start.41 = (bf16[48,1152]{1,0:T(8,128)(2,1)}, bf16[48,1152]{1,0:T(8,128)(2,1)S(1)}, u32[]{:S(2)}, u32[]{:S(2)}) collective-permute-start(bf16[48,1152]{1,0:T(8,128)(2,1)} %get-tuple-element.295), channel_id=1, source_target_pairs={{0,24},{2,26},{4,28},{6,30},{8,0},{10,2},{12,4},{14,6},{16,8},{18,... | collective-permute-start | bytes 331784 | tf_op jit(solution)/shard_map/ppermute | solution.py:68
  (80 other events, 505.3 us)

commit v5 on v4

--- a/solution.py
+++ b/solution.py
@@ -1257,22 +1257,22 @@
     model_sum, head_sum, hidden_sum = unpack(
         [packed, *ring.around_square(packed)], ((6, features), (4, half), (3, full))
     )
-    early_parts = square_end(
-        (early_own, out_own),
-        after((early_second, out_second), input_grad),
+    narrow_parts = square_end(
+        (early_own, out_own, late_own),
+        after((early_second, out_second, late_second), input_grad),
         ring.lines[0][0],
     )
-    early_got = ring.start_lines(early_parts)
-    late_parts = square_end((late_own,), (late_second,), ring.lines[0][0])
-    late_got = ring.start_lines(late_parts)
+    narrow_got = ring.start_lines(narrow_parts)
     wide_terms = ring.last_terms(wide_parts, wide_got)
-    early_terms = ring.last_terms(early_parts, early_got)
-    late_terms = ring.last_terms(late_parts, late_got)
+    narrow_terms = ring.last_terms(narrow_parts, narrow_got)
     up_grad, down_grad = finish([wide_terms], [[(0, 0, full)], [(0, full, full)]])
     early = last_pair * PAIR
     query_weight_grad, key_weight_grad, value_weight_grad, out_grad = finish(
-        [early_terms, late_terms],
-        [[(0, at * early, early), (1, at * PAIR, PAIR)] for at in range(3)]
+        [narrow_terms],
+        [
+            [(0, at * early, early), (0, 3 * early + half + at * PAIR, PAIR)]
+            for at in range(3)
+        ]
         + [[(0, 3 * early, half)]],
     )
     return (

time: 275 us -> 273 us (level)
    ppermute x45 -> x42, starting transfers between devices: 64.7 us -> 55.6 us  [shift(): return lax.ppermute(values, 'dp', pairs)]
    ppermute x1, starting transfers between devices: 1.52 us -> 9.32 us  [around_square(): lax.ppermute(values, 'dp', pairs)]
    pallas_call x3 -> x2, Pallas kernels: 6.95 us -> 5.45 us  [square_end(): pl.pallas_call(body, out_shape=[shape_of((rows, width), f32)] + [shape_of...]
    unnamed x104 -> x100, local copies, waits for them, and re-layouts: 13.3 us -> 14.1 us
    ppermute x45 -> x42, waiting for transfers between devices: 18.3 us -> 17.9 us  [shift(): return lax.ppermute(values, 'dp', pairs)]
  transfers between devices with their start and end apart: 55 -> 52, of which waited for: 15 -> 14; matrix products, arithmetic and copies ran while one was open for 3% -> 3% of each run, Pallas kernels for 49% -> 48%
where the time goes in v5:
time: 273 us; the launch traced here: 269 us
  Pallas kernels  154 us (56%)
  starting transfers between devices  66.9 us (25%)
  waiting for transfers between devices  22.6 us (8%)
  local copies, waits for them, and re-layouts  17.5 us (6%)
  other arithmetic  5.42 us (2%)
    ppermute x42, starting transfers between devices, shift(): return lax.ppermute(values, 'dp', pairs)  55.6 us
    pallas_call x3, Pallas kernels, attend_backward(): pl.pallas_call(body, grid=(1,), out_shape=[shape_of((length, PAIR), bf16)...  24.1 us
    pallas_call x5, Pallas kernels, weight_grad(): pl.pallas_call(body, grid=(width // tile,), out_shape=[shape_of((features...  23.8 us
    pallas_call x3, Pallas kernels, attend_forward(): pl.pallas_call(body, grid=(1,), out_shape=[shape_of((length, PAIR), f32),...  18.8 us
    ppermute x42, waiting for transfers between devices, shift(): return lax.ppermute(values, 'dp', pairs)  17.9 us
    unnamed x100, local copies, waits for them, and re-layouts  14.1 us
    pallas_call x1, Pallas kernels, feed_back(): pl.pallas_call(body, grid_spec=pltpu.PrefetchScalarGridSpec(num_scalar_pr...  14 us
    pallas_call x1, Pallas kernels, feed_up(): pl.pallas_call(body, grid=(TILES,), out_shape=[shape_of((length, features...  10.6 us
  transfers between devices with their start and end apart: 52, of which 14 were waited for; matrix products, arithmetic and copies ran while one was open for 3% of the time, Pallas kernels for 48%

profile of v5, /device:TPU:0, one launch (start us, length us, event | category | flops | bytes accessed | tf_op | source)
XLA Modules:
  0.0 269.1 jit_solution(7359851117639388586)
XLA Ops:
  2.7 5.0 %collective-permute-start.2 = (bf16[48,1152]{1,0:T(8,128)(2,1)}, bf16[48,1152]{1,0:T(8,128)(2,1)S(1)}, u32[]{:S(2)}, u32[]{:S(2)}) collective-permute-start(bf16[48,1152]{1,0:T(8,128)(2,1)} %join.3), channel_id=1, source_target_pairs={{0,24},{2,26},{4,28},{6,30},{8,0},{10,2},{12,4},{14,6},{16,8},{18,... | collective-permute-start | bytes 331784 | tf_op jit(solution)/shard_map/ppermute | solution.py:68
  9.9 5.9 %prepare.1 = (bf16[1024,768]{1,0:T(8,128)(2,1)}, bf16[1024,768]{1,0:T(8,128)(2,1)}, bf16[1024,768]{1,0:T(8,128)(2,1)}, bf16[768,1024]{1,0:T(8,128)(2,1)}, bf16[768,1024]{1,0:T(8,128)(2,1)}, /*index=5*/f32[8,768]{1,0:T(8,128)}) custom-call(s32[1]{0:T(128)} %bitcast.core_ref, bf16[512,768]{1,0:T(8,128)(2,1)} %x.1, bf16[512,768]{1,0:T(8,128)(2,1)} %copy-done.6, ...), custom_call_target="tpu_custom_call" | custom-call | flops 31457280 | bytes 11010048 | tf_op jit(solution)/shard_map/prepare/pallas_call | solution.py:396
  38.0 5.7 %project.1 = (bf16[768,1152]{1,0:T(8,128)(2,1)}, bf16[1024,384]{1,0:T(8,128)(2,1)}, bf16[1024,384]{1,0:T(8,128)(2,1)}, bf16[1024,384]{1,0:T(8,128)(2,1)}) custom-call(s32[16]{0:T(128)} %stack.113.order_ref, bf16[192,1152]{1,0:T(8,128)(2,1)} %copy-done.10, bf16[192,1152]{1,0:T(8,128)(2,1)} %copy-done.31, bf16[192,1152]{1,0:T(8,128)(2,1)} %copy-done.30, ...), custom_call_target="tpu_custom_call" | custom-call | flops 7247757312 | bytes 7471104 | tf_op jit(solution)/shard_map/project/pallas_call | solution.py:451
  50.5 6.2 %attend_forward.3 = (f32[1024,128]{1,0:T(8,128)}, f32[8,1024]{1,0:T(8,128)}) custom-call(s32[1]{0:T(128)S(6)} %copy.29.prefix_ref, bf16[1024,384]{1,0:T(8,128)(2,1)} %get-tuple-element.217.query_ref, bf16[1024,384]{1,0:T(8,128)(2,1)} %get-tuple-element.218.key_ref, bf16[1024,384]{1,0:T(8,128)(2,1)} %get-tuple-element.219.value_ref), custom_call_target="tpu_custom_call" | custom-call | flops 8589934592 | bytes 1310720 | tf_op jit(solution)/shard_map/attend_forward/pallas_call | solution.py:502
  57.4 6.2 %attend_forward.4 = (f32[1024,128]{1,0:T(8,128)}, f32[8,1024]{1,0:T(8,128)}) custom-call(s32[1]{0:T(128)S(6)} %copy.29.prefix_ref, bf16[1024,384]{1,0:T(8,128)(2,1)} %get-tuple-element.217.query_ref, bf16[1024,384]{1,0:T(8,128)(2,1)} %get-tuple-element.218.key_ref, bf16[1024,384]{1,0:T(8,128)(2,1)} %get-tuple-element.219.value_ref), custom_call_target="tpu_custom_call" | custom-call | flops 8589934592 | bytes 1310720 | tf_op jit(solution)/shard_map/attend_forward/pallas_call | solution.py:502
  67.8 6.4 %attend_forward.5 = (f32[1024,128]{1,0:T(8,128)}, f32[8,1024]{1,0:T(8,128)}) custom-call(s32[1]{0:T(128)S(6)} %copy.29.prefix_ref, bf16[1024,384]{1,0:T(8,128)(2,1)} %get-tuple-element.217.query_ref, bf16[1024,384]{1,0:T(8,128)(2,1)} %get-tuple-element.218.key_ref, bf16[1024,384]{1,0:T(8,128)(2,1)} %get-tuple-element.219.value_ref), custom_call_target="tpu_custom_call" | custom-call | flops 8589934592 | bytes 1310720 | tf_op jit(solution)/shard_map/attend_forward/pallas_call | solution.py:502
  80.0 6.6 %mix.1 = (bf16[768,384]{1,0:T(8,128)(2,1)}, bf16[768,1536]{1,0:T(8,128)(2,1)}, bf16[1024,896]{1,0:T(8,128)(2,1)}, f32[8,768]{1,0:T(8,128)}) custom-call(s32[16]{0:T(128)} %stack.113.order_ref, bf16[192,1920]{1,0:T(8,128)(2,1)} %copy-done.32, bf16[192,1920]{1,0:T(8,128)(2,1)} %copy-done.19, bf16[192,1920]{1,0:T(8,128)(2,1)} %copy-done.18, ...), custom_call_target="tpu_custom_call" | custom-call | flops 2415919104 | bytes 10616832 | tf_op jit(solution)/shard_map/mix/pallas_call | solution.py:615
  93.7 10.6 %feed_up.1 = (f32[1024,768]{1,0:T(8,128)}, bf16[768,1024]{1,0:T(8,128)(2,1)}, bf16[1024,1536]{1,0:T(8,128)(2,1)}, bf16[1024,1536]{1,0:T(8,128)(2,1)}) custom-call(bf16[1024,896]{1,0:T(8,128)(2,1)} %get-tuple-element.202.one, bf16[1024,896]{1,0:T(8,128)(2,1)} %copy-done, f32[8,768]{1,0:T(8,128)} %get-tuple-element.203.side_one, f32[8,768]{1,0:T(8,128)} %copy-done.36, ...), custom_call_target="tpu_custom_call" | custom-call | flops 9663676416 | bytes 18087936 | tf_op jit(solution)/shard_map/feed_up/pallas_call | solution.py:656
  105.0 8.3 %feed_down.1 = (bf16[768,1536]{1,0:T(8,128)(2,1)}, bf16[1024,896]{1,0:T(8,128)(2,1)}, f32[8,768]{1,0:T(8,128)}) custom-call(s32[16]{0:T(128)} %stack.113.order_ref, bf16[192,1536]{1,0:T(8,128)(2,1)} %constant_dynamic-update-slice_fusion.4.refs_0_, bf16[192,1536]{1,0:T(8,128)(2,1)} %copy-done.25, bf16[192,1536]{1,0:T(8,128)(2,1)} %copy-done.24, ...), custom_call_target="tpu_custom_call" | custom-call | flops 9663676416 | bytes 9437184 | tf_op jit(solution)/shard_map/feed_down/pallas_call | solution.py:708
  118.6 14.0 %feed_back.1 = (bf16[512,768]{1,0:T(8,128)(2,1)}, bf16[1024,1536]{1,0:T(8,128)(2,1)}, bf16[1024,1536]{1,0:T(8,128)(2,1)}, bf16[1024,768]{1,0:T(8,128)(2,1)}, f32[8,1536]{1,0:T(8,128)}) custom-call(s32[1]{0:T(128)} %bitcast.core_ref, bf16[1024,896]{1,0:T(8,128)(2,1)} %get-tuple-element.209.one, bf16[1024,896]{1,0:T(8,128)(2,1)} %copy-done.39, ...), custom_call_target="tpu_custom_call" | custom-call | flops 19327352832 | bytes 26738688 | tf_op jit(solution)/shard_map/feed_back/pallas_call | solution.py:790
  132.8 6.0 %weight_grad.6 = (bf16[384,1536]{1,0:T(8,128)(2,1)}, bf16[384,1536]{1,0:T(8,128)(2,1)}) custom-call(s32[16]{0:T(128)} %stack.119.order_ref, bf16[768,1024]{1,0:T(8,128)(2,1)} %get-tuple-element.239.refs_0_, bf16[1024,1536]{1,0:T(8,128)(2,1)} %get-tuple-element.240.refs_1_), custom_call_target="tpu_custom_call" | custom-call | flops 9663676416 | bytes 7077888 | tf_op jit(solution)/shard_map/weight_grad/pallas_call | solution.py:1079
  140.7 5.9 %weight_grad.5 = (bf16[384,1536]{1,0:T(8,128)(2,1)}, bf16[384,1536]{1,0:T(8,128)(2,1)}) custom-call(s32[16]{0:T(128)} %stack.118.order_ref, bf16[768,1024]{1,0:T(8,128)(2,1)} %get-tuple-element.234.refs_0_, bf16[1024,1536]{1,0:T(8,128)(2,1)} %get-tuple-element.235.refs_1_), custom_call_target="tpu_custom_call" | custom-call | flops 9663676416 | bytes 7077888 | tf_op jit(solution)/shard_map/weight_grad/pallas_call | solution.py:1079
  148.2 10.4 %mix_back.1 = (f32[1024,768]{1,0:T(8,128)}, bf16[768,1024]{1,0:T(8,128)(2,1)}, bf16[1024,384]{1,0:T(8,128)(2,1)}, bf16[1024,384]{1,0:T(8,128)(2,1)}, f32[8,768]{1,0:T(8,128)}, /*index=5*/f32[8,384]{1,0:T(8,128)}) custom-call(bf16[1024,768]{1,0:T(8,128)(2,1)} %get-tuple-element.220.back_one, bf16[1024,768]{1,0:T(8,128)(2,1)} %copy-done.1, ...), custom_call_target="tpu_custom_call" | custom-call | flops 2415919104 | bytes 19464192 | tf_op jit(solution)/shard_map/mix_back/pallas_call | solution.py:898
  158.6 8.0 %attend_backward.4 = (bf16[1024,128]{1,0:T(8,128)(2,1)}, bf16[1024,128]{1,0:T(8,128)(2,1)}, bf16[1024,128]{1,0:T(8,128)(2,1)}) custom-call(s32[1]{0:T(128)S(6)} %copy.29.prefix_ref, bf16[1024,384]{1,0:T(8,128)(2,1)} %get-tuple-element.217.query_ref, bf16[1024,384]{1,0:T(8,128)(2,1)} %get-tuple-element.218.key_ref, ...), custom_call_target="tpu_custom_call" | custom-call | flops 21474836480 | bytes 2359296 | tf_op jit(solution)/shard_map/attend_backward/pallas_call | solution.py:577
  166.6 8.1 %attend_backward.3 = (bf16[1024,128]{1,0:T(8,128)(2,1)}, bf16[1024,128]{1,0:T(8,128)(2,1)}, bf16[1024,128]{1,0:T(8,128)(2,1)}) custom-call(s32[1]{0:T(128)S(6)} %copy.29.prefix_ref, bf16[1024,384]{1,0:T(8,128)(2,1)} %get-tuple-element.217.query_ref, bf16[1024,384]{1,0:T(8,128)(2,1)} %get-tuple-element.218.key_ref, ...), custom_call_target="tpu_custom_call" | custom-call | flops 21474836480 | bytes 2359296 | tf_op jit(solution)/shard_map/attend_backward/pallas_call | solution.py:577
  179.7 5.0 %weight_grad.7 = (bf16[384,768]{1,0:T(8,128)(2,1)}, bf16[384,768]{1,0:T(8,128)(2,1)}) custom-call(s32[16]{0:T(128)} %stack.119.order_ref, bf16[768,1024]{1,0:T(8,128)(2,1)} %get-tuple-element.229.refs_0_, bf16[1024,128]{1,0:T(8,128)(2,1)} %get-tuple-element.264.refs_1_.refs_0_, bf16[1024,128]{1,0:T(8,128)(2,1)} %get-tuple-element.265.refs_2_.refs_1_, ...), custom_call_target="tpu_custom_call" | custom-call | flops 4831838208 | bytes 4325376 | tf_op jit(solution)/shard_map/weight_grad/pallas_call | solution.py:1079
  184.7 3.4 %weight_grad.8 = (bf16[384,384]{1,0:T(8,128)(2,1)}, bf16[384,384]{1,0:T(8,128)(2,1)}) custom-call(s32[16]{0:T(128)} %stack.118.order_ref, bf16[768,1024]{1,0:T(8,128)(2,1)} %get-tuple-element.227.refs_0_, bf16[1024,384]{1,0:T(8,128)(2,1)} %get-tuple-element.251.refs_1_), custom_call_target="tpu_custom_call" | custom-call | flops 2415919104 | bytes 2949120 | tf_op jit(solution)/shard_map/weight_grad/pallas_call | solution.py:1079
  190.0 8.0 %attend_backward.5 = (bf16[1024,128]{1,0:T(8,128)(2,1)}, bf16[1024,128]{1,0:T(8,128)(2,1)}, bf16[1024,128]{1,0:T(8,128)(2,1)}) custom-call(s32[1]{0:T(128)S(6)} %copy.29.prefix_ref, bf16[1024,384]{1,0:T(8,128)(2,1)} %get-tuple-element.217.query_ref, bf16[1024,384]{1,0:T(8,128)(2,1)} %get-tuple-element.218.key_ref, ...), custom_call_target="tpu_custom_call" | custom-call | flops 21474836480 | bytes 2359296 | tf_op jit(solution)/shard_map/attend_backward/pallas_call | solution.py:577
  202.1 3.8 %collective-permute-start.36 = (bf16[48,3072]{1,0:T(8,128)(2,1)}, bf16[48,3072]{1,0:T(8,128)(2,1)S(1)}, u32[]{:S(2)}, u32[]{:S(2)}) collective-permute-start(bf16[48,3072]{1,0:T(8,128)(2,1)} %get-tuple-element.263), channel_id=1, source_target_pairs={{0,24},{2,26},{4,28},{6,30},{8,0},{10,2},{12,4},{14,6},{16,8},{18,... | collective-permute-start | bytes 884744 | tf_op jit(solution)/shard_map/ppermute | solution.py:68
  205.9 6.7 %project_back.1 = (bf16[512,768]{1,0:T(8,128)(2,1)}, f32[512,768]{1,0:T(8,128)}, f32[8,384]{1,0:T(8,128)}) custom-call(s32[1]{0:T(128)} %bitcast.core_ref, bf16[1024,128]{1,0:T(8,128)(2,1)} %get-tuple-element.264.refs_1_.refs_0_, bf16[1024,128]{1,0:T(8,128)(2,1)} %get-tuple-element.265.refs_2_.refs_1_, bf16[1024,128]{1,0:T(8,128)(2,1)} %get-tuple-element.277.refs_2_.refs_1_, ...), custom_call_target="tpu_custom_call" | custom-call | flops 7247757312 | bytes 8847360 | tf_op jit(solution)/shard_map/project_back/pallas_call | solution.py:982
  212.7 3.5 %weight_grad.9 = (bf16[384,384]{1,0:T(8,128)(2,1)}, bf16[384,384]{1,0:T(8,128)(2,1)}) custom-call(s32[16]{0:T(128)} %stack.119.order_ref, bf16[768,1024]{1,0:T(8,128)(2,1)} %get-tuple-element.229.refs_0_, bf16[1024,128]{1,0:T(8,128)(2,1)} %get-tuple-element.277.refs_2_.refs_1_, bf16[1024,128]{1,0:T(8,128)(2,1)} %get-tuple-element.278.refs_5_.refs_2_, ...), custom_call_target="tpu_custom_call" | custom-call | flops 2415919104 | bytes 2949120 | tf_op jit(solution)/shard_map/weight_grad/pallas_call | solution.py:1079
  222.5 3.9 %input_back.1 = (f32[512,768]{1,0:T(8,128)}, f32[8,768]{1,0:T(8,128)}) custom-call(s32[1]{0:T(128)} %bitcast.core_ref, bf16[512,768]{1,0:T(8,128)(2,1)} %copy-done.4, f32[512,768]{1,0:T(8,128)} %get-tuple-element.284.own, f32[1024,768]{1,0:T(8,128)} %get-tuple-element.285.mid, bf16[512,768]{1,0:T(8,128)(2,1)} %x.1, f32[6,768]{1,0:T(8,128)} %model.7), custom_call_target="tpu_custom_call" | custom-call | flops 15728640 | bytes 6291456 | tf_op jit(solution)/shard_map/input_back/pallas_call | solution.py:1020
  244.3 9.3 %collective-permute-start.51 = (f32[84,128]{1,0:T(8,128)S(1)}, f32[84,128]{1,0:T(8,128)S(1)}, u32[]{:S(2)}, u32[]{:S(2)}) collective-permute-start(f32[84,128]{1,0:T(8,128)S(1)} %add_add_fusion.refs_0_), channel_id=1, source_target_pairs={{0,6},{2,4},{4,2},{6,0},{8,14},{10,12},{12,10},{14,8},{16,22},{18,... | collective-permute-start | bytes 129032 | tf_op jit(solution)/shard_map/ppermute | solution.py:159
  253.6 5.2 %collective-permute-done.44.refs_2_ = bf16[48,3072]{1,0:T(8,128)(2,1)S(1)} collective-permute-done((bf16[48,3072]{1,0:T(8,128)(2,1)S(1)}, bf16[48,3072]{1,0:T(8,128)(2,1)S(1)}, u32[]{:S(2)}, u32[]{:S(2)}) %collective-permute-start.44) | collective-permute-done | bytes 294944 | tf_op jit(solution)/shard_map/ppermute | solution.py:68
  (230 shorter events, 104.7 us)
Async XLA Ops:
  24.7 19.0 %collective-permute-start.7 = (bf16[48,1920]{1,0:T(8,128)(2,1)}, bf16[48,1920]{1,0:T(8,128)(2,1)S(1)}, u32[]{:S(2)}, u32[]{:S(2)}) collective-permute-start(bf16[48,1920]{1,0:T(8,128)(2,1)} %join.2), channel_id=1, source_target_pairs={{0,24},{2,26},{4,28},{6,30},{8,0},{10,2},{12,4},{14,6},{16,8},{18,... | collective-permute-start | bytes 552968 | tf_op jit(solution)/shard_map/ppermute | solution.py:68
  26.3 17.4 %collective-permute-start.6 = (bf16[48,1920]{1,0:T(8,128)(2,1)}, bf16[48,1920]{1,0:T(8,128)(2,1)S(1)}, u32[]{:S(2)}, u32[]{:S(2)}) collective-permute-start(bf16[48,1920]{1,0:T(8,128)(2,1)} %join.2), channel_id=1, source_target_pairs={{0,16},{2,18},{4,20},{6,22},{8,24},{10,26},{12,28},{14,30},{16,0},... | collective-permute-start | bytes 552968 | tf_op jit(solution)/shard_map/ppermute | solution.py:68
  27.0 16.7 %collective-permute-start.5 = (bf16[48,1920]{1,0:T(8,128)(2,1)}, bf16[48,1920]{1,0:T(8,128)(2,1)S(1)}, u32[]{:S(2)}, u32[]{:S(2)}) collective-permute-start(bf16[48,1920]{1,0:T(8,128)(2,1)} %join.2), channel_id=1, source_target_pairs={{0,8},{2,10},{4,12},{6,14},{8,16},{10,18},{12,20},{14,22},{16,24},... | collective-permute-start | bytes 552968 | tf_op jit(solution)/shard_map/ppermute | solution.py:68
  43.8 13.6 %collective-permute-start.14 = (bf16[48,1536]{1,0:T(8,128)(2,1)S(1)}, bf16[48,1536]{1,0:T(8,128)(2,1)S(1)}, u32[]{:S(2)}, u32[]{:S(2)}) collective-permute-start(bf16[48,1536]{1,0:T(8,128)(2,1)S(1)} %copy-done.26), channel_id=1, source_target_pairs={{0,24},{2,26},{4,28},{6,30},{8,0},{10,2},{12,4},{14,6},{16,8},{18,... | collective-permute-start | bytes 442376 | tf_op jit(solution)/shard_map/ppermute | solution.py:68
  44.6 21.4 %collective-permute-start.13 = (bf16[48,1536]{1,0:T(8,128)(2,1)S(1)}, bf16[48,1536]{1,0:T(8,128)(2,1)S(1)}, u32[]{:S(2)}, u32[]{:S(2)}) collective-permute-start(bf16[48,1536]{1,0:T(8,128)(2,1)S(1)} %copy-done.26), channel_id=1, source_target_pairs={{0,16},{2,18},{4,20},{6,22},{8,24},{10,26},{12,28},{14,30},{16,0},... | collective-permute-start | bytes 442376 | tf_op jit(solution)/shard_map/ppermute | solution.py:68
  48.4 16.2 %collective-permute-start.16 = (bf16[192,1920]{1,0:T(8,128)(2,1)S(1)}, bf16[192,1920]{1,0:T(8,128)(2,1)S(1)}, u32[]{:S(2)}, u32[]{:S(2)}) collective-permute-start(bf16[192,1920]{1,0:T(8,128)(2,1)S(1)} %constant_dynamic-update-slice_fusion.refs_0_), channel_id=1, source_target_pairs={{0,4},{2,6},{4,0},{6,2},{8,12},{10,14},{12,8},{14,10},{16,20},{18,... | collective-permute-start | bytes 2211848 | tf_op jit(solution)/shard_map/ppermute | solution.py:68
  49.9 16.0 %collective-permute-start.15 = (bf16[192,1920]{1,0:T(8,128)(2,1)S(1)}, bf16[192,1920]{1,0:T(8,128)(2,1)S(1)}, u32[]{:S(2)}, u32[]{:S(2)}) collective-permute-start(bf16[192,1920]{1,0:T(8,128)(2,1)S(1)} %constant_dynamic-update-slice_fusion.refs_0_), channel_id=1, source_target_pairs={{0,2},{2,0},{4,6},{6,4},{8,10},{10,8},{12,14},{14,12},{16,18},{18,... | collective-permute-start | bytes 2211848 | tf_op jit(solution)/shard_map/ppermute | solution.py:68
  88.9 15.4 %collective-permute-start.22 = (bf16[96,1536]{1,0:T(8,128)(2,1)S(1)}, bf16[96,1536]{1,0:T(8,128)(2,1)S(1)}, u32[]{:S(2)}, u32[]{:S(2)}) collective-permute-start(bf16[96,1536]{1,0:T(8,128)(2,1)S(1)} %slice.91), channel_id=1, source_target_pairs={{0,2},{2,0},{4,6},{6,4},{8,10},{10,8},{12,14},{14,12},{16,18},{18,... | collective-permute-start | bytes 884744 | tf_op jit(solution)/shard_map/ppermute | solution.py:68
  132.6 14.4 %collective-permute-start.27 = (bf16[1024,768]{1,0:T(8,128)(2,1)}, bf16[1024,768]{1,0:T(8,128)(2,1)S(1)}, u32[]{:S(2)}, u32[]{:S(2)}) collective-permute-start(bf16[1024,768]{1,0:T(8,128)(2,1)} %get-tuple-element.220.back_one), channel_id=1, source_target_pairs={{0,1},{1,0},{2,3},{3,2},{4,5},{5,4},{6,7},{7,6},{8,9},{9,8},{10,11... | collective-permute-start | bytes 4718600 | tf_op jit(solution)/shard_map/ppermute | solution.py:26
  138.9 35.8 %collective-permute-start.29 = (bf16[384,1536]{1,0:T(8,128)(2,1)}, bf16[384,1536]{1,0:T(8,128)(2,1)S(1)}, u32[]{:S(2)}, u32[]{:S(2)}) collective-permute-start(bf16[384,1536]{1,0:T(8,128)(2,1)} %get-tuple-element.242), channel_id=1, source_target_pairs={{0,2},{2,0},{4,6},{6,4},{8,10},{10,8},{12,14},{14,12},{16,18},{18,... | collective-permute-start | bytes 3538952 | tf_op jit(solution)/shard_map/ppermute | solution.py:68
  146.6 28.2 %collective-permute-start.28 = (bf16[384,1536]{1,0:T(8,128)(2,1)}, bf16[384,1536]{1,0:T(8,128)(2,1)S(1)}, u32[]{:S(2)}, u32[]{:S(2)}) collective-permute-start(bf16[384,1536]{1,0:T(8,128)(2,1)} %get-tuple-element.237), channel_id=1, source_target_pairs={{0,4},{2,6},{4,0},{6,2},{8,12},{10,14},{12,8},{14,10},{16,20},{18,... | collective-permute-start | bytes 3538952 | tf_op jit(solution)/shard_map/ppermute | solution.py:68
  176.3 21.7 %collective-permute-start.31 = (bf16[192,1536]{1,0:T(8,128)(2,1)}, bf16[192,1536]{1,0:T(8,128)(2,1)S(1)}, u32[]{:S(2)}, u32[]{:S(2)}) collective-permute-start(bf16[192,1536]{1,0:T(8,128)(2,1)} %get-tuple-element.314), channel_id=1, source_target_pairs={{0,2},{2,0},{4,6},{6,4},{8,10},{10,8},{12,14},{14,12},{16,18},{18,... | collective-permute-start | bytes 1769480 | tf_op jit(solution)/shard_map/ppermute | solution.py:68
  179.2 18.8 %collective-permute-start.30 = (bf16[192,1536]{1,0:T(8,128)(2,1)S(1)}, bf16[192,1536]{1,0:T(8,128)(2,1)S(1)}, u32[]{:S(2)}, u32[]{:S(2)}) collective-permute-start(bf16[192,1536]{1,0:T(8,128)(2,1)S(1)} %get-tuple-element.316), channel_id=1, source_target_pairs={{0,4},{2,6},{4,0},{6,2},{8,12},{10,14},{12,8},{14,10},{16,20},{18,... | collective-permute-start | bytes 1769480 | tf_op jit(solution)/shard_map/ppermute | solution.py:68
  188.1 28.0 %collective-permute-start.34 = (bf16[384,384]{1,0:T(8,128)(2,1)}, bf16[384,384]{1,0:T(8,128)(2,1)S(1)}, u32[]{:S(2)}, u32[]{:S(2)}) collective-permute-start(bf16[384,384]{1,0:T(8,128)(2,1)} %get-tuple-element.252), channel_id=1, source_target_pairs={{0,4},{2,6},{4,0},{6,2},{8,12},{10,14},{12,8},{14,10},{16,20},{18,... | collective-permute-start | bytes 884744 | tf_op jit(solution)/shard_map/ppermute | solution.py:68
  189.6 28.2 %collective-permute-start.33 = (bf16[384,768]{1,0:T(8,128)(2,1)}, bf16[384,768]{1,0:T(8,128)(2,1)S(1)}, u32[]{:S(2)}, u32[]{:S(2)}) collective-permute-start(bf16[384,768]{1,0:T(8,128)(2,1)} %get-tuple-element.250), channel_id=1, source_target_pairs={{0,2},{2,0},{4,6},{6,4},{8,10},{10,8},{12,14},{14,12},{16,18},{18,... | collective-permute-start | bytes 1769480 | tf_op jit(solution)/shard_map/ppermute | solution.py:68
  202.1 15.7 %collective-permute-start.35 = (bf16[48,3072]{1,0:T(8,128)(2,1)}, bf16[48,3072]{1,0:T(8,128)(2,1)S(1)}, u32[]{:S(2)}, u32[]{:S(2)}) collective-permute-start(bf16[48,3072]{1,0:T(8,128)(2,1)} %get-tuple-element.261), channel_id=1, source_target_pairs={{0,8},{2,10},{4,12},{6,14},{8,16},{10,18},{12,20},{14,22},{16,24},... | collective-permute-start | bytes 884744 | tf_op jit(solution)/shard_map/ppermute | solution.py:68
  202.1 15.7 %collective-permute-start.36 = (bf16[48,3072]{1,0:T(8,128)(2,1)}, bf16[48,3072]{1,0:T(8,128)(2,1)S(1)}, u32[]{:S(2)}, u32[]{:S(2)}) collective-permute-start(bf16[48,3072]{1,0:T(8,128)(2,1)} %get-tuple-element.263), channel_id=1, source_target_pairs={{0,24},{2,26},{4,28},{6,30},{8,0},{10,2},{12,4},{14,6},{16,8},{18,... | collective-permute-start | bytes 884744 | tf_op jit(solution)/shard_map/ppermute | solution.py:68
  218.8 15.5 %collective-permute-start.39 = (bf16[192,384]{1,0:T(8,128)(2,1)S(1)}, bf16[192,384]{1,0:T(8,128)(2,1)S(1)}, u32[]{:S(2)}, u32[]{:S(2)}) collective-permute-start(bf16[192,384]{1,0:T(8,128)(2,1)S(1)} %get-tuple-element.322), channel_id=1, source_target_pairs={{0,2},{2,0},{4,6},{6,4},{8,10},{10,8},{12,14},{14,12},{16,18},{18,... | collective-permute-start | bytes 442376 | tf_op jit(solution)/shard_map/ppermute | solution.py:68
  220.1 15.3 %collective-permute-start.38 = (bf16[192,768]{1,0:T(8,128)(2,1)S(1)}, bf16[192,768]{1,0:T(8,128)(2,1)S(1)}, u32[]{:S(2)}, u32[]{:S(2)}) collective-permute-start(bf16[192,768]{1,0:T(8,128)(2,1)S(1)} %get-tuple-element.318), channel_id=1, source_target_pairs={{0,4},{2,6},{4,0},{6,2},{8,12},{10,14},{12,8},{14,10},{16,20},{18,... | collective-permute-start | bytes 884744 | tf_op jit(solution)/shard_map/ppermute | solution.py:68
  235.4 23.4 %collective-permute-start.44 = (bf16[48,3072]{1,0:T(8,128)(2,1)S(1)}, bf16[48,3072]{1,0:T(8,128)(2,1)S(1)}, u32[]{:S(2)}, u32[]{:S(2)}) collective-permute-start(bf16[48,3072]{1,0:T(8,128)(2,1)S(1)} %copy-done.42), channel_id=1, source_target_pairs={{0,16},{2,18},{4,20},{6,22},{8,24},{10,26},{12,28},{14,30},{16,0},... | collective-permute-start | bytes 884744 | tf_op jit(solution)/shard_map/ppermute | solution.py:68
  240.1 25.9 %collective-permute-start.41 = (bf16[48,1536]{1,0:T(8,128)(2,1)}, bf16[48,1536]{1,0:T(8,128)(2,1)S(1)}, u32[]{:S(2)}, u32[]{:S(2)}) collective-permute-start(bf16[48,1536]{1,0:T(8,128)(2,1)} %get-tuple-element.293), channel_id=1, source_target_pairs={{0,8},{2,10},{4,12},{6,14},{8,16},{10,18},{12,20},{14,22},{16,24},... | collective-permute-start | bytes 442376 | tf_op jit(solution)/shard_map/ppermute | solution.py:68
  241.7 24.3 %collective-permute-start.42 = (bf16[48,1536]{1,0:T(8,128)(2,1)}, bf16[48,1536]{1,0:T(8,128)(2,1)S(1)}, u32[]{:S(2)}, u32[]{:S(2)}) collective-permute-start(bf16[48,1536]{1,0:T(8,128)(2,1)} %get-tuple-element.294), channel_id=1, source_target_pairs={{0,16},{2,18},{4,20},{6,22},{8,24},{10,26},{12,28},{14,30},{16,0},... | collective-permute-start | bytes 442376 | tf_op jit(solution)/shard_map/ppermute | solution.py:68
  242.6 23.4 %collective-permute-start.43 = (bf16[48,1536]{1,0:T(8,128)(2,1)}, bf16[48,1536]{1,0:T(8,128)(2,1)S(1)}, u32[]{:S(2)}, u32[]{:S(2)}) collective-permute-start(bf16[48,1536]{1,0:T(8,128)(2,1)} %get-tuple-element.295), channel_id=1, source_target_pairs={{0,24},{2,26},{4,28},{6,30},{8,0},{10,2},{12,4},{14,6},{16,8},{18,... | collective-permute-start | bytes 442376 | tf_op jit(solution)/shard_map/ppermute | solution.py:68
  244.3 15.3 %collective-permute-start.51 = (f32[84,128]{1,0:T(8,128)S(1)}, f32[84,128]{1,0:T(8,128)S(1)}, u32[]{:S(2)}, u32[]{:S(2)}) collective-permute-start(f32[84,128]{1,0:T(8,128)S(1)} %add_add_fusion.refs_0_), channel_id=1, source_target_pairs={{0,6},{2,4},{4,2},{6,0},{8,14},{10,12},{12,10},{14,8},{16,22},{18,... | collective-permute-start | bytes 129032 | tf_op jit(solution)/shard_map/ppermute | solution.py:159
  (75 other events, 483.2 us)
